TPU v7x, 32 devices: a whole 2x2x4 slice. The times are simulated.
32 devices in a mesh: group: 4 (over y, x), ctx: 8 (over z, core).
Axes of the slice: x: 2, y: 2, z: 4, core: 2. Of those that a mesh axis runs over, the one named last changes fastest.
Arguments:
- tokens: bfloat16 [4, 2048, 1024], P('group', 'ctx'), may hold values from -6 to 6
- cotangent: bfloat16 [4, 2048, 1024], P('group', 'ctx'), may hold values from -6 to 6
- block_table: int32 [4, 16], P('group'), may hold values from 0 to 15, each once within a row
- norm1_gain: bfloat16 [1024], P('ctx'), may hold values from 0.5 to 1.5
- w_query: bfloat16 [1024, 1024], P('ctx'), may hold values from -0.1875 to 0.1875
- w_key: bfloat16 [1024, 1024], P('ctx'), may hold values from -0.1875 to 0.1875
- w_value: bfloat16 [1024, 1024], P('ctx'), may hold values from -0.1875 to 0.1875
- w_out: bfloat16 [1024, 1024], P('ctx'), may hold values from -1.5 to 1.5
- norm2_gain: bfloat16 [1024], P('ctx'), may hold values from 0.5 to 1.5
- w_gate: bfloat16 [1024, 2816], P('ctx'), may hold values from -0.1875 to 0.1875
- w_up: bfloat16 [1024, 2816], P('ctx'), may hold values from -0.1875 to 0.1875
- w_down: bfloat16 [2816, 1024], P('ctx'), may hold values from -0.15625 to 0.15625
Outputs:
- output: bfloat16 [4, 2048, 1024], P('group', 'ctx')
- tokens_grad: bfloat16 [4, 2048, 1024], P('group', 'ctx')
- grad_norm1_gain: float32 [1024], P('ctx')
- grad_w_query: float32 [1024, 1024], P('ctx')
- grad_w_key: float32 [1024, 1024], P('ctx')
- grad_w_value: float32 [1024, 1024], P('ctx')
- grad_w_out: float32 [1024, 1024], P('ctx')
- grad_norm2_gain: float32 [1024], P('ctx')
- grad_w_gate: float32 [1024, 2816], P('ctx')
- grad_w_up: float32 [1024, 2816], P('ctx')
- grad_w_down: float32 [2816, 1024], P('ctx')
Inputs may be any that keep to these rules, and one draw needn't show every extreme that they name: Each row of block_table names every block of the family once.
All inputs are finite; a program needn't handle non-finite values.
Results may differ from a plain program's by a relative error of at most 0.023.
Values may be sent and summed in bfloat16 or wider, within the bound.
A program may use at most 256 MiB of HBM per device.

v0:
```python
import jax
import jax.numpy as jnp
from jax import lax
from jax.sharding import PartitionSpec as P

HEADS = 16
HEAD = 64
BLK = 128
KEYBLK = 512
PROMPT_MAX = 2048
CONT = 256


EPS = 1e-06
SCALE = 0.125


def rms_scale(hidden, gain):
    return hidden * lax.rsqrt(jnp.mean(hidden * hidden, axis=-1, keepdims=True) + EPS) * gain


def gated(gate, upper):
    return jax.nn.gelu(gate, approximate=True) * upper


def matmul(left, right):
    return jnp.dot(left, right, preferred_element_type=jnp.float32)


def inner(left, right):
    return lax.dot_general(
        left, right, (((0,), (0,)), ((), ())), preferred_element_type=jnp.float32
    )


def outer(left, right):
    return lax.dot_general(
        left, right, (((1,), (1,)), ((), ())), preferred_element_type=jnp.float32
    )


def family_index(table):
    offsets = jnp.arange(BLK, dtype=jnp.int32)
    return (table[:, None] * BLK + offsets[None, :]).reshape(-1)


def segment_of(index, prompt_len):
    return jnp.where(index < prompt_len, 0, 1 + (index - prompt_len) // CONT)


def allowed(query_index, key_index, prompt_len):
    query_seg = segment_of(query_index, prompt_len)
    key_seg = segment_of(key_index, prompt_len)
    same = (query_seg[:, None] == key_seg[None, :]) & (key_index[None, :] <= query_index[:, None])
    prompt = (key_seg[None, :] == 0) & (query_seg[:, None] > 0)
    return same | prompt


def head_split(block):
    return block.reshape(block.shape[0], HEADS, HEAD)


def scores_of(query_heads, key_block, query_index, key_index, prompt_len):
    score = (
        jnp.einsum(
            "qhd,khd->hqk", query_heads, head_split(key_block), preferred_element_type=jnp.float32
        )
        * SCALE
    )
    return (score, allowed(query_index, key_index, prompt_len))


def attend_stats(queries, keys, query_index, key_index, prompt_len):
    query_heads = head_split(queries)

    def step(carry, number):
        best, total = carry
        start = number * KEYBLK
        key_block = lax.dynamic_slice_in_dim(keys, start, KEYBLK, 0)
        block_index = lax.dynamic_slice_in_dim(key_index, start, KEYBLK, 0)
        score, keep = scores_of(query_heads, key_block, query_index, block_index, prompt_len)
        score = jnp.where(keep[None], score, -1e30)
        larger = jnp.maximum(best, jnp.max(score, axis=-1))
        terms = jnp.where(keep[None], jnp.exp(score - larger[:, :, None]), 0.0)
        total = total * jnp.exp(best - larger) + jnp.sum(terms, axis=-1)
        return ((larger, total), None)

    start_best = jnp.full((HEADS, queries.shape[0]), -1e30, jnp.float32)
    (best, total), ignored = lax.scan(
        step, (start_best, jnp.zeros_like(start_best)), jnp.arange(keys.shape[0] // KEYBLK)
    )
    return best + jnp.log(total)


def attend_values(queries, keys, values, lse, query_index, key_index, prompt_len):
    query_heads = head_split(queries)

    def step(acc, number):
        start = number * KEYBLK
        key_block = lax.dynamic_slice_in_dim(keys, start, KEYBLK, 0)
        value_block = lax.dynamic_slice_in_dim(values, start, KEYBLK, 0)
        block_index = lax.dynamic_slice_in_dim(key_index, start, KEYBLK, 0)
        score, keep = scores_of(query_heads, key_block, query_index, block_index, prompt_len)
        prob = jnp.where(keep[None], jnp.exp(score - lse[:, :, None]), 0.0).astype(jnp.bfloat16)
        return (
            acc
            + jnp.einsum(
                "hqk,khd->qhd", prob, head_split(value_block), preferred_element_type=jnp.float32
            ),
            None,
        )

    start_acc = jnp.zeros((queries.shape[0], HEADS, HEAD), jnp.float32)
    acc, ignored = lax.scan(step, start_acc, jnp.arange(keys.shape[0] // KEYBLK))
    return acc.reshape(queries.shape[0], HEADS * HEAD)


def block_grads(query_heads, grad_heads, key_block, value_block, lse, delta, keep):
    key_heads = head_split(key_block)
    value_heads = head_split(value_block)
    score = (
        jnp.einsum("qhd,khd->hqk", query_heads, key_heads, preferred_element_type=jnp.float32)
        * SCALE
    )
    prob = jnp.where(keep[None], jnp.exp(score - lse[:, :, None]), 0.0)
    dvalue = jnp.einsum(
        "hqk,qhd->khd", prob.astype(jnp.bfloat16), grad_heads, preferred_element_type=jnp.float32
    )
    dprob = jnp.einsum("qhd,khd->hqk", grad_heads, value_heads, preferred_element_type=jnp.float32)
    dscore = (prob * (dprob - delta[:, :, None])).astype(jnp.bfloat16)
    dquery = (
        jnp.einsum("hqk,khd->qhd", dscore, key_heads, preferred_element_type=jnp.float32) * SCALE
    )
    dkey = (
        jnp.einsum("hqk,qhd->khd", dscore, query_heads, preferred_element_type=jnp.float32) * SCALE
    )
    return (dquery, dkey, dvalue)


def local(
    tokens,
    cotangent,
    block_table,
    norm1_gain,
    w_query,
    w_key,
    w_value,
    w_out,
    norm2_gain,
    w_gate,
    w_up,
    w_down,
):
    row_count = tokens.shape[1]
    width = tokens.shape[2]
    every_index = family_index(block_table[0])
    prompt_len = min(PROMPT_MAX, every_index.shape[0] // 2)
    own_index = lax.dynamic_slice_in_dim(
        every_index, lax.axis_index("ctx") * row_count, row_count, 0
    )
    gain1, wq_full, wk_full, wv_full, wo_full = (
        lax.all_gather(norm1_gain, "ctx", axis=0, tiled=True),
        lax.all_gather(w_query, "ctx", axis=0, tiled=True),
        lax.all_gather(w_key, "ctx", axis=0, tiled=True),
        lax.all_gather(w_value, "ctx", axis=0, tiled=True),
        lax.all_gather(w_out, "ctx", axis=0, tiled=True),
    )
    inputs = tokens[0].astype(jnp.float32)
    normed1, norm1_pull = jax.vjp(rms_scale, inputs, gain1.astype(jnp.float32))
    first_low = normed1.astype(jnp.bfloat16)
    queries = matmul(first_low, wq_full).astype(jnp.bfloat16)
    keys_own = matmul(first_low, wk_full).astype(jnp.bfloat16)
    values_own = matmul(first_low, wv_full).astype(jnp.bfloat16)
    keys_all, values_all = (
        lax.all_gather(keys_own, "ctx", axis=0, tiled=True),
        lax.all_gather(values_own, "ctx", axis=0, tiled=True),
    )
    lse = attend_stats(queries, keys_all, own_index, every_index, prompt_len)
    attended_wide = attend_values(
        queries, keys_all, values_all, lse, own_index, every_index, prompt_len
    )
    attended = attended_wide.astype(jnp.bfloat16)
    hidden = inputs + matmul(attended, wo_full)
    gain2, wg_full, wu_full, wd_full = (
        lax.all_gather(norm2_gain, "ctx", axis=0, tiled=True),
        lax.all_gather(w_gate, "ctx", axis=0, tiled=True),
        lax.all_gather(w_up, "ctx", axis=0, tiled=True),
        lax.all_gather(w_down, "ctx", axis=0, tiled=True),
    )
    normed2, norm2_pull = jax.vjp(rms_scale, hidden, gain2.astype(jnp.float32))
    second_low = normed2.astype(jnp.bfloat16)
    gate = matmul(second_low, wg_full)
    upper = matmul(second_low, wu_full)
    mixed_wide, gate_pull = jax.vjp(gated, gate, upper)
    mixed = mixed_wide.astype(jnp.bfloat16)
    result = hidden + matmul(mixed, wd_full)
    output = result.astype(jnp.bfloat16)[None]
    grad_low = cotangent[0]
    grad_down = inner(mixed, grad_low)
    dmixed = outer(grad_low, wd_full)
    dgate, dupper = gate_pull(dmixed)
    dgate_low = dgate.astype(jnp.bfloat16)
    dupper_low = dupper.astype(jnp.bfloat16)
    grad_gate = inner(second_low, dgate_low)
    grad_up = inner(second_low, dupper_low)
    dnormed2 = outer(dgate_low, wg_full) + outer(dupper_low, wu_full)
    dhidden_norm, grad_gain2 = norm2_pull(dnormed2)
    dhidden = grad_low.astype(jnp.float32) + dhidden_norm
    attn_low = dhidden.astype(jnp.bfloat16)
    grad_out_w = inner(attended, attn_low)
    dattended = outer(attn_low, wo_full).astype(jnp.bfloat16)
    delta = jnp.sum(
        (dattended.astype(jnp.float32) * attended_wide).reshape(row_count, HEADS, HEAD), axis=-1
    ).T
    query_heads = head_split(queries)
    grad_heads = head_split(dattended)

    def key_step(carry, number):
        start = number * KEYBLK
        key_block = lax.dynamic_slice_in_dim(keys_all, start, KEYBLK, 0)
        value_block = lax.dynamic_slice_in_dim(values_all, start, KEYBLK, 0)
        block_index = lax.dynamic_slice_in_dim(every_index, start, KEYBLK, 0)
        keep = allowed(own_index, block_index, prompt_len)
        dquery, dkey, dvalue = block_grads(
            query_heads, grad_heads, key_block, value_block, lse, delta, keep
        )
        joined = jnp.concatenate(
            [dkey.reshape(KEYBLK, width), dvalue.reshape(KEYBLK, width)], axis=1
        )
        return (carry + dquery, joined)

    start_query = jnp.zeros((row_count, HEADS, HEAD), jnp.float32)
    query_sum, key_terms = lax.scan(
        key_step, start_query, jnp.arange(every_index.shape[0] // KEYBLK)
    )
    summed = lax.psum_scatter(
        key_terms.reshape(every_index.shape[0], 2 * width).astype(jnp.bfloat16),
        "ctx",
        scatter_dimension=0,
        tiled=True,
    ).astype(jnp.float32)
    query_grad = query_sum.reshape(row_count, width)
    key_grad = summed[:, :width]
    value_grad = summed[:, width:]
    query_low = query_grad.astype(jnp.bfloat16)
    key_low = key_grad.astype(jnp.bfloat16)
    value_low = value_grad.astype(jnp.bfloat16)
    grad_query = inner(first_low, query_low)
    grad_key = inner(first_low, key_low)
    grad_value = inner(first_low, value_low)
    dnormed1 = outer(query_low, wq_full) + outer(key_low, wk_full) + outer(value_low, wv_full)
    dinput_norm, grad_gain1 = norm1_pull(dnormed1)
    tokens_grad = (dhidden + dinput_norm).astype(jnp.bfloat16)[None]
    shards = (
        lax.psum_scatter(
            grad_gain1.astype(jnp.bfloat16), "ctx", scatter_dimension=0, tiled=True
        ).astype(jnp.float32),
        lax.psum_scatter(
            grad_query.astype(jnp.bfloat16), "ctx", scatter_dimension=0, tiled=True
        ).astype(jnp.float32),
        lax.psum_scatter(
            grad_key.astype(jnp.bfloat16), "ctx", scatter_dimension=0, tiled=True
        ).astype(jnp.float32),
        lax.psum_scatter(
            grad_value.astype(jnp.bfloat16), "ctx", scatter_dimension=0, tiled=True
        ).astype(jnp.float32),
        lax.psum_scatter(
            grad_out_w.astype(jnp.bfloat16), "ctx", scatter_dimension=0, tiled=True
        ).astype(jnp.float32),
        lax.psum_scatter(
            grad_gain2.astype(jnp.bfloat16), "ctx", scatter_dimension=0, tiled=True
        ).astype(jnp.float32),
        lax.psum_scatter(
            grad_gate.astype(jnp.bfloat16), "ctx", scatter_dimension=0, tiled=True
        ).astype(jnp.float32),
        lax.psum_scatter(
            grad_up.astype(jnp.bfloat16), "ctx", scatter_dimension=0, tiled=True
        ).astype(jnp.float32),
        lax.psum_scatter(
            grad_down.astype(jnp.bfloat16), "ctx", scatter_dimension=0, tiled=True
        ).astype(jnp.float32),
    )
    shards = (
        lax.psum(shards[0].astype(jnp.bfloat16), "group").astype(jnp.float32),
        lax.psum(shards[1].astype(jnp.bfloat16), "group").astype(jnp.float32),
        lax.psum(shards[2].astype(jnp.bfloat16), "group").astype(jnp.float32),
        lax.psum(shards[3].astype(jnp.bfloat16), "group").astype(jnp.float32),
        lax.psum(shards[4].astype(jnp.bfloat16), "group").astype(jnp.float32),
        lax.psum(shards[5].astype(jnp.bfloat16), "group").astype(jnp.float32),
        lax.psum(shards[6].astype(jnp.bfloat16), "group").astype(jnp.float32),
        lax.psum(shards[7].astype(jnp.bfloat16), "group").astype(jnp.float32),
        lax.psum(shards[8].astype(jnp.bfloat16), "group").astype(jnp.float32),
    )
    return (
        output,
        tokens_grad,
        shards[0],
        shards[1],
        shards[2],
        shards[3],
        shards[4],
        shards[5],
        shards[6],
        shards[7],
        shards[8],
    )


def solution(mesh):
    in_specs = (
        P("group", "ctx", None),
        P("group", "ctx", None),
        P("group", None),
        P("ctx"),
        P("ctx", None),
        P("ctx", None),
        P("ctx", None),
        P("ctx", None),
        P("ctx"),
        P("ctx", None),
        P("ctx", None),
        P("ctx", None),
    )
    out_specs = (
        P("group", "ctx", None),
        P("group", "ctx", None),
        P("ctx"),
        P("ctx", None),
        P("ctx", None),
        P("ctx", None),
        P("ctx", None),
        P("ctx"),
        P("ctx", None),
        P("ctx", None),
        P("ctx", None),
    )
    return jax.shard_map(local, mesh=mesh, in_specs=in_specs, out_specs=out_specs, check_vma=False)
```

profile of v0, /device:TPU:0, one launch (start us, length us, event | category | flops | bytes accessed | tf_op | source)
XLA Modules:
  0.0 1079.1 jit_solution(14566623661992682458)
XLA Ops:
  9.5 13.5 %all-gather = bf16[8,1,128]{2,1,0:T(2,128)(2,1)S(1)} all-gather(bf16[1,1,128]{2,1,0:T(2,128)(2,1)} %bitcast.253), channel_id=1, replica_groups=mesh['group'=4,'ctx'=8] {'ctx'}, dimensions={0}, use_global_device_ids=true | all-gather | bytes 2304 | tf_op jit(solution)/shard_map/all_gather | solution.py:162
  24.3 17.2 %all-gather.16.cloned.1.call-done = bf16[1024,1024]{1,0:T(8,128)(2,1)} async-done(((bf16[128,1024]{1,0:T(8,128)(2,1)}), bf16[1024,1024]{1,0:T(8,128)(2,1)}) %all-gather.16.cloned.1.call-update) | async-done | bytes 2097168 | tf_op jit(solution)/shard_map/all_gather | solution.py:164
  44.9 26.8 %all-gather.12.cloned.1.call-done = bf16[1024,1024]{1,0:T(8,128)(2,1)} async-done(((bf16[128,1024]{1,0:T(8,128)(2,1)}), bf16[1024,1024]{1,0:T(8,128)(2,1)}) %all-gather.12.cloned.1.call-update) | async-done | bytes 2097168 | tf_op jit(solution)/shard_map/all_gather | solution.py:165
  77.9 10.3 all-gather.1
  88.2 13.7 %all-gather.20.cloned.1.call-done = bf16[1024,1024]{1,0:T(8,128)(2,1)} async-done(((bf16[128,1024]{1,0:T(8,128)(2,1)}), bf16[1024,1024]{1,0:T(8,128)(2,1)}) %all-gather.20.cloned.1.call-update) | async-done | bytes 2097168 | tf_op jit(solution)/shard_map/all_gather | solution.py:163
  104.5 46.1 %all-gather.18.cloned.1.call-done = bf16[2048,1024]{1,0:T(8,128)(2,1)} async-done(((bf16[256,1024]{1,0:T(8,128)(2,1)}), bf16[2048,1024]{1,0:T(8,128)(2,1)}) %all-gather.18.cloned.1.call-update) | async-done | bytes 4194320 | tf_op jit(solution)/shard_map/all_gather | solution.py:175
  150.6 6.5 copy.55
  157.2 49.2 %while.46 = (s32[]{:T(128)}, f32[16,256]{1,0:T(8,128)S(1)}, f32[16,256]{1,0:T(8,128)S(1)}, s32[256]{0:T(256)S(1)}, s32[4]{0:T(128)S(1)}, /*index=5*/s32[2048]{0:...) while((s32[]{:T(128)}, f32[16,256]{1,0:T(8,128)S(1)}, ...), condition=%wide.region_4.5_spmd.clone, body=%wide.region_1.4_spmd.clone.sunk | while | flops 285903872 | bytes 21069512 | solution.py:89
  206.4 6.6 copy.54
  213.0 31.5 %while.47 = (s32[]{:T(128)}, f32[256,16,64]{0,2,1:T(8,128)}, s32[4]{0:T(128)S(1)}, bf16[2048,1024]{0,1:T(8,128)(2,1)}, s32[256]{0:T(256)S(1)}, /*index=5*/s32[20...) while((s32[]{:T(128)}, f32[256,16,64]{0,2,1:T(8,128)}, ...), condition=%wide.region_6.7_spmd.clone, body=%wide.region_5.6_spmd.clone.sunk | while | flops 546454528 | bytes 9207505 | solution.py:114
  250.0 39.4 %all-gather.24.cloned.1.call-done = bf16[1024,2816]{1,0:T(8,128)(2,1)} async-done(((bf16[128,2816]{1,0:T(8,128)(2,1)}), bf16[1024,2816]{1,0:T(8,128)(2,1)}) %all-gather.24.cloned.1.call-update) | async-done | bytes 5767184 | tf_op jit(solution)/shard_map/all_gather | solution.py:186
  289.5 5.8 fusion.91
  295.3 54.9 %all-gather.26.cloned.1.call-done = bf16[1024,2816]{1,0:T(8,128)(2,1)} async-done(((bf16[128,2816]{1,0:T(8,128)(2,1)}), bf16[1024,2816]{1,0:T(8,128)(2,1)}) %all-gather.26.cloned.1.call-update) | async-done | bytes 5767184 | tf_op jit(solution)/shard_map/all_gather | solution.py:187
  350.2 5.9 fusion.92
  356.2 54.9 %all-gather.28.cloned.1.call-done = bf16[2816,1024]{1,0:T(8,128)(2,1)} async-done(((bf16[352,1024]{1,0:T(8,128)(2,1)}), bf16[2816,1024]{1,0:T(8,128)(2,1)}) %all-gather.28.cloned.1.call-update) | async-done | bytes 5767184 | tf_op jit(solution)/shard_map/all_gather | solution.py:188
  411.0 10.2 multiply_convert_fusion
  421.2 5.4 fusion.93
  434.8 103.0 %while.48 = (s32[]{:T(128)}, f32[256,16,64]{0,2,1:T(8,128)}, bf16[4,512,2048]{2,1,0:T(8,128)(2,1)}, s32[4]{0:T(128)S(1)}, bf16[2048,1024]{0,1:T(8,128)(2,1)}, /*...) while((s32[]{:T(128)}, f32[256,16,64]{0,2,1:T(8,128)}, ...), condition=%wide.region_11.12_spmd.clone, body=%wide.region_10.11_spmd.clone.sunk | while | flops 1369848832 | bytes 118947672 | solution.py:233
  543.6 5.6 convolution_convert_fusion.2
  549.3 5.6 convolution_convert_fusion.1
  561.6 64.7 %reduce-scatter.9.cloned.1.call-done = bf16[256,2048]{1,0:T(8,128)(2,1)} async-done(((bf16[2048,2048]{1,0:T(8,128)(2,1)}), bf16[256,2048]{1,0:T(8,128)(2,1)}) %reduce-scatter.9.cloned.1.call-update) | async-done | bytes 1048592 | tf_op jit(solution)/shard_map/reduce_scatter | solution.py:236
  631.9 30.7 %reduce-scatter.11.cloned.1.call-done = bf16[128,1024]{1,0:T(8,128)(2,1)} async-done(((bf16[1024,1024]{1,0:T(8,128)(2,1)}), bf16[128,1024]{1,0:T(8,128)(2,1)}) %reduce-scatter.11.cloned.1.call-update) | async-done | bytes 262160 | tf_op jit(solution)/shard_map/reduce_scatter | solution.py:258
  662.7 36.7 %reduce-scatter.17.cloned.1.call-done = bf16[128,1024]{1,0:T(8,128)(2,1)} async-done(((bf16[1024,1024]{1,0:T(8,128)(2,1)}), bf16[128,1024]{1,0:T(8,128)(2,1)}) %reduce-scatter.17.cloned.1.call-update) | async-done | bytes 262160 | tf_op jit(solution)/shard_map/reduce_scatter | solution.py:267
  699.4 65.8 %reduce-scatter.19.cloned.1.call-done = bf16[128,2816]{1,0:T(8,128)(2,1)} async-done(((bf16[1024,2816]{1,0:T(8,128)(2,1)}), bf16[128,2816]{1,0:T(8,128)(2,1)}) %reduce-scatter.19.cloned.1.call-update) | async-done | bytes 720912 | tf_op jit(solution)/shard_map/reduce_scatter | solution.py:273
  765.2 65.4 %reduce-scatter.21.cloned.1.call-done = bf16[128,2816]{1,0:T(8,128)(2,1)} async-done(((bf16[1024,2816]{1,0:T(8,128)(2,1)}), bf16[128,2816]{1,0:T(8,128)(2,1)}) %reduce-scatter.21.cloned.1.call-update) | async-done | bytes 720912 | tf_op jit(solution)/shard_map/reduce_scatter | solution.py:276
  830.6 65.4 %reduce-scatter.23.cloned.1.call-done = bf16[352,1024]{1,0:T(8,128)(2,1)} async-done(((bf16[2816,1024]{1,0:T(8,128)(2,1)}), bf16[352,1024]{1,0:T(8,128)(2,1)}) %reduce-scatter.23.cloned.1.call-update) | async-done | bytes 720912 | tf_op jit(solution)/shard_map/reduce_scatter | solution.py:279
  896.0 36.3 %reduce-scatter.13.cloned.1.call-done = bf16[128,1024]{1,0:T(8,128)(2,1)} async-done(((bf16[1024,1024]{1,0:T(8,128)(2,1)}), bf16[128,1024]{1,0:T(8,128)(2,1)}) %reduce-scatter.13.cloned.1.call-update) | async-done | bytes 262160 | tf_op jit(solution)/shard_map/reduce_scatter | solution.py:261
  932.3 36.6 %reduce-scatter.15.cloned.1.call-done = bf16[128,1024]{1,0:T(8,128)(2,1)} async-done(((bf16[1024,1024]{1,0:T(8,128)(2,1)}), bf16[128,1024]{1,0:T(8,128)(2,1)}) %reduce-scatter.15.cloned.1.call-update) | async-done | bytes 262160 | tf_op jit(solution)/shard_map/reduce_scatter | solution.py:264
  972.7 5.4 fusion.54
  980.7 15.0 %all-reduce.2 = (bf16[1024]{0:T(1024)(128)(2,1)S(1)}, bf16[1024]{0:T(1024)(128)(2,1)S(1)}) all-reduce(bf16[1024]{0:T(1024)(128)(2,1)S(1)} %get-tuple-element.669, bf16[1024]{0:T(1024)(128)(2,1)S(1)} %get-tuple-element.667), channel_id=3, replica_groups=mesh['group'=4,'ctx'=8] {'ctx'}, use_global_device_ids=true, to_apply=%region_15.16.clone | all-reduce | flops 2048 | bytes 8192
  995.9 9.7 all-reduce.3
  1007.8 53.3 %all-reduce.7.cloned.1.call-done = (bf16[128,1024]{1,0:T(8,128)(2,1)}, bf16[128,1024]{1,0:T(8,128)(2,1)}, bf16[128,1024]{1,0:T(8,128)(2,1)}, bf16[128,1024]{1,0:...) async-done(((bf16[128,1024]{1,0:T(8,128)(2,1)}, bf16[128,1024]{1,0:T(8,128)(2,1)}, bf16[128,1024]{1,0:T(8,128)(2,1)}, ...) | async-done | bytes 3211280 | tf_op jit(solution)/shard_map/psum | solution.py:285
  (310 shorter events, 241.4 us)
Async XLA Ops:
  7.2 64.5 %copy-start.2 = (bf16[1,256,1024]{2,1,0:T(8,128)(2,1)S(1)}, bf16[1,256,1024]{2,1,0:T(8,128)(2,1)}, u32[]{:S(2)}) copy-start(bf16[1,256,1024]{2,1,0:T(8,128)(2,1)} %param.18) | copy-start | bytes 1572868
  7.2 34.3 %all-gather.16.cloned.1.call-start = ((), (), s32[]{:S(2)}) async-start(), calls=%async_computation.10 | async-start | bytes 2359296 | tf_op jit(solution)/shard_map/all_gather | solution.py:164
  7.9 63.8 %all-gather.12.cloned.1.call-start = ((), (), s32[]{:S(2)}) async-start(), calls=%async_computation.8 | async-start | bytes 2359296 | tf_op jit(solution)/shard_map/all_gather | solution.py:165
  8.7 93.3 %all-gather.20.cloned.1.call-start = ((), (), s32[]{:S(2)}) async-start(), calls=%async_computation.12 | async-start | bytes 2359296 | tf_op jit(solution)/shard_map/all_gather | solution.py:163
  9.4 141.2 %all-gather.18.cloned.1.call-start = ((), (), s32[]{:S(2)}) async-start(), calls=%async_computation.11 | async-start | bytes 4718592 | tf_op jit(solution)/shard_map/all_gather | solution.py:175
  23.0 78.9 %copy-start.28 = (f32[8,1,128]{2,1,0:T(1,128)}, f32[8,1,128]{2,1,0:T(1,128)S(1)}, u32[]{:S(2)}) copy-start(f32[8,1,128]{2,1,0:T(1,128)S(1)} %convert_element_type.219) | copy-start | bytes 12292
  24.2 50.6 %copy-start.32 = (f32[256]{0:T(256)}, f32[256]{0:T(256)S(1)}, u32[]{:S(2)}) copy-start(f32[256]{0:T(256)S(1)} %fusion.57) | copy-start | bytes 3076
  24.3 77.7 %copy-start.30 = (f32[256]{0:T(256)}, f32[256]{0:T(256)S(1)}, u32[]{:S(2)}) copy-start(f32[256]{0:T(256)S(1)} %fusion.80) | copy-start | bytes 3076
  44.8 33.0 %copy-start.37 = (s32[1,16]{1,0:T(1,128)S(1)}, s32[1,16]{1,0:T(1,128)}, u32[]{:S(2)}) copy-start(s32[1,16]{1,0:T(1,128)} %param.20) | copy-start | bytes 196
  44.8 33.0 %copy-start.34 = (bf16[128]{0:T(256)(128)(2,1)S(1)}, bf16[128]{0:T(256)(128)(2,1)}, u32[]{:S(2)}) copy-start(bf16[128]{0:T(256)(128)(2,1)} %param.26) | copy-start | bytes 772
  44.8 161.6 %all-gather.14.cloned.1.call-start = ((), (), s32[]{:S(2)}) async-start(), calls=%async_computation.9 | async-start | bytes 4718592 | tf_op jit(solution)/shard_map/all_gather | solution.py:176
  74.9 172.2 %all-gather.22.cloned.1.call-start = ((), (), s32[]{:S(2)}) async-start(), calls=%async_computation.13 | async-start | bytes 2359296 | tf_op jit(solution)/shard_map/all_gather | solution.py:166
  75.4 214.0 %all-gather.24.cloned.1.call-start = ((), (), s32[]{:S(2)}) async-start(), calls=%async_computation.14 | async-start | bytes 6488064 | tf_op jit(solution)/shard_map/all_gather | solution.py:186
  76.2 274.1 %all-gather.26.cloned.1.call-start = ((), (), s32[]{:S(2)}) async-start(), calls=%async_computation.15 | async-start | bytes 6488064 | tf_op jit(solution)/shard_map/all_gather | solution.py:187
  76.9 334.1 %all-gather.28.cloned.1.call-start = ((), (), s32[]{:S(2)}) async-start(), calls=%async_computation.16 | async-start | bytes 6488064 | tf_op jit(solution)/shard_map/all_gather | solution.py:188
  77.7 548.6 %reduce-scatter.9.cloned.1.call-start = ((), (), s32[]{:S(2)}) async-start(), calls=%async_computation.17 | async-start | bytes 9437184 | tf_op jit(solution)/shard_map/reduce_scatter | solution.py:236
  249.8 178.8 %copy-start.5 = (f32[256,1024]{1,0:T(8,128)}, f32[256,1024]{1,0:T(8,128)S(1)}, u32[]{:S(2)}) copy-start(f32[256,1024]{1,0:T(8,128)S(1)} %get-tuple-element.765) | copy-start | bytes 3145732
  250.0 100.2 %copy-start.9 = (bf16[256,1024]{1,0:T(8,128)(2,1)}, bf16[256,1024]{1,0:T(8,128)(2,1)S(1)}, u32[]{:S(2)}) copy-start(bf16[256,1024]{1,0:T(8,128)(2,1)S(1)} %multiply_convert_fusion.2) | copy-start | bytes 1572868
  295.3 115.7 %copy-start.19 = (bf16[1,256,1024]{2,1,0:T(8,128)(2,1)S(1)}, bf16[1,256,1024]{2,1,0:T(8,128)(2,1)}, u32[]{:S(2)}) copy-start(bf16[1,256,1024]{2,1,0:T(8,128)(2,1)} %param.19) | copy-start | bytes 1572868
  537.8 124.8 %reduce-scatter.11.cloned.1.call-start = ((), (), s32[]{:S(2)}) async-start(), calls=%async_computation.18 | async-start | bytes 2359296 | tf_op jit(solution)/shard_map/reduce_scatter | solution.py:258
  541.4 157.9 %reduce-scatter.17.cloned.1.call-start = ((), (), s32[]{:S(2)}) async-start(), calls=%async_computation.21 | async-start | bytes 2359296 | tf_op jit(solution)/shard_map/reduce_scatter | solution.py:267
  543.5 221.7 %reduce-scatter.19.cloned.1.call-start = ((), (), s32[]{:S(2)}) async-start(), calls=%async_computation.22 | async-start | bytes 6488064 | tf_op jit(solution)/shard_map/reduce_scatter | solution.py:273
  549.2 281.3 %reduce-scatter.21.cloned.1.call-start = ((), (), s32[]{:S(2)}) async-start(), calls=%async_computation.23 | async-start | bytes 6488064 | tf_op jit(solution)/shard_map/reduce_scatter | solution.py:276
  554.9 341.1 %reduce-scatter.23.cloned.1.call-start = ((), (), s32[]{:S(2)}) async-start(), calls=%async_computation.24 | async-start | bytes 6488064 | tf_op jit(solution)/shard_map/reduce_scatter | solution.py:279
  561.5 370.8 %reduce-scatter.13.cloned.1.call-start = ((), (), s32[]{:S(2)}) async-start(), calls=%async_computation.19 | async-start | bytes 2359296 | tf_op jit(solution)/shard_map/reduce_scatter | solution.py:261
  629.6 339.3 %reduce-scatter.15.cloned.1.call-start = ((), (), s32[]{:S(2)}) async-start(), calls=%async_computation.20 | async-start | bytes 2359296 | tf_op jit(solution)/shard_map/reduce_scatter | solution.py:264
  631.9 337.1 %copy-start.38 = (u32[32]{0:T(128)S(1)}, u32[32]{0:T(128)}, u32[]{:S(2)}) copy-start(u32[32]{0:T(128)} %constant.348) | copy-start | bytes 388
  631.9 338.3 %copy-start.12 = (bf16[256,16,64]{0,2,1:T(8,128)(2,1)S(1)}, bf16[256,16,64]{0,2,1:T(8,128)(2,1)}, u32[]{:S(2)}) copy-start(bf16[256,16,64]{0,2,1:T(8,128)(2,1)} %copy-done.11) | copy-start | bytes 1572868
  631.9 429.1 %all-reduce.7.cloned.1.call-start = ((), (), s32[]{:S(2)}) async-start(), calls=%async_computation.25 | async-start | bytes 6422528 | tf_op jit(solution)/shard_map/psum | solution.py:285
  979.7 27.0 %copy-start.33 = (f32[256]{0:T(256)S(1)}, f32[256]{0:T(256)}, u32[]{:S(2)}) copy-start(f32[256]{0:T(256)} %copy-done.32) | copy-start | bytes 3076
  1061.0 7.4 copy-start.25
  1061.0 8.6 copy-start.24
  (37 other events, 128.4 us)
Sparse Core Ops, SparseCore 0:
  9.6 31.7 all-gather.15
  43.1 28.5 all-gather.11
  73.3 28.5 all-gather.19
  104.0 46.6 all-gather.17
  152.7 45.8 all-gather.13
  200.0 27.8 all-gather.21
  229.5 59.8 all-gather.23
  291.1 59.0 all-gather.25
  351.9 59.0 all-gather.27
  537.9 88.2 reduce-scatter.8
  628.6 34.0 reduce-scatter.10
  664.8 34.5 reduce-scatter.16
  701.7 63.4 reduce-scatter.18
  767.4 63.1 reduce-scatter.20
  832.7 63.2 reduce-scatter.22
  898.1 34.1 reduce-scatter.12
  934.5 34.3 reduce-scatter.14
  972.7 88.2 all-reduce.6
where the time goes:
time: 1100 us; the launch traced here: 1080 us
  waiting for transfers between devices  713 us (65%)
  matrix products  181 us (16%)
  local copies, waits for them, and re-layouts  66.8 us (6%)
  blocking collectives  48.6 us (4%)
  other arithmetic  44.8 us (4%)
  between operations  15.6 us (1%)
    reduce_scatter x1, waiting for transfers between devices, local(): lax.psum_scatter(grad_gate.astype(jnp.bfloat16), 'ctx', scatter_dimension...  65.8 us
    reduce_scatter x1, waiting for transfers between devices, local(): lax.psum_scatter(grad_down.astype(jnp.bfloat16), 'ctx', scatter_dimension...  65.4 us
    reduce_scatter x1, waiting for transfers between devices, local(): lax.psum_scatter(grad_up.astype(jnp.bfloat16), 'ctx', scatter_dimension=0...  65.4 us
    reduce_scatter x1, waiting for transfers between devices, local(): lax.psum_scatter(key_terms.reshape(every_index.shape[0], 2 * width).astyp...  64.7 us
    all_gather x1, waiting for transfers between devices, local(): lax.all_gather(w_up, 'ctx', axis=0, tiled=True)  54.9 us
    all_gather x1, waiting for transfers between devices, local(): lax.all_gather(w_down, 'ctx', axis=0, tiled=True)  54.9 us
    psum x1, waiting for transfers between devices, local(): lax.psum(shards[1].astype(jnp.bfloat16), 'group').astype(jnp.float32)  53.3 us
    all_gather x1, waiting for transfers between devices, local(): lax.all_gather(keys_own, 'ctx', axis=0, tiled=True)  46.1 us
  transfers between devices with their start and end apart: 18, of which 16 were waited for; matrix products, arithmetic and copies ran while one was open for 14% of the time, Pallas kernels for 0%

commit v1 on v0

--- a/solution.py
+++ b/solution.py
@@ -1,6 +1,9 @@
 import jax
 import jax.numpy as jnp
 from jax import lax
+from jax.experimental import pallas as pl
+from jax.experimental.pallas import tpu as pltpu
+from jax.sharding import Mesh
 from jax.sharding import PartitionSpec as P
 
 HEADS = 16
@@ -306,7 +309,1033 @@
     )
 
 
-def solution(mesh):
+PLANE = 4
+CORES = 2
+TP = ("group", "core")
+F32 = jnp.float32
+BF16 = jnp.bfloat16
+
+
+def dot_nt(left, right):
+    return lax.dot_general(left, right, (((1,), (1,)), ((), ())), preferred_element_type=F32)
+
+
+def place_rows(table_ref, blocks, chunk):
+    for stored in range(blocks):
+        line, core, half = stored // 4, (stored // 2) % 2, stored % 2
+        start = table_ref[stored] * BLK
+        for part in range(2):
+            plane = 2 * half + part
+            row = ((plane * CORES + core) * PLANE + line) * chunk
+            yield row, pl.multiple_of(start + part * chunk, chunk)
+
+
+def head_mask(rows, head):
+    lane = lax.broadcasted_iota(jnp.int32, (rows, 2 * HEAD), 1)
+    return (lane >= head * HEAD) & (lane < (head + 1) * HEAD)
+
+
+def causal_mask():
+    key = lax.broadcasted_iota(jnp.int32, (CONT, CONT), 0)
+    query = lax.broadcasted_iota(jnp.int32, (CONT, CONT), 1)
+    return key <= query
+
+
+def attend_kernel(table_ref, qkv_ref, att_ref, lse_ref, ot_ref, qs, ks, vs, vt, att):
+    total = qkv_ref.shape[0]
+    chunk = BLK // 2
+    width = 2 * HEAD
+    for row, place in place_rows(table_ref, total // BLK, chunk):
+        for number, ref in enumerate((qs, ks, vs)):
+            block = qkv_ref[row : row + chunk, number * width : (number + 1) * width]
+            ref[pl.ds(place, chunk), :] = block * jnp.bfloat16(SCALE) if number == 0 else block
+
+    @pl.loop(0, total // CONT)
+    def _(number):
+        start = pl.multiple_of(number * CONT, CONT)
+        vt[:, pl.ds(start, CONT)] = vs[pl.ds(start, CONT), :].astype(F32).T.astype(BF16)
+
+    def one(start, before):
+        query = qs[pl.ds(start, CONT), :]
+        outs = []
+        for head in range(2):
+            masked = jnp.where(head_mask(CONT, head), query, jnp.zeros_like(query))
+            own = dot_nt(ks[pl.ds(start, CONT), :], masked)
+            own = jnp.where(causal_mask(), own, -1e30)
+            best = jnp.max(own, axis=0, keepdims=True)
+            if before:
+                past = dot_nt(ks[0:before, :], masked)
+                best = jnp.maximum(best, jnp.max(past, axis=0, keepdims=True))
+            terms = jnp.exp(own - best)
+            total_terms = jnp.sum(terms, axis=0, keepdims=True)
+            rows = slice(head * HEAD, (head + 1) * HEAD)
+            out = matmul(vt[rows, pl.ds(start, CONT)], terms.astype(BF16))
+            if before:
+                terms = jnp.exp(past - best)
+                total_terms = total_terms + jnp.sum(terms, axis=0, keepdims=True)
+                out = out + matmul(vt[rows, 0:before], terms.astype(BF16))
+            outs.append(out / total_terms)
+            lse_ref[head : head + 1, pl.ds(start, CONT)] = best + jnp.log(total_terms)
+        joined = jnp.concatenate(outs, axis=0)
+        ot_ref[:, pl.ds(start, CONT)] = joined.astype(BF16)
+        att[pl.ds(start, CONT), :] = joined.T.astype(BF16)
+
+    prompt = total // 2
+    for number in range(prompt // CONT):
+        one(number * CONT, number * CONT)
+
+    @pl.loop(prompt // CONT, total // CONT)
+    def _(number):
+        one(pl.multiple_of(number * CONT, CONT), prompt)
+
+    for row, place in place_rows(table_ref, total // BLK, chunk):
+        att_ref[row : row + chunk, :] = att[pl.ds(place, chunk), :]
+
+
+def attend_grad_kernel(
+    table_ref, qkv_ref, datt_ref, lse_ref, ot_ref, out_ref, qs, ks, vs, gs, kt, dqs, dks, dvs
+):
+    total = qkv_ref.shape[0]
+    chunk = BLK // 2
+    width = 2 * HEAD
+    for row, place in place_rows(table_ref, total // BLK, chunk):
+        for number, ref in enumerate((qs, ks, vs)):
+            block = qkv_ref[row : row + chunk, number * width : (number + 1) * width]
+            ref[pl.ds(place, chunk), :] = block * jnp.bfloat16(SCALE) if number == 0 else block
+        gs[pl.ds(place, chunk), :] = datt_ref[row : row + chunk, :]
+
+    @pl.loop(0, total // CONT)
+    def _(number):
+        start = pl.multiple_of(number * CONT, CONT)
+        kt[:, pl.ds(start, CONT)] = ks[pl.ds(start, CONT), :].astype(F32).T.astype(BF16)
+
+    dks[...] = jnp.zeros_like(dks)
+    dvs[...] = jnp.zeros_like(dvs)
+
+    def one(start, before):
+        query = qs[pl.ds(start, CONT), :]
+        grad = gs[pl.ds(start, CONT), :]
+        product = grad.astype(F32).T * ot_ref[:, pl.ds(start, CONT)].astype(F32)
+        outs = []
+        for head in range(2):
+            rows = slice(head * HEAD, (head + 1) * HEAD)
+            delta = jnp.sum(product[rows], axis=0, keepdims=True)
+            lse = lse_ref[head : head + 1, pl.ds(start, CONT)]
+            keep = head_mask(CONT, head)
+            query_head = jnp.where(keep, query, jnp.zeros_like(query))
+            grad_head = jnp.where(keep, grad, jnp.zeros_like(grad))
+            parts = [(pl.ds(start, CONT), True)]
+            if before:
+                parts.append((pl.ds(0, before), False))
+            dq = None
+            for keys, diagonal in parts:
+                prob = jnp.exp(dot_nt(ks[keys, :], query_head) - lse)
+                if diagonal:
+                    prob = jnp.where(causal_mask(), prob, 0.0)
+                dprob = dot_nt(vs[keys, :], grad_head)
+                dscore = (prob * (dprob - delta)).astype(BF16)
+                dvs[keys, :] += matmul(prob.astype(BF16), grad_head)
+                dks[keys, :] += matmul(dscore, query_head)
+                term = matmul(kt[rows, keys], dscore)
+                dq = term if dq is None else dq + term
+            outs.append(dq)
+        joined = jnp.concatenate(outs, axis=0) * SCALE
+        dqs[pl.ds(start, CONT), :] = joined.T.astype(BF16)
+
+    prompt = total // 2
+    for number in range(prompt // CONT):
+        one(number * CONT, number * CONT)
+
+    @pl.loop(prompt // CONT, total // CONT)
+    def _(number):
+        one(pl.multiple_of(number * CONT, CONT), prompt)
+
+    for row, place in place_rows(table_ref, total // BLK, chunk):
+        out_ref[row : row + chunk, 0:width] = dqs[pl.ds(place, chunk), :]
+        out_ref[row : row + chunk, width : 2 * width] = dks[pl.ds(place, chunk), :].astype(BF16)
+        out_ref[row : row + chunk, 2 * width :] = dvs[pl.ds(place, chunk), :].astype(BF16)
+
+
+def vmem(count):
+    return [pl.BlockSpec(memory_space=pltpu.VMEM)] * count
+
+
+def attend(table, qkv):
+    total, width = qkv.shape[0], 2 * HEAD
+    return pl.pallas_call(
+        attend_kernel,
+        out_shape=(
+            jax.ShapeDtypeStruct((total, width), BF16),
+            jax.ShapeDtypeStruct((2, total), F32),
+            jax.ShapeDtypeStruct((width, total), BF16),
+        ),
+        in_specs=[pl.BlockSpec(memory_space=pltpu.SMEM)] + vmem(1),
+        out_specs=tuple(vmem(3)),
+        scratch_shapes=[pltpu.VMEM((total, width), BF16)] * 3
+        + [pltpu.VMEM((width, total), BF16), pltpu.VMEM((total, width), BF16)],
+        compiler_params=pltpu.CompilerParams(vmem_limit_bytes=40 << 20),
+        name="attend",
+    )(table, qkv)
+
+
+def attend_grad(table, qkv, datt, lse, ot):
+    total, width = qkv.shape[0], 2 * HEAD
+    return pl.pallas_call(
+        attend_grad_kernel,
+        out_shape=jax.ShapeDtypeStruct((total, 3 * width), BF16),
+        in_specs=[pl.BlockSpec(memory_space=pltpu.SMEM)] + vmem(4),
+        out_specs=vmem(1)[0],
+        scratch_shapes=[pltpu.VMEM((total, width), BF16)] * 4
+        + [pltpu.VMEM((width, total), BF16), pltpu.VMEM((total, width), BF16)]
+        + [pltpu.VMEM((total, width), F32)] * 2,
+        compiler_params=pltpu.CompilerParams(vmem_limit_bytes=50 << 20),
+        name="attend_grad",
+    )(table, qkv, datt, lse, ot)
+
+
+MESH = pl.DeviceIdType.MESH
+COPIES = 128
+
+
+def spots():
+    chip, line, core = lax.axis_index("group"), lax.axis_index("z"), lax.axis_index("core")
+    side = chip + 1 - 2 * lax.rem(chip, 2)
+    over = lax.rem(chip + 2, PLANE)
+    far = PLANE - 1 - chip
+    return chip, line, core, side, over, far
+
+
+def plane_partners():
+    chip, line, core, side, over, far = spots()
+    return [(q, line, core) for q in (far, side, over)]
+
+
+def line_partners():
+    chip, line, core, side, over, far = spots()
+    lines = [lax.rem(line + d, PLANE) for d in range(1, PLANE)]
+    same = [(chip, z, core) for z in lines]
+    return same + [(chip, z, 1 - core) for z in lines] + [(chip, line, 1 - core)]
+
+
+class Copies:
+    def __init__(self, sems):
+        self.sems, self.count, self.started = sems, 0, []
+
+    def number(self):
+        self.count += 1
+        return self.count - 1
+
+    def enter(self):
+        barrier = pltpu.get_barrier_semaphore()
+        partners = plane_partners() + line_partners()
+        for partner in partners:
+            pl.semaphore_signal(barrier, inc=1, device_id=partner, device_id_type=MESH)
+        pl.semaphore_wait(barrier, len(partners))
+
+    def send(self, source, target, partner):
+        number = self.number()
+        copy = pltpu.make_async_remote_copy(
+            src_ref=source,
+            dst_ref=target,
+            send_sem=self.sems.at[0, number],
+            recv_sem=self.sems.at[1, number],
+            device_id=partner,
+            device_id_type=MESH,
+        )
+        copy.start()
+        self.started.append(copy)
+        return copy
+
+    def keep(self, source, target):
+        copy = pltpu.make_async_copy(source, target, self.sems.at[0, self.number()])
+        copy.start()
+        return copy
+
+    def finish(self):
+        for copy in self.started:
+            copy.wait_send()
+
+
+def arrived(copies):
+    for copy in copies:
+        copy.wait_recv()
+
+
+def finished(copies):
+    for copy in copies:
+        copy.wait()
+
+
+def gather_stream(copies, own_ref, out_ref, twin=True):
+    chip, line, core, side, over, far = spots()
+    half = own_ref.shape[0] // 2
+    to_far, to_side, to_over = plane_partners()
+    to_twin = (chip, line, 1 - core)
+
+    def slot_of(q):
+        return CORES * q + core if twin else q
+
+    def part(slot, number):
+        return out_ref.at[slot, pl.ds(number * half, half)]
+
+    def own(number):
+        return own_ref.at[pl.ds(number * half, half)]
+
+    def on(slot, number, partner):
+        return copies.send(part(slot, number), part(slot, number), partner)
+
+    def share(slot, number):
+        return [on(slot, number, to_twin)] if twin else []
+
+    mine, slot_side, slot_over, slot_far = map(slot_of, (chip, side, over, far))
+    sides, overs = [None, None], [None, None]
+    overs[0] = copies.send(own(0), part(mine, 0), to_over)
+    sides[1] = copies.send(own(1), part(mine, 1), to_side)
+    sides[0] = copies.send(own(0), part(mine, 0), to_side)
+    overs[1] = copies.send(own(1), part(mine, 1), to_over)
+    twins = [copies.send(own(h), part(mine, h), to_twin) for h in range(2)] if twin else []
+    local = copies.keep(own_ref, out_ref.at[mine])
+    yield
+    overs[0].wait_recv()
+    far0 = on(slot_over, 0, to_side)
+    twins += share(slot_over, 0)
+    sides[1].wait_recv()
+    far1 = on(slot_side, 1, to_over)
+    twins += share(slot_side, 1)
+    yield
+    sides[0].wait_recv()
+    twins += share(slot_side, 0)
+    overs[1].wait_recv()
+    twins += share(slot_over, 1)
+    yield
+    far0.wait_recv()
+    twins += share(slot_far, 0)
+    far1.wait_recv()
+    twins += share(slot_far, 1)
+    arrived(twins)
+    local.wait()
+    yield
+
+
+def scatter_stream(copies, part_ref, out_ref, scratch):
+    twin, mine, from_side, from_over, go = scratch
+    chip, line, core, side, over, far = spots()
+    rows = out_ref.shape[0]
+    half = rows // 2
+    to_far, to_side, to_over = plane_partners()
+    to_twin = (chip, line, 1 - core)
+    twins, locals_ = [], []
+    for n, q in enumerate((far, side, over, chip)):
+        slot = CORES * q + (1 - core)
+        twins.append([])
+        for h in range(2):
+            half_rows = pl.ds(h * half, half)
+            twins[n].append(copies.send(part_ref.at[slot, half_rows], twin.at[n, half_rows], to_twin))
+        locals_.append(copies.keep(part_ref.at[CORES * q + core], mine.at[n]))
+    yield
+
+    def pair(n, h):
+        part = slice(h * half, (h + 1) * half)
+        twins[n][h].wait_recv()
+        return mine[n, part].astype(F32) + twin[n, part].astype(F32)
+
+    def put(n, h, value):
+        part = slice(h * half, (h + 1) * half)
+        go[n, part] = value.astype(BF16)
+        return go.at[n, pl.ds(h * half, half)]
+
+    locals_[0].wait()
+    far0 = copies.send(put(0, 0, pair(0, 0)), from_side.at[0], to_side)
+    far1 = copies.send(put(0, 1, pair(0, 1)), from_over.at[0], to_over)
+    locals_[1].wait()
+    side0 = copies.send(put(1, 0, pair(1, 0)), from_side.at[1], to_side)
+    locals_[2].wait()
+    over1 = copies.send(put(2, 1, pair(2, 1)), from_over.at[2], to_over)
+    yield
+    value = pair(2, 0)
+    far0.wait_recv()
+    over0 = copies.send(put(2, 0, value + from_side[0].astype(F32)), from_over.at[1], to_over)
+    value = pair(1, 1)
+    far1.wait_recv()
+    side1 = copies.send(put(1, 1, value + from_over[0].astype(F32)), from_side.at[2], to_side)
+    yield
+    locals_[3].wait()
+    first, second = pair(3, 0), pair(3, 1)
+    side0.wait_recv()
+    first = first + from_side[1].astype(F32)
+    over1.wait_recv()
+    second = second + from_over[2].astype(F32)
+    over0.wait_recv()
+    out_ref[0:half] = first + from_over[1].astype(F32)
+    side1.wait_recv()
+    out_ref[half:rows] = second + from_side[2].astype(F32)
+    yield
+
+
+def scatter_scratch(rows, width):
+    return [
+        pltpu.VMEM((PLANE, rows, width), BF16),
+        pltpu.VMEM((PLANE, rows, width), BF16),
+        pltpu.VMEM((3, rows // 2, width), BF16),
+        pltpu.VMEM((3, rows // 2, width), BF16),
+        pltpu.VMEM((3, rows, width), BF16),
+    ]
+
+
+def inward_stream(copies, own_ref, mid, out_ref):
+    chip, line, core, side, over, far = spots()
+    chunk = own_ref.shape[0] // PLANE
+
+    def rows(q):
+        return own_ref.at[pl.ds(q * chunk, chunk)]
+
+    sent = [copies.send(rows(q[0]), mid.at[chip], q) for q in plane_partners()]
+    local = copies.keep(rows(chip), mid.at[chip])
+    yield
+    local.wait()
+    arrived(sent)
+    moved = [copies.send(mid.at[q[1]], out_ref.at[line], q) for q in line_partners()[: PLANE - 1]]
+    local = copies.keep(mid.at[line], out_ref.at[line])
+    yield
+    arrived(moved)
+    local.wait()
+    yield
+
+
+def outward_stream(copies, own_ref, mid, out_ref):
+    chip, line, core, side, over, far = spots()
+    chunk = own_ref.shape[1]
+    moved = [copies.send(own_ref.at[q[1]], mid.at[line], q) for q in line_partners()[: PLANE - 1]]
+    local = copies.keep(own_ref.at[line], mid.at[line])
+    yield
+    local.wait()
+    arrived(moved)
+    target = out_ref.at[pl.ds(chip * chunk, chunk)]
+    sent = [copies.send(mid.at[q[0]], target, q) for q in plane_partners()]
+    local = copies.keep(mid.at[chip], target)
+    yield
+    arrived(sent)
+    local.wait()
+    yield
+
+
+def columns_stream(copies, piece_ref, out_ref):
+    chip, line, core, side, over, far = spots()
+    mine = out_ref.at[CORES * line + core]
+    sent = [copies.send(piece_ref.at[q[2]], mine, q) for q in line_partners()]
+    local = copies.keep(piece_ref.at[core], mine)
+    yield
+    arrived(sent)
+    local.wait()
+    yield
+
+
+def rows_stream(copies, shard_ref, mid, out_ref):
+    chip, line, core, side, over, far = spots()
+    width = shard_ref.shape[1] // PLANE
+    quarter = pl.ds(pl.multiple_of(chip * width, width), width)
+    sent = [copies.send(shard_ref.at[:, quarter], mid.at[line], q) for q in line_partners()[: PLANE - 1]]
+    local = copies.keep(shard_ref.at[:, quarter], mid.at[line])
+    yield
+    local.wait()
+    arrived(sent)
+    sent = [copies.send(mid.at[q[0]], out_ref.at[:, quarter], q) for q in plane_partners()]
+    local = copies.keep(mid.at[chip], out_ref.at[:, quarter])
+    yield
+    arrived(sent)
+    local.wait()
+    yield
+
+
+def unit_rows(value):
+    inverse = lax.rsqrt(jnp.mean(value * value, axis=-1, keepdims=True) + EPS)
+    return value * inverse, inverse
+
+
+def start_kernel(
+    tok_ref, cot_ref, small_ref, qkv_ref, wo_ref,
+    n1_ref, x_ref, cotp_ref, line_ref, plane_ref, wqkv_ref, wout_ref,
+    mid_x, mid_c, mid_w, normed, lines, sems,
+):
+    copies = Copies(sems)
+    chip, line, core, side, over, far = spots()
+    copies.enter()
+    tokens = inward_stream(copies, tok_ref, mid_x, x_ref)
+    next(tokens)
+    mine = CORES * line + core
+    small = [copies.send(small_ref, lines.at[mine], q) for q in line_partners()]
+    small += [copies.send(small_ref, plane_ref.at[chip], q) for q in plane_partners()]
+    local = [copies.keep(small_ref, lines.at[mine]), copies.keep(small_ref, plane_ref.at[chip])]
+    next(tokens)
+    cots = inward_stream(copies, cot_ref, mid_c, cotp_ref)
+    next(cots)
+    arrived(small)
+    finished(local)
+    line_ref[...] = lines[...]
+    next(tokens)
+    weights = columns_stream(copies, qkv_ref, wqkv_ref)
+    next(weights)
+    rows = rows_stream(copies, wo_ref, mid_w, wout_ref)
+    next(rows)
+    chunk = x_ref.shape[1]
+    ranks = lines.shape[0]
+    gain = jnp.concatenate([lines[s, 0:1, :] for s in range(ranks)], axis=1)
+    for n in range(PLANE):
+        unit, ignored = unit_rows(x_ref[n].astype(F32))
+        normed[n * chunk : (n + 1) * chunk] = (unit * gain).astype(BF16)
+    gather = gather_stream(copies, normed, n1_ref)
+    next(gather)
+    next(gather)
+    next(cots)
+    next(gather)
+    next(gather)
+    next(rows)
+    next(weights)
+    next(rows)
+    next(cots)
+    copies.finish()
+
+
+def comm_call(kernel, name, number, out_shape, in_specs, out_specs, scratch, vmem_mib=32):
+    return pl.pallas_call(
+        kernel,
+        out_shape=out_shape,
+        in_specs=in_specs,
+        out_specs=out_specs,
+        scratch_shapes=scratch + [pltpu.SemaphoreType.DMA((2, COPIES))],
+        compiler_params=pltpu.CompilerParams(
+            collective_id=number, has_side_effects=True, vmem_limit_bytes=vmem_mib << 20
+        ),
+        name=name,
+    )
+
+
+ANY = pl.BlockSpec(memory_space=pl.ANY)
+IN_VMEM = pl.BlockSpec(memory_space=pltpu.VMEM)
+
+
+def start(tokens, cotangent, small, qkv, w_out):
+    rows, width = tokens.shape
+    ranks = PLANE * CORES
+    chunks = (PLANE, rows // PLANE, width)
+    shapes = (
+        jax.ShapeDtypeStruct((ranks, rows, width), BF16),
+        jax.ShapeDtypeStruct(chunks, BF16),
+        jax.ShapeDtypeStruct(chunks, BF16),
+        jax.ShapeDtypeStruct((ranks,) + small.shape, F32),
+        jax.ShapeDtypeStruct((PLANE,) + small.shape, F32),
+        jax.ShapeDtypeStruct((ranks,) + qkv.shape[1:], BF16),
+        jax.ShapeDtypeStruct(w_out.shape, BF16),
+    )
+    return comm_call(
+        start_kernel, "start", 1, shapes, [ANY] * 5,
+        (ANY, IN_VMEM, ANY, IN_VMEM, ANY, ANY, ANY),
+        [pltpu.VMEM(chunks, BF16)] * 2
+        + [pltpu.VMEM((PLANE, w_out.shape[0], width // PLANE), BF16)]
+        + [pltpu.VMEM((rows, width), BF16), pltpu.VMEM((ranks,) + small.shape, F32)],
+    )(tokens, cotangent, small, qkv, w_out)
+
+
+def gains_of(line_ref, row):
+    return jnp.concatenate([line_ref[s, row : row + 1, :] for s in range(line_ref.shape[0])], axis=1)
+
+
+def middle_kernel(
+    part_ref, x_ref, line_ref, gu_ref, wd_ref,
+    n2_ref, h1_ref, wgu_ref, wdown_ref,
+    *rest,
+):
+    scratch, (summed, normed, mid_w, sems) = rest[:5], rest[5:]
+    copies = Copies(sems)
+    copies.enter()
+    scatter = scatter_stream(copies, part_ref, summed, scratch)
+    next(scatter)
+    weights = columns_stream(copies, gu_ref, wgu_ref)
+    rows = rows_stream(copies, wd_ref, mid_w, wdown_ref)
+    next(rows)
+    next(weights)
+    next(scatter)
+    next(scatter)
+    next(scatter)
+    gain = gains_of(line_ref, 1)
+    chunk = x_ref.shape[1]
+    for n in range(PLANE):
+        part = slice(n * chunk, (n + 1) * chunk)
+        hidden = x_ref[n].astype(F32) + summed[part]
+        h1_ref[part] = hidden
+        unit, ignored = unit_rows(hidden)
+        normed[part] = (unit * gain).astype(BF16)
+    gather = gather_stream(copies, normed, n2_ref)
+    next(gather)
+    next(gather)
+    next(gather)
+    next(rows)
+    next(gather)
+    next(rows)
+    next(weights)
+    copies.finish()
+
+
+def middle(partial, x, lines, gate_up, w_down):
+    ranks = PLANE * CORES
+    rows, width = PLANE * x.shape[1], x.shape[2]
+    shapes = (
+        jax.ShapeDtypeStruct((ranks, rows, width), BF16),
+        jax.ShapeDtypeStruct((rows, width), F32),
+        jax.ShapeDtypeStruct((ranks,) + gate_up.shape[1:], BF16),
+        jax.ShapeDtypeStruct(w_down.shape, BF16),
+    )
+    return comm_call(
+        middle_kernel, "middle", 2, shapes, [ANY, IN_VMEM, IN_VMEM, ANY, ANY],
+        (ANY, IN_VMEM, ANY, ANY),
+        scatter_scratch(rows, width)
+        + [pltpu.VMEM((rows, width), F32), pltpu.VMEM((rows, width), BF16)]
+        + [pltpu.VMEM((PLANE, w_down.shape[0], width // PLANE), BF16)],
+    )(partial.reshape(ranks, rows, width), x, lines, gate_up, w_down)
+
+
+def column_grads_stream(copies, grad_ref, recv, sum_ref):
+    chip, line, core, side, over, far = spots()
+    sent = [
+        copies.send(grad_ref.at[CORES * q[1] + q[2]], recv.at[core, line], q)
+        for q in line_partners()
+    ]
+    local = copies.keep(grad_ref.at[CORES * line + core], recv.at[core, line])
+    yield
+    arrived(sent)
+    local.wait()
+    for number in range(CORES):
+        total = recv[number, 0].astype(F32)
+        for family in range(1, PLANE):
+            total = total + recv[number, family].astype(F32)
+        sum_ref[number] = total.astype(BF16)
+    yield
+
+
+def row_grads_stream(copies, grad_ref, mid, recv, summed, out_ref):
+    chip, line, core, side, over, far = spots()
+    width = out_ref.shape[1] // PLANE
+
+    def quarter(q):
+        return pl.ds(pl.multiple_of(q * width, width), width)
+
+    sent = [copies.send(grad_ref.at[:, quarter(q[0])], mid.at[chip], q) for q in plane_partners()]
+    local = copies.keep(grad_ref.at[:, quarter(chip)], mid.at[chip])
+    yield
+    local.wait()
+    arrived(sent)
+    sent = [copies.send(mid.at[q[1]], recv.at[line], q) for q in line_partners()[: PLANE - 1]]
+    local = copies.keep(mid.at[line], recv.at[line])
+    yield
+    arrived(sent)
+    local.wait()
+    total = recv[0].astype(F32)
+    for family in range(1, PLANE):
+        total = total + recv[family].astype(F32)
+    summed[...] = total.astype(BF16)
+    sent = [copies.send(summed, out_ref.at[:, quarter(chip)], q) for q in plane_partners()]
+    local = copies.keep(summed, out_ref.at[:, quarter(chip)])
+    yield
+    arrived(sent)
+    local.wait()
+    yield
+
+
+def gain_grads_stream(copies, own, recv, summed, plane, out_ref):
+    chip, line, core, side, over, far = spots()
+    mine = CORES * line + core
+    sent = [copies.send(own.at[CORES * q[1] + q[2]], recv.at[mine], q) for q in line_partners()]
+    local = copies.keep(own.at[mine], recv.at[mine])
+    yield
+    arrived(sent)
+    local.wait()
+    summed[...] = jnp.sum(recv[...], axis=0)
+    sent = [copies.send(summed, plane.at[chip], q) for q in plane_partners()]
+    local = copies.keep(summed, plane.at[chip])
+    yield
+    arrived(sent)
+    local.wait()
+    out_ref[...] = jnp.sum(plane[...], axis=0)
+    yield
+
+
+def norm_back(grad, value, gain):
+    unit, inverse = unit_rows(value)
+    scaled = grad * gain
+    back = inverse * (scaled - unit * jnp.mean(scaled * unit, axis=-1, keepdims=True))
+    return back, jnp.sum(grad * unit, axis=0, keepdims=True)
+
+
+def back_kernel(
+    part_ref, h1_ref, cot_ref, line_ref, gu_ref,
+    ga_ref, dh1_ref, gain_ref, gusum_ref,
+    *rest,
+):
+    scratch, (summed, low, recv, sems) = rest[:5], rest[5:]
+    copies = Copies(sems)
+    copies.enter()
+    scatter = scatter_stream(copies, part_ref, summed, scratch)
+    next(scatter)
+    columns = column_grads_stream(copies, gu_ref, recv, gusum_ref)
+    next(columns)
+    next(scatter)
+    next(scatter)
+    next(scatter)
+    gain = gains_of(line_ref, 1)
+    chunk = cot_ref.shape[1]
+    gain_ref[...] = jnp.zeros_like(gain_ref)
+    for n in range(PLANE):
+        part = slice(n * chunk, (n + 1) * chunk)
+        back, by_gain = norm_back(summed[part], h1_ref[part], gain)
+        grad = cot_ref[n].astype(F32) + back
+        gain_ref[0:1] += by_gain
+        dh1_ref[part] = grad
+        low[part] = grad.astype(BF16)
+    gather = gather_stream(copies, low, ga_ref)
+    next(gather)
+    next(gather)
+    next(gather)
+    next(gather)
+    next(columns)
+    copies.finish()
+
+
+def back(partial, h1, cot, lines, gate_up_grad):
+    ranks = PLANE * CORES
+    rows, width = h1.shape
+    shapes = (
+        jax.ShapeDtypeStruct((ranks, rows, width), BF16),
+        jax.ShapeDtypeStruct((rows, width), F32),
+        jax.ShapeDtypeStruct((8, width), F32),
+        jax.ShapeDtypeStruct((CORES,) + gate_up_grad.shape[1:], BF16),
+    )
+    return comm_call(
+        back_kernel, "back", 3, shapes, [ANY, IN_VMEM, IN_VMEM, IN_VMEM, ANY],
+        (ANY, IN_VMEM, IN_VMEM, IN_VMEM),
+        scatter_scratch(rows, width)
+        + [pltpu.VMEM((rows, width), F32), pltpu.VMEM((rows, width), BF16)]
+        + [pltpu.VMEM((CORES, PLANE) + gate_up_grad.shape[1:], BF16)],
+    )(partial, h1, cot, lines, gate_up_grad)
+
+
+def last_kernel(
+    part_ref, mixed_ref, x_ref, h1_ref, dh1_ref, line_ref, gain_ref,
+    gusum_ref, qkv_ref, wo_ref, wd_ref,
+    out_ref, grad_ref, gains_ref, gu_all, qkv_all, wo_all, wd_all,
+    *rest,
+):
+    scratch, other, rest = rest[:5], rest[5:10], rest[10:]
+    summed, mixed, low, mid_a, mid_b, recv_qkv, qkvsum, rest = *rest[:7], rest[7:]
+    mid_wo, recv_wo, sum_wo, mid_wd, recv_wd, sum_wd, own, recv_gain, sum_gain, plane, sems = rest
+    copies = Copies(sems)
+    copies.enter()
+    scatter = scatter_stream(copies, part_ref, summed, scratch)
+    next(scatter)
+    qkv = column_grads_stream(copies, qkv_ref, recv_qkv, qkvsum)
+    next(qkv)
+    next(scatter)
+    second = scatter_stream(copies, mixed_ref, mixed, other)
+    next(second)
+    next(scatter)
+    wd = row_grads_stream(copies, wd_ref, mid_wd, recv_wd, sum_wd, wd_all)
+    next(wd)
+    wo = row_grads_stream(copies, wo_ref, mid_wo, recv_wo, sum_wo, wo_all)
+    next(wo)
+    next(scatter)
+    gain = gains_of(line_ref, 0)
+    chunk, width = x_ref.shape[1], x_ref.shape[2]
+    total = jnp.zeros((1, width), F32)
+    for n in range(PLANE):
+        part = slice(n * chunk, (n + 1) * chunk)
+        back, by_gain = norm_back(summed[part], x_ref[n].astype(F32), gain)
+        total = total + by_gain
+        low[n] = (dh1_ref[part] + back).astype(BF16)
+    tokens = outward_stream(copies, low, mid_a, grad_ref)
+    next(tokens)
+    shard = line_ref.shape[2]
+    own[...] = jnp.zeros_like(own)
+    for s in range(PLANE * CORES):
+        part = slice(s * shard, (s + 1) * shard)
+        own[s, 0:1] = total[:, part]
+        own[s, 1:2] = gain_ref[0:1, part]
+    gains = gain_grads_stream(copies, own, recv_gain, sum_gain, plane, gains_ref)
+    next(gains)
+    next(second)
+    next(wd)
+    next(wo)
+    next(second)
+    next(qkv)
+    gather_qkv = gather_stream(copies, qkvsum, qkv_all, twin=False)
+    next(gather_qkv)
+    gather_gu = gather_stream(copies, gusum_ref, gu_all, twin=False)
+    next(gather_gu)
+    next(second)
+    for n in range(PLANE):
+        part = slice(n * chunk, (n + 1) * chunk)
+        low_out = (h1_ref[part] + mixed[part]).astype(BF16)
+        mid_b[1, n] = low_out
+    output = outward_stream(copies, mid_b.at[1], mid_b.at[0], out_ref)
+    next(output)
+    next(gains)
+    next(tokens)
+    next(gather_qkv)
+    next(wd)
+    next(wo)
+    next(gather_gu)
+    next(output)
+    for stream in (gather_qkv, gather_qkv, gather_gu, gather_gu, tokens, gains, wd, wo, output):
+        next(stream)
+    copies.finish()
+
+
+def last(partial, mixed, x, h1, dh1, lines, gain2, gate_up_sum, qkv_grad, out_grad, down_grad):
+    ranks = PLANE * CORES
+    rows, width = h1.shape
+    quarter = width // PLANE
+    small = lines.shape[1:]
+    shapes = (
+        jax.ShapeDtypeStruct((rows, width), BF16),
+        jax.ShapeDtypeStruct((rows, width), BF16),
+        jax.ShapeDtypeStruct(small, F32),
+        jax.ShapeDtypeStruct((PLANE,) + gate_up_sum.shape, BF16),
+        jax.ShapeDtypeStruct((PLANE, CORES) + qkv_grad.shape[1:], BF16),
+        jax.ShapeDtypeStruct(out_grad.shape, BF16),
+        jax.ShapeDtypeStruct(down_grad.shape, BF16),
+    )
+    scratch = scatter_scratch(rows, width) * 2
+    scratch += [pltpu.VMEM((rows, width), F32)] * 2
+    scratch += [pltpu.VMEM(x.shape, BF16)] * 2 + [pltpu.VMEM((2,) + x.shape, BF16)]
+    scratch += [pltpu.VMEM((CORES, PLANE) + qkv_grad.shape[1:], BF16)]
+    scratch += [pltpu.VMEM((CORES,) + qkv_grad.shape[1:], BF16)]
+    for grad in (out_grad, down_grad):
+        scratch += [pltpu.VMEM((PLANE, grad.shape[0], quarter), BF16)] * 2
+        scratch += [pltpu.VMEM((grad.shape[0], quarter), BF16)]
+    scratch += [pltpu.VMEM(lines.shape, F32)] * 2 + [pltpu.VMEM(small, F32), pltpu.VMEM((PLANE,) + small, F32)]
+    return comm_call(
+        last_kernel, "last", 4, shapes,
+        [ANY, ANY] + [IN_VMEM] * 5 + [ANY] * 4,
+        (ANY, ANY, IN_VMEM, ANY, ANY, ANY, ANY),
+        scratch, 48,
+    )(partial, mixed, x, h1, dh1, lines, gain2, gate_up_sum, qkv_grad, out_grad, down_grad)
+
+
+def feed_kernel(n2_ref, cot_ref, wgu_ref, wd_ref, mix_ref, dn2_ref, ggu_ref, gd_ref, wgu_t, wd_t, wd_p, ggu, gd):
+    step = pl.program_id(0)
+    hidden, lanes = wd_ref.shape[0], wd_p.shape[0]
+
+    @pl.when(step == 0)
+    def _():
+        wd_p[...] = jnp.zeros_like(wd_p)
+        wd_p[0:hidden] = wd_ref[...]
+        for s in range(wgu_ref.shape[0]):
+            shard = wgu_ref.shape[1]
+            wgu_t[:, s * shard : (s + 1) * shard] = wgu_ref[s].T
+        wd_t[...] = wd_p[...].T
+        ggu[...] = jnp.zeros_like(ggu)
+        gd[...] = jnp.zeros_like(gd)
+
+    block, cot = n2_ref[0], cot_ref[0]
+    gate_up = matmul(block, wgu_ref[...].reshape(-1, 2 * lanes))
+    gate, upper = gate_up[:, :lanes], gate_up[:, lanes:]
+    cubic = 0.7978845608028654 * (gate + 0.044715 * gate * gate * gate)
+    bend = jnp.tanh(cubic)
+    half = 0.5 * (1.0 + bend)
+    active = gate * half
+    slope = half + (0.5 * 0.7978845608028654) * gate * (1.0 - bend * bend) * (
+        1.0 + 3 * 0.044715 * gate * gate
+    )
+    mixed = (active * upper).astype(BF16)
+    mix_ref[0] = matmul(mixed, wd_p[...]).astype(BF16)
+    du = matmul(cot, wd_t[...])
+    dab = jnp.concatenate([(du * upper * slope).astype(BF16), (du * active).astype(BF16)], axis=1)
+    dn2_ref[0] = matmul(dab, wgu_t[...]).astype(BF16)
+    ggu[...] += inner(block, dab)
+    gd[...] += inner(mixed, cot)
+
+    @pl.when(step == pl.num_programs(0) - 1)
+    def _():
+        shard = ggu_ref.shape[1]
+        for s in range(ggu_ref.shape[0]):
+            ggu_ref[s] = ggu[s * shard : (s + 1) * shard].astype(BF16)
+        gd_ref[...] = gd[0:hidden].astype(BF16)
+
+
+def feed(n2, cot, w_gu, w_d):
+    ranks, rows, width = n2.shape
+    lanes = w_gu.shape[2] // 2
+    block = pl.BlockSpec((1, rows, width), lambda i: (i, 0, 0))
+    whole3 = pl.BlockSpec(w_gu.shape, lambda i: (0, 0, 0))
+    whole2 = pl.BlockSpec(w_d.shape, lambda i: (0, 0))
+    tokens = jax.ShapeDtypeStruct(n2.shape, BF16)
+    return pl.pallas_call(
+        feed_kernel,
+        grid=(ranks,),
+        out_shape=(
+            tokens, tokens,
+            jax.ShapeDtypeStruct(w_gu.shape, BF16),
+            jax.ShapeDtypeStruct(w_d.shape, BF16),
+        ),
+        in_specs=[block, block, whole3, whole2],
+        out_specs=(block, block, whole3, whole2),
+        scratch_shapes=[
+            pltpu.VMEM((2 * lanes, width), BF16),
+            pltpu.VMEM((width, lanes), BF16),
+            pltpu.VMEM((lanes, width), BF16),
+            pltpu.VMEM((width, 2 * lanes), F32),
+            pltpu.VMEM((lanes, width), F32),
+        ],
+        compiler_params=pltpu.CompilerParams(
+            dimension_semantics=("arbitrary",), vmem_limit_bytes=48 << 20
+        ),
+        name="feed",
+    )(n2, cot, w_gu, w_d)
+
+
+def attend_back_kernel(n1_ref, dqkv_ref, att_ref, ga_ref, wqkv_ref, dn1_ref, gqkv_ref, gwo_ref, w_t, gqkv, gwo):
+    step = pl.program_id(0)
+
+    @pl.when(step == 0)
+    def _():
+        for s in range(wqkv_ref.shape[0]):
+            shard = wqkv_ref.shape[1]
+            w_t[:, s * shard : (s + 1) * shard] = wqkv_ref[s].T
+        gqkv[...] = jnp.zeros_like(gqkv)
+        gwo[...] = jnp.zeros_like(gwo)
+
+    dqkv = dqkv_ref[...]
+    dn1_ref[0] = matmul(dqkv, w_t[...]).astype(BF16)
+    gqkv[...] += inner(n1_ref[0], dqkv)
+    gwo[...] += inner(att_ref[...], ga_ref[0])
+
+    @pl.when(step == pl.num_programs(0) - 1)
+    def _():
+        shard = gqkv_ref.shape[1]
+        for s in range(gqkv_ref.shape[0]):
+            gqkv_ref[s] = gqkv[s * shard : (s + 1) * shard].astype(BF16)
+        gwo_ref[...] = gwo[...].astype(BF16)
+
+
+def attend_back(n1, dqkv, att, ga, w_qkv):
+    ranks, rows, width = n1.shape
+    heads, cols = att.shape[1], dqkv.shape[1]
+    block = pl.BlockSpec((1, rows, width), lambda i: (i, 0, 0))
+    whole3 = pl.BlockSpec(w_qkv.shape, lambda i: (0, 0, 0))
+    return pl.pallas_call(
+        attend_back_kernel,
+        grid=(ranks,),
+        out_shape=(
+            jax.ShapeDtypeStruct(n1.shape, BF16),
+            jax.ShapeDtypeStruct(w_qkv.shape, BF16),
+            jax.ShapeDtypeStruct((heads, width), BF16),
+        ),
+        in_specs=[
+            block,
+            pl.BlockSpec((rows, cols), lambda i: (i, 0)),
+            pl.BlockSpec((rows, heads), lambda i: (i, 0)),
+            block,
+            whole3,
+        ],
+        out_specs=(block, whole3, pl.BlockSpec((heads, width), lambda i: (0, 0))),
+        scratch_shapes=[
+            pltpu.VMEM((cols, width), BF16),
+            pltpu.VMEM((width, cols), F32),
+            pltpu.VMEM((heads, width), F32),
+        ],
+        compiler_params=pltpu.CompilerParams(
+            dimension_semantics=("arbitrary",), vmem_limit_bytes=40 << 20
+        ),
+        name="attend_back",
+    )(n1, dqkv, att, ga, w_qkv)
+
+
+def padded(piece, size):
+    return jnp.pad(piece, ((0, 0), (0, size - piece.shape[1])))
+
+
+def plane_local(
+    tokens,
+    cotangent,
+    block_table,
+    norm1_gain,
+    w_query,
+    w_key,
+    w_value,
+    w_out,
+    norm2_gain,
+    w_gate,
+    w_up,
+    w_down,
+):
+    chip, line, core = lax.axis_index("group"), lax.axis_index("z"), lax.axis_index("core")
+    rows, width = tokens.shape[1:]
+    heads = width // (PLANE * CORES)
+    hidden = w_gate.shape[1] // (PLANE * CORES)
+    lanes = -(-hidden // 128) * 128
+
+    def column(w, size, number):
+        return lax.dynamic_slice_in_dim(w, (chip * CORES + number) * size, size, 1)
+
+    def pieces(weights, size, wide):
+        return jnp.stack([
+            jnp.concatenate([padded(column(w, size, number), wide) for w in weights], axis=1)
+            for number in range(CORES)
+        ])
+
+    table_row = jnp.pad(block_table.astype(F32), ((0, 0), (0, heads - block_table.shape[1])))
+    small = jnp.concatenate([norm1_gain[None].astype(F32), norm2_gain[None].astype(F32), table_row])
+    small = jnp.pad(small, ((0, 5), (0, 0)))
+    n1, x, cot, gains_all, plane_small, w_qkv, w_o = start(
+        tokens[0], cotangent[0], small, pieces((w_query, w_key, w_value), heads, heads), w_out
+    )
+    table = lax.dynamic_index_in_dim(plane_small, line, 0, keepdims=False)
+    table = table[2, : block_table.shape[1]].astype(jnp.int32)
+    cot_all = lax.all_gather(cot.reshape(rows, width), TP, axis=0, tiled=False)
+
+    qkv = matmul(n1.reshape(-1, width), w_qkv.reshape(width, -1)).astype(BF16)
+    att, lse, ot = attend(table, qkv)
+    n2, h1, w_gu, w_d = middle(
+        matmul(att, w_o).astype(BF16), x, gains_all, pieces((w_gate, w_up), hidden, lanes), w_down
+    )
+    mixed, dn2, g_gu, g_down = feed(n2, cot_all, w_gu, w_d)
+    ga, dh1, gain2, gu_sum = back(dn2, h1, cot, gains_all, g_gu)
+    datt = outer(ga.reshape(-1, width), w_o).astype(BF16)
+    dqkv = attend_grad(table, qkv, datt, lse, ot)
+    dn1, g_qkv, g_out = attend_back(n1, dqkv, att, ga, w_qkv)
+    output, tokens_grad, gain_grads, g_gu, g_qkv, g_out, g_down = last(
+        dn1, mixed, x, h1, dh1, gains_all, gain2, gu_sum, g_qkv, g_out, g_down
+    )
+
+    def whole(grad, begin, size):
+        piece = grad[..., begin : begin + size].reshape(-1, grad.shape[2], size)
+        return piece.swapaxes(0, 1).reshape(grad.shape[2], -1).astype(F32)
+
+    return (
+        output[None],
+        tokens_grad[None],
+        gain_grads[0],
+        whole(g_qkv, 0, heads),
+        whole(g_qkv, heads, heads),
+        whole(g_qkv, 2 * heads, heads),
+        g_out.astype(F32),
+        gain_grads[1],
+        whole(g_gu, 0, hidden),
+        whole(g_gu, lanes, hidden),
+        g_down.astype(F32),
+    )
+
+
+def plane_solution(mesh):
+    split = Mesh(mesh.devices.reshape(PLANE, PLANE, CORES), ("group", "z", "core"))
+    ctx = ("z", "core")
+    token, weight = P("group", ctx, None), P(ctx, None)
+    in_specs = (token, token, P("group", None), P(ctx)) + (weight,) * 4 + (P(ctx),) + (weight,) * 3
+    out_specs = (token, token, P(ctx)) + (weight,) * 4 + (P(ctx),) + (weight,) * 3
+    return jax.shard_map(
+        plane_local, mesh=split, in_specs=in_specs, out_specs=out_specs, check_vma=False
+    )
+
+
+def family_solution(mesh):
     in_specs = (
         P("group", "ctx", None),
         P("group", "ctx", None),
@@ -335,3 +1364,10 @@
         P("ctx", None),
     )
     return jax.shard_map(local, mesh=mesh, in_specs=in_specs, out_specs=out_specs, check_vma=False)
+
+
+def solution(mesh):
+    groups, ranks = mesh.shape["group"], mesh.shape["ctx"]
+    if groups == PLANE and ranks == 2 * PLANE:
+        return plane_solution(mesh)
+    return family_solution(mesh)

time: 1100 us -> 387 us (0.35); the launches traced: 1080 us -> 387 us
  waiting for transfers between devices: 713 us -> 0.02 us
  Pallas kernels: 0 us -> 327 us
  matrix products: 181 us -> 7.08 us
  blocking collectives: 48.6 us -> 0 us
  other arithmetic: 44.8 us -> 6.57 us
  local copies, waits for them, and re-layouts: 66.8 us -> 31.5 us
    reduce_scatter x8 -> x0, waiting for transfers between devices: 402 us -> none  [the longest x1 65.8 us: local(): lax.psum_scatter(grad_gate.astype(jnp.bfloat16), 'ctx', scatter_dimension...]
    pallas_call x0 -> x8, Pallas kernels: none -> 327 us  [the longest x1 95.1 us: last(): comm_call(last_kernel, 'last', 4, shapes, [ANY, ANY] + [IN_VMEM] * 5 + [A...]
    all_gather x9 -> x1, waiting for transfers between devices: 253 us -> 0.01 us  [plane_local(): cot_all = lax.all_gather(cot.reshape(rows, width), TP, axis=0, tiled=False)]
    dot_general x35 -> x0, matrix products: 129 us -> none  [the longest x7 26.1 us: inner(): lax.dot_general(left, right, (((0,), (0,)), ((), ())), preferred_element_...]
    psum x1 -> x0, waiting for transfers between devices: 53.3 us -> none  [local(): lax.psum(shards[1].astype(jnp.bfloat16), 'group').astype(jnp.float32)]
    all_gather x2 -> x0, blocking collectives: 23.8 us -> none  [the longest x1 13.5 us: local(): lax.all_gather(norm1_gain, 'ctx', axis=0, tiled=True)]
    dynamic_slice x25 -> x3, local copies, waits for them, and re-layouts: 26.2 us -> 2.92 us  [column(): return lax.dynamic_slice_in_dim(w, (chip * CORES + number) * size, size, 1)]
    dot_general x7 -> x2, matrix products: 28.7 us -> 5.82 us  [matmul(): return jnp.dot(left, right, preferred_element_type=jnp.float32)]
  transfers between devices with their start and end apart: 18 -> 1, of which waited for: 16 -> 0; matrix products, arithmetic and copies ran while one was open for 14% -> 2% of each run, Pallas kernels for 0% -> 20%
where the time goes in v1:
time: 387 us
  Pallas kernels  327 us (84%)
  local copies, waits for them, and re-layouts  31.5 us (8%)
  between operations  14.4 us (4%)
  matrix products  7.08 us (2%)
  other arithmetic  6.57 us (2%)
    pallas_call x1, Pallas kernels, last(): comm_call(last_kernel, 'last', 4, shapes, [ANY, ANY] + [IN_VMEM] * 5 + [A...  95.1 us
    pallas_call x1, Pallas kernels, middle(): comm_call(middle_kernel, 'middle', 2, shapes, [ANY, IN_VMEM, IN_VMEM, ANY...  64.8 us
    pallas_call x1, Pallas kernels, start(): comm_call(start_kernel, 'start', 1, shapes, [ANY] * 5, (ANY, IN_VMEM, ANY...  60.4 us
    pallas_call x1, Pallas kernels, back(): comm_call(back_kernel, 'back', 3, shapes, [ANY, IN_VMEM, IN_VMEM, IN_VMEM...  47.3 us
    unnamed x48, local copies, waits for them, and re-layouts  24.5 us
    pallas_call x1, Pallas kernels, feed(): pl.pallas_call(feed_kernel, grid=(ranks,), out_shape=(tokens, tokens, jax...  23.8 us
    pallas_call x1, Pallas kernels, attend_grad(): pl.pallas_call(attend_grad_kernel, out_shape=jax.ShapeDtypeStruct((total,...  15.7 us
    pallas_call x1, Pallas kernels, attend(): pl.pallas_call(attend_kernel, out_shape=(jax.ShapeDtypeStruct((total, wid...  11 us
  transfers between devices with their start and end apart: 1, of which 0 were waited for; matrix products, arithmetic and copies ran while one was open for 2% of the time, Pallas kernels for 20%

profile of v1, /device:TPU:0, one launch (start us, length us, event | category | flops | bytes accessed | tf_op | source)
XLA Modules:
  0.0 386.5 jit_solution(10491310979472085165)
XLA Ops:
  10.3 1.0 copy-done.14
  11.3 1.0 copy-done.15
  12.4 0.9 copy-done.20
  13.3 60.4 %start.1 = (bf16[8,256,1024]{2,1,0:T(8,128)(2,1)S(1)}, bf16[4,64,1024]{2,1,0:T(8,128)(2,1)S(1)}, bf16[4,64,1024]{2,1,0:T(8,128)(2,1)}, f32[8,8,128]{2,1,0:T(8,12...) custom-call(bf16[256,1024]{1,0:T(8,128)(2,1)S(1)} %bitcast.83, ...), custom_call_target="tpu_custom_call" | custom-call | tf_op jit(solution)/shard_map/start/pallas_call | solution.py:830
  73.7 2.0 copy-done.4
  75.7 4.6 %convolution_convert_fusion.1.qkv_ref = bf16[2048,384]{1,0:T(8,128)(2,1)S(1)} fusion(bf16[2048,1024]{1,0:T(8,128)(2,1)} %bitcast.80, bf16[1024,384]{1,0:T(8,128)(2,1)S(1)} %bitcast.82), kind=kOutput, calls=%fused_computation.1 | convolution fusion | flops 1611399168 | bytes 6553600 | tf_op jit(solution)/shard_map/dot_general | solution.py:30
  80.3 11.0 %attend.1 = (bf16[2048,128]{1,0:T(8,128)(2,1)S(1)}, f32[2,2048]{1,0:T(2,128)S(1)}, bf16[128,2048]{1,0:T(8,128)(2,1)S(1)}) custom-call(s32[16]{0:T(128)S(1)} %convert_bitcast_fusion.3.table_ref, bf16[2048,384]{1,0:T(8,128)(2,1)S(1)} %convolution_convert_fusion.1.qkv_ref), custom_call_target="tpu_custom_call" | custom-call | tf_op jit(solution)/shard_map/attend/pallas_call | solution.py:465
  91.3 1.3 constant_dynamic-slice_fusion.2
  92.8 1.2 convolution_convert_fusion
  94.1 64.8 %middle.1 = (bf16[8,256,1024]{2,1,0:T(8,128)(2,1)S(1)}, f32[256,1024]{1,0:T(8,128)S(1)}, bf16[8,128,768]{2,1,0:T(8,128)(2,1)S(1)}, bf16[352,1024]{1,0:T(8,128)(2,1)S(1)}) custom-call(bf16[8,256,1024]{2,1,0:T(8,128)(2,1)S(1)} %bitcast.79, bf16[4,64,1024]{2,1,0:T(8,128)(2,1)S(1)} %get-tuple-element.48.x_ref, f32[8,8,128]{2,1,0:T(8,128)S(1)} %get-tuple-element.49.line_ref, ...), custom_call_target="tpu_custom_call" | custom-call | tf_op jit(solution)/shard_map/middle/pallas_call | solution.py:888
  158.9 1.9 copy-done.7
  160.8 1.2 copy-done.8
  161.9 0.9 copy-done.12
  162.8 1.8 copy-done.9
  164.6 1.1 copy-done.13
  165.7 23.8 %feed.1 = (bf16[8,256,1024]{2,1,0:T(8,128)(2,1)}, bf16[8,256,1024]{2,1,0:T(8,128)(2,1)}, bf16[8,128,768]{2,1,0:T(8,128)(2,1)S(1)}, bf16[352,1024]{1,0:T(8,128)(2,1)S(1)}) custom-call(bf16[8,256,1024]{2,1,0:T(8,128)(2,1)} %copy-done.7, bf16[8,256,1024]{2,1,0:T(8,128)(2,1)} %all-gather.2.cloned.1.call-done.cot_ref, bf16[8,128,768]{2,1,0:T(8,128)(2,1)S(1)} %copy-done.9, ...), custom_call_target="tpu_custom_call" | custom-call | tf_op jit(solution)/shard_map/feed/pallas_call | solution.py:1170
  189.5 2.2 copy-done.3
  191.7 47.3 %back.1 = (bf16[8,256,1024]{2,1,0:T(8,128)(2,1)S(1)}, f32[256,1024]{1,0:T(8,128)S(1)}, f32[8,1024]{1,0:T(8,128)S(1)}, bf16[2,128,768]{2,1,0:T(8,128)(2,1)S(1)}) custom-call(bf16[8,256,1024]{2,1,0:T(8,128)(2,1)S(1)} %copy-done.3, f32[256,1024]{1,0:T(8,128)S(1)} %get-tuple-element.55.h1_ref, bf16[4,64,1024]{2,1,0:T(8,128)(2,1)} %get-tuple-element.51.cot_ref, ...), custom_call_target="tpu_custom_call" | custom-call | tf_op jit(solution)/shard_map/back/pallas_call | solution.py:1012
  239.1 1.3 convolution_convert_fusion.2.datt_ref
  241.5 15.7 %attend_grad.1.dqkv_ref = bf16[2048,384]{1,0:T(8,128)(2,1)S(1)} custom-call(s32[16]{0:T(128)S(1)} %convert_bitcast_fusion.3.table_ref, bf16[2048,384]{1,0:T(8,128)(2,1)} %copy-done, bf16[2048,128]{1,0:T(8,128)(2,1)S(1)} %convolution_convert_fusion.2.datt_ref, f32[2,2048]{1,0:T(2,128)S(1)} %get-tuple-element.58.lse_ref, ...), custom_call_target="tpu_custom_call" | custom-call | tf_op jit(solution)/shard_map/attend_grad/pallas_call | solution.py:483
  257.2 8.8 %attend_back.1 = (bf16[8,256,1024]{2,1,0:T(8,128)(2,1)S(1)}, bf16[8,128,384]{2,1,0:T(8,128)(2,1)S(1)}, bf16[128,1024]{1,0:T(8,128)(2,1)S(1)}) custom-call(bf16[8,256,1024]{2,1,0:T(8,128)(2,1)S(1)} %copy-done.5, bf16[2048,384]{1,0:T(8,128)(2,1)S(1)} %attend_grad.1.dqkv_ref, bf16[2048,128]{1,0:T(8,128)(2,1)S(1)} %get-tuple-element.46.att_ref, ...), custom_call_target="tpu_custom_call" | custom-call | tf_op jit(solution)/shard_map/attend_back/pallas_call | solution.py:1223
  266.0 2.0 copy-done.1
  267.9 95.1 %last.1 = (bf16[256,1024]{1,0:T(8,128)(2,1)S(1)}, bf16[256,1024]{1,0:T(8,128)(2,1)S(1)}, f32[8,128]{1,0:T(8,128)S(1)}, bf16[4,2,128,768]{3,2,1,0:T(8,128)(2,1)},...) custom-call(bf16[8,256,1024]{2,1,0:T(8,128)(2,1)} %copy-done.1, ...), custom_call_target="tpu_custom_call" | custom-call | tf_op jit(solution)/shard_map/last/pallas_call | solution.py:1114
  363.6 0.8 convert_element_type.126
  364.7 0.9 copy_bitcast_fusion
  365.5 0.9 copy_bitcast_fusion.1
  366.4 0.9 copy_bitcast_fusion.2
  367.3 1.3 convert_element_type.135
  368.9 1.6 copy.39
  370.5 2.9 copy.41
  373.6 1.6 copy.38
  375.2 2.9 copy.40
  (57 shorter events, 7.2 us)
Async XLA Ops:
  7.2 155.6 %all-gather.2.cloned.1.call-start = ((), (), s32[]{:S(2)}) async-start(), calls=%async_computation | async-start | bytes 4718592 | tf_op jit(solution)/shard_map/all_gather | solution.py:1292
  10.3 1.0 copy-start.14
  11.3 1.0 copy-start.15
  12.4 0.9 copy-start.20
  73.7 2.0 copy-start.4
  75.7 17.1 %copy-start.18 = (bf16[128,1024]{1,0:T(8,128)(2,1)}, bf16[128,1024]{1,0:T(8,128)(2,1)S(1)}, u32[]{:S(2)}) copy-start(bf16[128,1024]{1,0:T(8,128)(2,1)S(1)} %get-tuple-element.47) | copy-start | bytes 786436
  80.3 13.7 %copy-start = (bf16[2048,384]{1,0:T(8,128)(2,1)}, bf16[2048,384]{1,0:T(8,128)(2,1)S(1)}, u32[]{:S(2)}) copy-start(bf16[2048,384]{1,0:T(8,128)(2,1)S(1)} %convolution_convert_fusion.1.qkv_ref) | copy-start | bytes 4718596
  92.8 1.3 copy-start.11
  158.9 1.9 copy-start.7
  160.8 1.2 copy-start.8
  161.9 0.9 copy-start.12
  162.8 26.7 %copy-start.2 = (f32[256,1024]{1,0:T(8,128)}, f32[256,1024]{1,0:T(8,128)S(1)}, u32[]{:S(2)}) copy-start(f32[256,1024]{1,0:T(8,128)S(1)} %get-tuple-element.55.h1_ref) | copy-start | bytes 3145732
  162.8 1.8 copy-start.9
  164.6 1.1 copy-start.13
  189.5 2.2 copy-start.3
  191.7 47.3 %copy-start.19 = (bf16[128,1024]{1,0:T(8,128)(2,1)S(1)}, bf16[128,1024]{1,0:T(8,128)(2,1)}, u32[]{:S(2)}) copy-start(bf16[128,1024]{1,0:T(8,128)(2,1)} %copy-done.18) | copy-start | bytes 786436
  239.0 2.0 copy-start.6
  239.0 2.3 copy-start.10
  239.0 2.4 copy-start.16
  240.3 16.9 %copy-start.5 = (bf16[8,256,1024]{2,1,0:T(8,128)(2,1)S(1)}, bf16[8,256,1024]{2,1,0:T(8,128)(2,1)}, u32[]{:S(2)}) copy-start(bf16[8,256,1024]{2,1,0:T(8,128)(2,1)} %copy-done.4) | copy-start | bytes 12582916
  257.2 10.8 %copy-start.17 = (bf16[2,128,768]{2,1,0:T(8,128)(2,1)S(1)}, bf16[2,128,768]{2,1,0:T(8,128)(2,1)}, u32[]{:S(2)}) copy-start(bf16[2,128,768]{2,1,0:T(8,128)(2,1)} %copy-done.16) | copy-start | bytes 1179652
  266.0 2.0 copy-start.1
  364.5 4.1 %copy-start.21 = (bf16[4,2,128,768]{3,2,1,0:T(8,128)(2,1)S(1)}, bf16[4,2,128,768]{3,2,1,0:T(8,128)(2,1)}, u32[]{:S(2)}) copy-start(bf16[4,2,128,768]{3,2,1,0:T(8,128)(2,1)} %get-tuple-element.73) | copy-start | bytes 4718596
Sparse Core Ops, SparseCore 0:
  75.8 48.7 all-gather.1

commit v2 on v0

--- a/solution.py
+++ b/solution.py
@@ -1,6 +1,9 @@
 import jax
 import jax.numpy as jnp
 from jax import lax
+from jax.experimental import pallas as pl
+from jax.experimental.pallas import tpu as pltpu
+from jax.sharding import Mesh
 from jax.sharding import PartitionSpec as P
 
 HEADS = 16
@@ -306,7 +309,973 @@
     )
 
 
-def solution(mesh):
+PLANE = 4
+CORES = 2
+TP = ("group", "core")
+F32 = jnp.float32
+BF16 = jnp.bfloat16
+
+
+def dot_nt(left, right):
+    return lax.dot_general(left, right, (((1,), (1,)), ((), ())), preferred_element_type=F32)
+
+
+def head_mask(rows, head):
+    lane = lax.broadcasted_iota(jnp.int32, (rows, 2 * HEAD), 1)
+    return (lane >= head * HEAD) & (lane < (head + 1) * HEAD)
+
+
+def causal_mask():
+    key = lax.broadcasted_iota(jnp.int32, (CONT, CONT), 0)
+    query = lax.broadcasted_iota(jnp.int32, (CONT, CONT), 1)
+    return key <= query
+
+
+MESH = pl.DeviceIdType.MESH
+COPIES = 224
+
+
+def spots():
+    chip, line, core = lax.axis_index("group"), lax.axis_index("z"), lax.axis_index("core")
+    side = chip + 1 - 2 * lax.rem(chip, 2)
+    over = lax.rem(chip + 2, PLANE)
+    far = PLANE - 1 - chip
+    return chip, line, core, side, over, far
+
+
+def plane_partners():
+    chip, line, core, side, over, far = spots()
+    return [(q, line, core) for q in (far, side, over)]
+
+
+def line_partners():
+    chip, line, core, side, over, far = spots()
+    lines = [lax.rem(line + d, PLANE) for d in range(1, PLANE)]
+    same = [(chip, z, core) for z in lines]
+    return same + [(chip, z, 1 - core) for z in lines] + [(chip, line, 1 - core)]
+
+
+class Copies:
+    def __init__(self, sems, parent=None):
+        self.sems, self.parent = sems, parent
+        self.count, self.started, self.branches = 0, [], []
+
+    def branch(self):
+        self.branches.append(Copies(self.sems, self))
+        return self.branches[-1]
+
+    def number(self):
+        if self.parent is not None:
+            return self.parent.number()
+        self.count += 1
+        return self.count - 1
+
+    def enter(self):
+        barrier = pltpu.get_barrier_semaphore()
+        partners = plane_partners() + line_partners()
+        for partner in partners:
+            pl.semaphore_signal(barrier, inc=1, device_id=partner, device_id_type=MESH)
+        pl.semaphore_wait(barrier, len(partners))
+
+    def send(self, source, target, partner):
+        number = self.number()
+        copy = pltpu.make_async_remote_copy(
+            src_ref=source,
+            dst_ref=target,
+            send_sem=self.sems.at[0, number],
+            recv_sem=self.sems.at[1, number],
+            device_id=partner,
+            device_id_type=MESH,
+        )
+        copy.start()
+        self.started.append(copy)
+        return copy
+
+    def keep(self, source, target):
+        copy = pltpu.make_async_copy(source, target, self.sems.at[0, self.number()])
+        copy.start()
+        return copy
+
+    def finish(self):
+        for copy in self.started:
+            copy.wait_send()
+        self.started = []
+        for branch in self.branches:
+            branch.finish()
+
+
+def arrived(copies):
+    for copy in copies:
+        copy.wait_recv()
+
+
+def finished(copies):
+    for copy in copies:
+        copy.wait()
+
+
+def gather_stream(copies, own_ref, out_ref, twin=True):
+    chip, line, core, side, over, far = spots()
+    half = own_ref.shape[0] // 2
+    to_far, to_side, to_over = plane_partners()
+    to_twin = (chip, line, 1 - core)
+
+    def slot_of(q):
+        return CORES * q + core if twin else q
+
+    def part(slot, number):
+        return out_ref.at[slot, pl.ds(number * half, half)]
+
+    def own(number):
+        return own_ref.at[pl.ds(number * half, half)]
+
+    def on(slot, number, partner):
+        return copies.send(part(slot, number), part(slot, number), partner)
+
+    def share(slot, number):
+        return [on(slot, number, to_twin)] if twin else []
+
+    mine, slot_side, slot_over, slot_far = map(slot_of, (chip, side, over, far))
+    sides, overs = [None, None], [None, None]
+    overs[0] = copies.send(own(0), part(mine, 0), to_over)
+    sides[1] = copies.send(own(1), part(mine, 1), to_side)
+    sides[0] = copies.send(own(0), part(mine, 0), to_side)
+    overs[1] = copies.send(own(1), part(mine, 1), to_over)
+    twins = [copies.send(own(h), part(mine, h), to_twin) for h in range(2)] if twin else []
+    local = copies.keep(own_ref, out_ref.at[mine])
+    yield
+    local.wait()
+    arrived(twins)
+    yield
+    overs[0].wait_recv()
+    far0 = on(slot_over, 0, to_side)
+    twins = share(slot_over, 0)
+    sides[1].wait_recv()
+    far1 = on(slot_side, 1, to_over)
+    twins += share(slot_side, 1)
+    yield
+    sides[0].wait_recv()
+    twins += share(slot_side, 0)
+    overs[1].wait_recv()
+    twins += share(slot_over, 1)
+    yield
+    arrived(twins)
+    yield
+    far0.wait_recv()
+    twins = share(slot_far, 0)
+    far1.wait_recv()
+    twins += share(slot_far, 1)
+    yield
+    arrived(twins)
+    yield
+
+
+def scatter_stream(copies, part_ref, out_ref, scratch):
+    twin, from_side, from_over, go = scratch
+    chip, line, core, side, over, far = spots()
+    rows = out_ref.shape[0]
+    half = rows // 2
+    to_far, to_side, to_over = plane_partners()
+    to_twin = (chip, line, 1 - core)
+    chips = (far, side, over, chip)
+    twins = [[], [], [], []]
+
+    def share(n, h):
+        half_rows = pl.ds(h * half, half)
+        source = part_ref.at[CORES * chips[n] + 1 - core, half_rows]
+        twins[n].append(copies.send(source, twin.at[n, half_rows], to_twin))
+
+    for n, h in ((1, 0), (2, 0), (2, 1), (1, 1), (3, 0), (3, 1)):
+        share(n, h)
+
+    def pair(n, h):
+        part = slice(h * half, (h + 1) * half)
+        twins[n][h].wait_recv()
+        own = part_ref[CORES * chips[n] + core, part]
+        return own.astype(F32) + twin[n, part].astype(F32)
+
+    def put(n, h, value):
+        part = slice(h * half, (h + 1) * half)
+        go[n, part] = value.astype(BF16)
+        return go.at[n, pl.ds(h * half, half)]
+
+    side0 = copies.send(put(1, 0, pair(1, 0)), from_side.at[1], to_side)
+    over1 = copies.send(put(2, 1, pair(2, 1)), from_over.at[2], to_over)
+    yield
+    share(0, 0)
+    share(0, 1)
+    far0 = copies.send(put(0, 0, pair(0, 0)), from_side.at[0], to_side)
+    far1 = copies.send(put(0, 1, pair(0, 1)), from_over.at[0], to_over)
+    yield
+    value = pair(2, 0)
+    far0.wait_recv()
+    over0 = copies.send(put(2, 0, value + from_side[0].astype(F32)), from_over.at[1], to_over)
+    value = pair(1, 1)
+    far1.wait_recv()
+    side1 = copies.send(put(1, 1, value + from_over[0].astype(F32)), from_side.at[2], to_side)
+    yield
+    first, second = pair(3, 0), pair(3, 1)
+    side0.wait_recv()
+    first = first + from_side[1].astype(F32)
+    over1.wait_recv()
+    second = second + from_over[2].astype(F32)
+    over0.wait_recv()
+    out_ref[0:half] = first + from_over[1].astype(F32)
+    side1.wait_recv()
+    out_ref[half:rows] = second + from_side[2].astype(F32)
+    yield
+
+
+def scatter_scratch(rows, width):
+    return [
+        pltpu.VMEM((PLANE, rows, width), BF16),
+        pltpu.VMEM((3, rows // 2, width), BF16),
+        pltpu.VMEM((3, rows // 2, width), BF16),
+        pltpu.VMEM((3, rows, width), BF16),
+    ]
+
+
+def inward_stream(copies, own_ref, mid, out_ref):
+    chip, line, core, side, over, far = spots()
+    chunk = own_ref.shape[0] // PLANE
+
+    def rows(q):
+        return own_ref.at[pl.ds(q * chunk, chunk)]
+
+    sent = [copies.send(rows(q[0]), mid.at[chip], q) for q in plane_partners()]
+    local = copies.keep(rows(chip), mid.at[chip])
+    yield
+    local.wait()
+    arrived(sent)
+    moved = [copies.send(mid.at[q[1]], out_ref.at[line], q) for q in line_partners()[: PLANE - 1]]
+    local = copies.keep(mid.at[line], out_ref.at[line])
+    yield
+    arrived(moved)
+    local.wait()
+    yield
+
+
+def outward_stream(copies, own_ref, mid, out_ref):
+    chip, line, core, side, over, far = spots()
+    chunk = own_ref.shape[1]
+    moved = [copies.send(own_ref.at[q[1]], mid.at[line], q) for q in line_partners()[: PLANE - 1]]
+    local = copies.keep(own_ref.at[line], mid.at[line])
+    yield
+    local.wait()
+    arrived(moved)
+    target = out_ref.at[pl.ds(chip * chunk, chunk)]
+    sent = [copies.send(mid.at[q[0]], target, q) for q in plane_partners()]
+    local = copies.keep(mid.at[chip], target)
+    yield
+    arrived(sent)
+    local.wait()
+    yield
+
+
+def columns_stream(copies, piece_ref, out_ref, lanes):
+    chip, line, core, side, over, far = spots()
+    mine = out_ref.at[CORES * line + core, :, lanes]
+    sent = [copies.send(piece_ref.at[q[2], :, lanes], mine, q) for q in line_partners()]
+    local = copies.keep(piece_ref.at[core, :, lanes], mine)
+    yield
+    arrived(sent)
+    local.wait()
+    yield
+
+
+def rows_stream(copies, shard_ref, mid, out_ref):
+    chip, line, core, side, over, far = spots()
+    width = shard_ref.shape[1] // PLANE
+    quarter = pl.ds(pl.multiple_of(chip * width, width), width)
+    sent = [copies.send(shard_ref.at[:, quarter], mid.at[line], q) for q in line_partners()[: PLANE - 1]]
+    local = copies.keep(shard_ref.at[:, quarter], mid.at[line])
+    yield
+    local.wait()
+    arrived(sent)
+    sent = [copies.send(mid.at[q[0]], out_ref.at[:, quarter], q) for q in plane_partners()]
+    local = copies.keep(mid.at[chip], out_ref.at[:, quarter])
+    yield
+    arrived(sent)
+    local.wait()
+    yield
+
+
+def unit_rows(value):
+    inverse = lax.rsqrt(jnp.mean(value * value, axis=-1, keepdims=True) + EPS)
+    return value * inverse, inverse
+
+
+def comm_call(kernel, name, number, out_shape, in_specs, out_specs, scratch, vmem_mib=32):
+    return pl.pallas_call(
+        kernel,
+        out_shape=out_shape,
+        in_specs=in_specs,
+        out_specs=out_specs,
+        scratch_shapes=scratch + [pltpu.SemaphoreType.DMA((2, COPIES))],
+        compiler_params=pltpu.CompilerParams(
+            collective_id=number, has_side_effects=True, vmem_limit_bytes=vmem_mib << 20
+        ),
+        name=name,
+    )
+
+
+ANY = pl.BlockSpec(memory_space=pl.ANY)
+IN_VMEM = pl.BlockSpec(memory_space=pltpu.VMEM)
+
+
+def gains_of(line_ref, row):
+    return jnp.concatenate([line_ref[s, row : row + 1, :] for s in range(line_ref.shape[0])], axis=1)
+
+
+def column_grads_stream(copies, grad_ref, recv, sum_ref):
+    chip, line, core, side, over, far = spots()
+    sent = [
+        copies.send(grad_ref.at[CORES * q[1] + q[2]], recv.at[core, line], q)
+        for q in line_partners()
+    ]
+    local = copies.keep(grad_ref.at[CORES * line + core], recv.at[core, line])
+    yield
+    arrived(sent)
+    local.wait()
+    for number in range(CORES):
+        total = recv[number, 0].astype(F32)
+        for family in range(1, PLANE):
+            total = total + recv[number, family].astype(F32)
+        sum_ref[number] = total.astype(BF16)
+    yield
+
+
+def row_grads_stream(copies, grad_ref, mid, recv, summed, out_ref):
+    chip, line, core, side, over, far = spots()
+    width = out_ref.shape[1] // PLANE
+
+    def quarter(q):
+        return pl.ds(pl.multiple_of(q * width, width), width)
+
+    sent = [copies.send(grad_ref.at[:, quarter(q[0])], mid.at[chip], q) for q in plane_partners()]
+    local = copies.keep(grad_ref.at[:, quarter(chip)], mid.at[chip])
+    yield
+    local.wait()
+    arrived(sent)
+    sent = [copies.send(mid.at[q[1]], recv.at[line], q) for q in line_partners()[: PLANE - 1]]
+    local = copies.keep(mid.at[line], recv.at[line])
+    yield
+    arrived(sent)
+    local.wait()
+    total = recv[0].astype(F32)
+    for family in range(1, PLANE):
+        total = total + recv[family].astype(F32)
+    summed[...] = total.astype(BF16)
+    sent = [copies.send(summed, out_ref.at[:, quarter(chip)], q) for q in plane_partners()]
+    local = copies.keep(summed, out_ref.at[:, quarter(chip)])
+    yield
+    arrived(sent)
+    local.wait()
+    yield
+
+
+def gain_grads_stream(copies, own, recv, summed, plane, out_ref):
+    chip, line, core, side, over, far = spots()
+    mine = CORES * line + core
+    sent = [copies.send(own.at[CORES * q[1] + q[2]], recv.at[mine], q) for q in line_partners()]
+    local = copies.keep(own.at[mine], recv.at[mine])
+    yield
+    arrived(sent)
+    local.wait()
+    summed[...] = jnp.sum(recv[...], axis=0)
+    sent = [copies.send(summed, plane.at[chip], q) for q in plane_partners()]
+    local = copies.keep(summed, plane.at[chip])
+    yield
+    arrived(sent)
+    local.wait()
+    out_ref[...] = jnp.sum(plane[...], axis=0)
+    yield
+
+
+def norm_back(grad, value, gain):
+    unit, inverse = unit_rows(value)
+    scaled = grad * gain
+    back = inverse * (scaled - unit * jnp.mean(scaled * unit, axis=-1, keepdims=True))
+    return back, jnp.sum(grad * unit, axis=0, keepdims=True)
+
+
+def chunk_row(stored, part, chunk):
+    plane, core, line = 2 * (stored % 2) + part, (stored // 2) % 2, stored // 4
+    return ((plane * CORES + core) * PLANE + line) * chunk
+
+
+def chosen(blocks, flags):
+    value = blocks[0]
+    for block, flag in zip(blocks[1:], flags[1:]):
+        value = jnp.where(flag, block, value)
+    return value
+
+
+def in_place_order(table_ref, source, lanes, target, scale=None):
+    chunk = BLK // 2
+    blocks = source.shape[0] // BLK
+    for place in range(blocks):
+        flags = [table_ref[0, stored] == place for stored in range(blocks)]
+        for part in range(2):
+            rows = [chunk_row(stored, part, chunk) for stored in range(blocks)]
+            block = chosen([source[row : row + chunk, lanes] for row in rows], flags)
+            row = place * BLK + part * chunk
+            target[row : row + chunk, :] = block if scale is None else block * scale
+
+
+def in_gathered_order(table_ref, source, target, lanes):
+    chunk = BLK // 2
+    blocks = source.shape[0] // BLK
+    for stored in range(blocks):
+        flags = [table_ref[0, stored] == place for place in range(blocks)]
+        for part in range(2):
+            rows = [place * BLK + part * chunk for place in range(blocks)]
+            block = chosen([source[row : row + chunk, :] for row in rows], flags)
+            row = chunk_row(stored, part, chunk)
+            target[row : row + chunk, lanes] = block
+
+
+def attend_block(number, prompt, qs, ks, vt, att, ot_ref, lse_ref):
+    start = number * CONT
+    before = min(start, prompt)
+    own_rows = slice(start, start + CONT)
+    query = qs[own_rows, :]
+    outs = []
+    for head in range(2):
+        masked = jnp.where(head_mask(CONT, head), query, jnp.zeros_like(query))
+        own = dot_nt(ks[own_rows, :], masked)
+        own = jnp.where(causal_mask(), own, -1e30)
+        best = jnp.max(own, axis=0, keepdims=True)
+        if before:
+            past = dot_nt(ks[0:before, :], masked)
+            best = jnp.maximum(best, jnp.max(past, axis=0, keepdims=True))
+        terms = jnp.exp(own - best)
+        total_terms = jnp.sum(terms, axis=0, keepdims=True)
+        rows = slice(head * HEAD, (head + 1) * HEAD)
+        out = matmul(vt[rows, own_rows], terms.astype(BF16))
+        if before:
+            terms = jnp.exp(past - best)
+            total_terms = total_terms + jnp.sum(terms, axis=0, keepdims=True)
+            out = out + matmul(vt[rows, 0:before], terms.astype(BF16))
+        outs.append(out / total_terms)
+        lse_ref[head : head + 1, own_rows] = best + jnp.log(total_terms)
+    joined = jnp.concatenate(outs, axis=0)
+    ot_ref[:, own_rows] = joined.astype(BF16)
+    att[own_rows, :] = joined.T.astype(BF16)
+
+
+def chip_slots(group):
+    chip, line, core, side, over, far = spots()
+    if group == 1:
+        return 2 * CORES, lambda n: CORES * (side + lax.div(n, CORES) * (over - side)) + lax.rem(n, CORES)
+    q = chip if group == 0 else far
+    return CORES, lambda n: CORES * q + n
+
+
+def each_slot(group, body):
+    count, slot_of = chip_slots(group)
+
+    @pl.loop(0, count)
+    def _(n):
+        body(slot_of(n))
+
+
+def front_kernel(
+    tok_ref, cot_ref, small_ref, table_ref, wq_ref, wk_ref, wv_ref, wo_ref, wg_ref, wu_ref, wd_ref,
+    n1_out, x_ref, cotp_ref, line_ref, wqkv, wout, qs, ks, vs, ot_ref, lse_ref, att_ref,
+    h1_ref, dn2_ref, mix_out, ggu_ref, gd_ref, table_out,
+    *rest,
+):
+    scratch, other, rest = rest[:4], rest[4:8], rest[8:]
+    mid_x, mid_c, mid_o, mid_d, tables, table, pieces, gate_w, up_w, gu, normed, rest = *rest[:11], rest[11:]
+    n1s, n2s, cots, qkv, vt, att, parts, summed, wgu, wgu_t, wd, wd_t, us, dabs, sems = rest
+    copies = Copies(sems)
+    chip, line, core, side, over, far = spots()
+    total, heads = qkv.shape[0], wo_ref.shape[0]
+    hidden, lanes = wd_ref.shape[0], wd.shape[0]
+    chunk, width = x_ref.shape[1], x_ref.shape[2]
+    ranks = PLANE * CORES
+
+    loads = [copies.keep(wg_ref, gate_w), copies.keep(wu_ref, up_w)]
+    for c in range(CORES):
+        column = pl.ds(pl.multiple_of((CORES * chip + c) * heads, heads), heads)
+        for n, w in enumerate((wq_ref, wk_ref, wv_ref)):
+            loads.append(copies.keep(w.at[:, column], pieces.at[c, :, n * heads : (n + 1) * heads]))
+    copies.enter()
+    tokens = inward_stream(copies, tok_ref, mid_x, x_ref)
+    next(tokens)
+    finished(loads)
+    query_key = columns_stream(copies, pieces, wqkv, pl.ds(0, 2 * heads))
+    next(query_key)
+    mine = CORES * line + core
+    small = [copies.send(small_ref, line_ref.at[mine], q) for q in line_partners()]
+    small += [copies.send(table_ref, tables.at[chip], q) for q in plane_partners()]
+    local = [copies.keep(small_ref, line_ref.at[mine]), copies.keep(table_ref, tables.at[chip])]
+    gu[...] = jnp.zeros_like(gu)
+    for k in range(PLANE):
+        @pl.when(chip == k)
+        def _():
+            for c in range(CORES):
+                begin = (CORES * k + c) * hidden
+                gu[c, :, 0:hidden] = gate_w[:, begin : begin + hidden]
+                gu[c, :, lanes : lanes + hidden] = up_w[:, begin : begin + hidden]
+    wd[hidden:lanes] = jnp.zeros((lanes - hidden, width), BF16)
+    next(tokens)
+    cotangents = inward_stream(copies, cot_ref, mid_c, cotp_ref)
+    next(cotangents)
+    arrived(small)
+    finished(local)
+    load = [copies.keep(tables.at[line], table), copies.keep(tables.at[line], table_out)]
+    next(tokens)
+    value = columns_stream(copies, pieces, wqkv, pl.ds(2 * heads, heads))
+    next(value)
+    out_rows = rows_stream(copies, wo_ref, mid_o, wout)
+    next(out_rows)
+    finished(load)
+    gain = gains_of(line_ref, 0)
+    for n in range(PLANE):
+        unit, ignored = unit_rows(x_ref[n].astype(F32))
+        normed[n * chunk : (n + 1) * chunk] = (unit * gain).astype(BF16)
+    gathering = copies.branch()
+    gather = gather_stream(gathering, normed, n1s)
+    next(gather)
+    next(gather)
+    next(gather)
+    next(query_key)
+    next(value)
+    next(cotangents)
+
+    def project(slot):
+        rows = pl.ds(pl.multiple_of(slot * PLANE * chunk, PLANE * chunk), PLANE * chunk)
+        qkv[rows, :] = matmul(n1s[slot], wqkv[...].reshape(width, 3 * heads)).astype(BF16)
+
+    each_slot(0, project)
+    next(gather)
+    next(gather)
+    each_slot(1, project)
+    next(gather)
+    next(out_rows)
+    next(gather)
+    each_slot(2, project)
+    keep_n1 = copies.keep(n1s, n1_out)
+    next(cotangents)
+    gather_cot = gather_stream(copies, cotp_ref.reshape(PLANE * chunk, width), cots)
+    next(gather_cot)
+    gate_up = columns_stream(copies, gu, wgu, pl.ds(0, 2 * lanes))
+    next(gate_up)
+    down_rows = rows_stream(copies, wd_ref, mid_d, wd.at[pl.ds(0, hidden)])
+    next(down_rows)
+
+    for n, ref in enumerate((qs, ks, vs)):
+        scale = jnp.bfloat16(SCALE) if n == 0 else None
+        in_place_order(table, qkv, slice(n * heads, (n + 1) * heads), ref, scale)
+    for start in range(0, total, CONT):
+        rows = slice(start, start + CONT)
+        vt[:, rows] = vs[rows, :].astype(F32).T.astype(BF16)
+    for number in range(total // CONT):
+        attend_block(number, total // 2, qs, ks, vt, att, ot_ref, lse_ref)
+        if number == 4:
+            next(gather_cot)
+            next(gather_cot)
+    next(gather_cot)
+    in_gathered_order(table, att, att_ref, slice(0, heads))
+    next(out_rows)
+
+    def spread(slot):
+        rows = pl.ds(pl.multiple_of(slot * PLANE * chunk, PLANE * chunk), PLANE * chunk)
+        parts[slot] = matmul(att_ref[rows, :], wout[...]).astype(BF16)
+
+    for group in range(3):
+        each_slot(group, spread)
+    scattering = copies.branch()
+    scatter = scatter_stream(scattering, parts, summed, scratch)
+    next(scatter)
+    next(scatter)
+    for ignored in gather_cot:
+        pass
+    next(scatter)
+    next(scatter)
+    gathering.finish()
+    gain = gains_of(line_ref, 1)
+    for n in range(PLANE):
+        part = slice(n * chunk, (n + 1) * chunk)
+        hidden_rows = x_ref[n].astype(F32) + summed[part]
+        h1_ref[part] = hidden_rows
+        unit, ignored = unit_rows(hidden_rows)
+        normed[part] = (unit * gain).astype(BF16)
+    gather = gather_stream(copies, normed, n2s)
+    next(gather)
+    next(gather)
+    next(gather)
+    next(gate_up)
+    for s in range(ranks):
+        wgu_t[:, s * heads : (s + 1) * heads] = wgu[s].T
+    next(gather)
+    next(down_rows)
+    scattering.finish()
+    next(down_rows)
+    wd_t[...] = wd[...].T
+
+    def feed(slot):
+        block, cot = n2s[slot], cots[slot]
+        both = matmul(block, wgu[...].reshape(width, 2 * lanes))
+        gate, upper = both[:, :lanes], both[:, lanes:]
+        bend = jnp.tanh(0.7978845608028654 * (gate + 0.044715 * gate * gate * gate))
+        half = 0.5 * (1.0 + bend)
+        active = gate * half
+        slope = half + (0.5 * 0.7978845608028654) * gate * (1.0 - bend * bend) * (
+            1.0 + 3 * 0.044715 * gate * gate
+        )
+        mixed = (active * upper).astype(BF16)
+        us[slot] = mixed
+        parts[slot] = matmul(mixed, wd[...]).astype(BF16)
+        du = matmul(cot, wd_t[...])
+        dabs[slot, :, 0:lanes] = (du * upper * slope).astype(BF16)
+        dabs[slot, :, lanes:] = (du * active).astype(BF16)
+        n1s[slot] = matmul(dabs[slot], wgu_t[...]).astype(BF16)
+
+    keep_n1.wait()
+    each_slot(0, feed)
+    next(gather)
+    each_slot(1, feed)
+    next(gather)
+    scatter = scatter_stream(copies, n1s, dn2_ref, other)
+    next(scatter)
+    next(gather)
+    each_slot(2, feed)
+    next(scatter)
+    keep_mix = copies.keep(parts, mix_out)
+
+    def tokens_of(ref, columns):
+        return jnp.concatenate([ref[slot, :, columns] for slot in range(ranks)], axis=0)
+
+    def by_rows(s):
+        columns = pl.ds(pl.multiple_of(s * heads, heads), heads)
+        grad = jnp.zeros((heads, 2 * lanes), F32)
+        for slot in range(ranks):
+            grad = grad + inner(n2s[slot, :, columns], dabs[slot])
+        ggu_ref[s] = grad.astype(BF16)
+
+    pl.loop(0, ranks // 2)(by_rows)
+    next(scatter)
+    pl.loop(ranks // 2, ranks)(by_rows)
+    grad = jnp.zeros((lanes, width), F32)
+    for slot in range(ranks):
+        grad = grad + inner(us[slot], cots[slot])
+    gd_ref[...] = grad[0:hidden].astype(BF16)
+    next(scatter)
+    keep_mix.wait()
+    copies.finish()
+
+
+def front(tokens, cotangent, small, table, w_query, w_key, w_value, w_out, w_gate, w_up, w_down):
+    rows, width = tokens.shape
+    heads, hidden = w_out.shape[0], w_down.shape[0]
+    lanes = -(-hidden // 128) * 128
+    ranks = PLANE * CORES
+    total = ranks * rows
+    chunks, blocks = (PLANE, rows // PLANE, width), (ranks, rows, width)
+    low = lambda *shape: jax.ShapeDtypeStruct(shape, BF16)
+    wide = lambda *shape: jax.ShapeDtypeStruct(shape, F32)
+    shapes = (
+        low(*blocks), low(*chunks), low(*chunks), wide(ranks, *small.shape), low(ranks, heads, 3 * heads),
+        low(heads, width), low(total, heads), low(total, heads), low(total, heads), low(heads, total),
+        wide(2, total), low(total, heads), wide(rows, width), wide(rows, width), low(*blocks),
+        low(ranks, heads, 2 * lanes), low(hidden, width), jax.ShapeDtypeStruct(table.shape, jnp.int32),
+    )
+    held = lambda *shape: pltpu.VMEM(shape, BF16)
+    scratch = scatter_scratch(rows, width) * 2
+    scratch += [held(*chunks), held(*chunks), held(PLANE, heads, width // PLANE), held(PLANE, hidden, width // PLANE)]
+    scratch += [pltpu.VMEM((PLANE,) + table.shape, jnp.int32), pltpu.SMEM(table.shape, jnp.int32)]
+    scratch += [held(CORES, heads, 3 * heads), held(*w_gate.shape), held(*w_up.shape), held(CORES, heads, 2 * lanes)]
+    scratch += [held(rows, width), held(*blocks), held(*blocks), held(*blocks), held(total, 3 * heads)]
+    scratch += [held(heads, total), held(total, heads), held(*blocks), pltpu.VMEM((rows, width), F32)]
+    scratch += [held(ranks, heads, 2 * lanes), held(2 * lanes, width), held(lanes, width), held(width, lanes)]
+    scratch += [held(ranks, rows, lanes), held(ranks, rows, 2 * lanes)]
+    return comm_call(
+        front_kernel, "front", 1, shapes, [ANY] * 11,
+        (ANY,) + (IN_VMEM,) * 13 + (ANY, IN_VMEM, IN_VMEM, ANY),
+        scratch, 60,
+    )(tokens, cotangent, small, table, w_query, w_key, w_value, w_out, w_gate, w_up, w_down)
+
+
+def attend_back_block(number, prompt, qs, ks, vs, gs, kt, ot_ref, lse_ref, dqs, dks, dvs):
+    start = number * CONT
+    own = slice(start, start + CONT)
+    query, grad = qs[own, :], gs[own, :]
+    product = grad.astype(F32).T * ot_ref[:, own].astype(F32)
+    outs = []
+    for head in range(2):
+        rows = slice(head * HEAD, (head + 1) * HEAD)
+        delta = jnp.sum(product[rows], axis=0, keepdims=True)
+        lse = lse_ref[head : head + 1, own]
+        keep = head_mask(CONT, head)
+        query_head = jnp.where(keep, query, jnp.zeros_like(query))
+        grad_head = jnp.where(keep, grad, jnp.zeros_like(grad))
+        dq = None
+        for keys in [own] + ([slice(0, min(start, prompt))] if start else []):
+            prob = jnp.exp(dot_nt(ks[keys, :], query_head) - lse)
+            if keys == own:
+                prob = jnp.where(causal_mask(), prob, 0.0)
+            dprob = dot_nt(vs[keys, :], grad_head)
+            dscore = (prob * (dprob - delta)).astype(BF16)
+            dvs[keys, :] += matmul(prob.astype(BF16), grad_head)
+            dks[keys, :] += matmul(dscore, query_head)
+            term = matmul(kt[rows, keys], dscore)
+            dq = term if dq is None else dq + term
+        outs.append(dq)
+    dqs[own, :] = (jnp.concatenate(outs, axis=0) * SCALE).T.astype(BF16)
+
+
+def rear_kernel(
+    table, summed_ref, h1_ref, cot_ref, x_ref, line_ref, n1_ref, mix_ref, wqkv_ref, wo_ref,
+    qs, ks, vs, ot_ref, lse_ref, att_ref, gu_ref, down_ref,
+    out_ref, grad_ref, gains_ref, gate_out, up_out, q_out, k_out, v_out, wo_all, wd_all,
+    *rest,
+):
+    scratch, other, rest = rest[:4], rest[4:8], rest[8:]
+    n1s, parts, gas, datt, gs, kt, dqs, dks, dvs, dqkv, w_t, rest = *rest[:11], rest[11:]
+    dh1, summed, mixed, low, low_tok, low_out, mid_tok, mid_out, rest = *rest[:8], rest[8:]
+    recv_gu, sum_gu, gu_all, gqkv, recv_qkv, sum_qkv, qkv_all, gwo, rest = *rest[:8], rest[8:]
+    mid_wo, recv_wo, sum_wo, mid_wd, recv_wd, sum_wd, own, recv_gain, sum_gain, plane, sems = rest
+    copies = Copies(sems)
+    total, heads = att_ref.shape
+    ranks = PLANE * CORES
+    chunk, width = x_ref.shape[1], x_ref.shape[2]
+    rows = PLANE * chunk
+    hidden = down_ref.shape[0]
+    lanes = gu_ref.shape[2] // 2
+    load_mix, load_n1 = copies.keep(mix_ref, parts), copies.keep(n1_ref, n1s)
+    copies.enter()
+    gain = gains_of(line_ref, 1)
+    gain2_sum = jnp.zeros((1, width), F32)
+    for n in range(PLANE):
+        part = slice(n * chunk, (n + 1) * chunk)
+        back, by_gain = norm_back(summed_ref[part], h1_ref[part], gain)
+        grad = cot_ref[n].astype(F32) + back
+        gain2_sum = gain2_sum + by_gain
+        dh1[part] = grad
+        low[part] = grad.astype(BF16)
+    gather = gather_stream(copies, low, gas)
+    next(gather)
+    gate_up = column_grads_stream(copies, gu_ref, recv_gu, sum_gu)
+    next(gate_up)
+    for start in range(0, total, CONT):
+        part = slice(start, start + CONT)
+        kt[:, part] = ks[part, :].astype(F32).T.astype(BF16)
+    for s in range(ranks):
+        w_t[:, s * heads : (s + 1) * heads] = wqkv_ref[s].T
+    dks[...] = jnp.zeros_like(dks)
+    dvs[...] = jnp.zeros_like(dvs)
+
+    def slot_rows(slot):
+        return pl.ds(pl.multiple_of(slot * rows, rows), rows)
+
+    def attended_grad(slot):
+        datt[slot_rows(slot), :] = outer(gas[slot], wo_ref[...]).astype(BF16)
+
+    next(gather)
+    each_slot(0, attended_grad)
+    next(gather)
+    next(gather)
+    next(gather)
+    each_slot(1, attended_grad)
+    next(gather)
+    load_mix.wait()
+    mixing = copies.branch()
+    second = scatter_stream(mixing, parts, mixed, other)
+    next(second)
+    next(gather)
+    each_slot(2, attended_grad)
+    in_place_order(table, datt, slice(0, heads), gs)
+    down = row_grads_stream(copies, down_ref, mid_wd, recv_wd, sum_wd, wd_all)
+    for number in range(total // CONT):
+        attend_back_block(number, total // 2, qs, ks, vs, gs, kt, ot_ref, lse_ref, dqs, dks, dvs)
+        if number == 1:
+            next(second)
+        if number == 4:
+            next(second)
+            next(down)
+        if number == 6:
+            next(gate_up)
+            gather_gu = gather_stream(copies, sum_gu, gu_all, twin=False)
+    next(second)
+    for n in range(PLANE):
+        part = slice(n * chunk, (n + 1) * chunk)
+        low_out[n] = (h1_ref[part] + mixed[part]).astype(BF16)
+    output = outward_stream(copies, low_out, mid_out, out_ref)
+    next(output)
+    ks_low, vs_low = gs, datt
+    for start in range(0, total, CONT):
+        part = slice(start, start + CONT)
+        ks_low[part, :] = dks[part, :].astype(BF16)
+        vs_low[part, :] = dvs[part, :].astype(BF16)
+    for n, ref in enumerate((dqs, ks_low, vs_low)):
+        in_gathered_order(table, ref, dqkv, slice(n * heads, (n + 1) * heads))
+    mixing.finish()
+
+    def spread(slot):
+        parts[slot] = matmul(dqkv[slot_rows(slot), :], w_t[...]).astype(BF16)
+
+    each_slot(1, spread)
+    each_slot(0, spread)
+    scatter = scatter_stream(copies, parts, summed, scratch)
+    next(scatter)
+    each_slot(2, spread)
+    next(scatter)
+    load_n1.wait()
+
+    def by_rows(s):
+        columns = pl.ds(pl.multiple_of(s * heads, heads), heads)
+        grad = jnp.zeros((heads, 3 * heads), F32)
+        for slot in range(ranks):
+            grad = grad + inner(n1s[slot, :, columns], dqkv[slot * rows : (slot + 1) * rows, :])
+        gqkv[s] = grad.astype(BF16)
+
+    pl.loop(0, ranks)(by_rows)
+    qkv = column_grads_stream(copies, gqkv, recv_qkv, sum_qkv)
+    next(qkv)
+    grad = jnp.zeros((heads, width), F32)
+    for slot in range(ranks):
+        grad = grad + inner(att_ref[slot * rows : (slot + 1) * rows, :], gas[slot])
+    gwo[...] = grad.astype(BF16)
+    next(scatter)
+    next(scatter)
+    gain = gains_of(line_ref, 0)
+    gain1_sum = jnp.zeros((1, width), F32)
+    for n in range(PLANE):
+        part = slice(n * chunk, (n + 1) * chunk)
+        back, by_gain = norm_back(summed[part], x_ref[n].astype(F32), gain)
+        gain1_sum = gain1_sum + by_gain
+        low_tok[n] = (dh1[part] + back).astype(BF16)
+    tokens = outward_stream(copies, low_tok, mid_tok, grad_ref)
+    next(tokens)
+    own[...] = jnp.zeros_like(own)
+    for s in range(ranks):
+        part = slice(s * heads, (s + 1) * heads)
+        own[s, 0:1] = gain1_sum[:, part]
+        own[s, 1:2] = gain2_sum[:, part]
+    gains = gain_grads_stream(copies, own, recv_gain, sum_gain, plane, gains_ref)
+    next(gains)
+    next(gather_gu)
+    next(down)
+    out_w = row_grads_stream(copies, gwo, mid_wo, recv_wo, sum_wo, wo_all)
+    next(out_w)
+    next(output)
+    next(gather_gu)
+    next(gather_gu)
+    next(qkv)
+    gather_qkv = gather_stream(copies, sum_qkv, qkv_all, twin=False)
+    next(gather_qkv)
+    next(out_w)
+    next(tokens)
+    next(gains)
+    next(gather_gu)
+    for ignored in gather_gu:
+        pass
+    next(down)
+    for chip in range(PLANE):
+        for c in range(CORES):
+            begin = (CORES * chip + c) * hidden
+            gate_out[:, begin : begin + hidden] = gu_all[chip, c, :, 0:hidden]
+            up_out[:, begin : begin + hidden] = gu_all[chip, c, :, lanes : lanes + hidden]
+    next(gather_qkv)
+    next(gather_qkv)
+    next(out_w)
+    for ignored in gather_qkv:
+        pass
+    for chip in range(PLANE):
+        for c in range(CORES):
+            begin = (CORES * chip + c) * heads
+            for n, ref in enumerate((q_out, k_out, v_out)):
+                ref[:, begin : begin + heads] = qkv_all[chip, c, :, n * heads : (n + 1) * heads]
+    for stream in (output, tokens, gains, down, out_w):
+        for ignored in stream:
+            pass
+    copies.finish()
+
+
+def rear(table, summed, h1, cot, x, lines, n1, mixed, w_qkv, w_o, qs, ks, vs, ot, lse, att, gate_up_grad, down_grad, ff):
+    ranks = PLANE * CORES
+    rows, width = h1.shape
+    total, heads = att.shape
+    hidden = down_grad.shape[0]
+    quarter = width // PLANE
+    small = lines.shape[1:]
+    low = lambda *shape: jax.ShapeDtypeStruct(shape, BF16)
+    shapes = (
+        low(rows, width), low(rows, width), jax.ShapeDtypeStruct(small, F32),
+        low(heads, ff), low(heads, ff), low(heads, width), low(heads, width), low(heads, width),
+        low(heads, width), low(hidden, width),
+    )
+    held = lambda *shape: pltpu.VMEM(shape, BF16)
+    wide = lambda *shape: pltpu.VMEM(shape, F32)
+    scratch = scatter_scratch(rows, width) * 2
+    scratch += [held(*n1.shape)] * 3 + [held(total, heads)] * 2 + [held(heads, total), held(total, heads)]
+    scratch += [wide(total, heads)] * 2 + [held(total, 3 * heads), held(3 * heads, width)]
+    scratch += [wide(rows, width)] * 3 + [held(rows, width)] + [held(*x.shape)] * 4
+    for grad in (gate_up_grad, w_qkv):
+        piece = (CORES,) + grad.shape[1:]
+        if grad is w_qkv:
+            scratch += [held(*grad.shape)]
+        scratch += [held(CORES, PLANE, *grad.shape[1:]), held(*piece), held(PLANE, *piece)]
+    scratch += [held(heads, width)]
+    for count in (heads, hidden):
+        scratch += [held(PLANE, count, quarter)] * 2 + [held(count, quarter)]
+    scratch += [wide(*lines.shape)] * 2 + [wide(*small), wide(PLANE, *small)]
+    return comm_call(
+        rear_kernel, "rear", 2, shapes,
+        [pl.BlockSpec(memory_space=pltpu.SMEM)] + [IN_VMEM] * 5 + [ANY] * 2 + [IN_VMEM] * 8 + [ANY] * 2,
+        (ANY, ANY) + (IN_VMEM,) * 6 + (ANY, ANY),
+        scratch, 60,
+    )(table, summed, h1, cot, x, lines, n1, mixed, w_qkv, w_o, qs, ks, vs, ot, lse, att, gate_up_grad, down_grad)
+
+
+def plane_local(
+    tokens,
+    cotangent,
+    block_table,
+    norm1_gain,
+    w_query,
+    w_key,
+    w_value,
+    w_out,
+    norm2_gain,
+    w_gate,
+    w_up,
+    w_down,
+):
+    rows, width = tokens.shape[1:]
+    heads = width // (PLANE * CORES)
+    small = jnp.stack([norm1_gain, norm2_gain]).astype(F32)
+    small = jnp.pad(small, ((0, 6), (0, 0)))
+    tables = jnp.pad(block_table, ((0, 7), (0, heads - block_table.shape[1])))
+    (
+        n1, x, cot, gains, w_qkv, w_o, qs, ks, vs, ot, lse, att, h1, dn2, mixed, g_gu, g_down, table
+    ) = front(tokens[0], cotangent[0], small, tables, w_query, w_key, w_value, w_out, w_gate, w_up, w_down)
+    output, tokens_grad, gain_grads, *grads = rear(
+        table, dn2, h1, cot, x, gains, n1, mixed, w_qkv, w_o, qs, ks, vs, ot, lse, att, g_gu, g_down,
+        w_gate.shape[1],
+    )
+    gate, up, query, key, value, out, down = [grad.astype(F32) for grad in grads]
+    return (
+        output[None], tokens_grad[None],
+        gain_grads[0], query, key, value, out, gain_grads[1], gate, up, down,
+    )
+
+
+def plane_solution(mesh):
+    split = Mesh(mesh.devices.reshape(PLANE, PLANE, CORES), ("group", "z", "core"))
+    ctx = ("z", "core")
+    token, weight = P("group", ctx, None), P(ctx, None)
+    in_specs = (token, token, P("group", None), P(ctx)) + (weight,) * 4 + (P(ctx),) + (weight,) * 3
+    out_specs = (token, token, P(ctx)) + (weight,) * 4 + (P(ctx),) + (weight,) * 3
+    return jax.shard_map(
+        plane_local, mesh=split, in_specs=in_specs, out_specs=out_specs, check_vma=False
+    )
+
+
+def family_solution(mesh):
     in_specs = (
         P("group", "ctx", None),
         P("group", "ctx", None),
@@ -335,3 +1304,10 @@
         P("ctx", None),
     )
     return jax.shard_map(local, mesh=mesh, in_specs=in_specs, out_specs=out_specs, check_vma=False)
+
+
+def solution(mesh):
+    groups, ranks = mesh.shape["group"], mesh.shape["ctx"]
+    if groups == PLANE and ranks == 2 * PLANE:
+        return plane_solution(mesh)
+    return family_solution(mesh)

time: 1100 us -> 309 us (0.28); the launches traced: 1080 us -> 306 us
  waiting for transfers between devices: 713 us -> 0 us
  Pallas kernels: 0 us -> 290 us
  matrix products: 181 us -> 0 us
  local copies, waits for them, and re-layouts: 66.8 us -> 4.31 us
  blocking collectives: 48.6 us -> 0 us
  other arithmetic: 44.8 us -> 10.3 us
  between operations: 15.6 us -> 0.91 us
    reduce_scatter x8 -> x0, waiting for transfers between devices: 402 us -> none  [the longest x1 65.8 us: local(): lax.psum_scatter(grad_gate.astype(jnp.bfloat16), 'ctx', scatter_dimension...]
    pallas_call x0 -> x2, Pallas kernels: none -> 290 us  [the longest x1 159 us: front(): comm_call(front_kernel, 'front', 1, shapes, [ANY] * 11, (ANY,) + (IN_VMEM...]
    all_gather x9 -> x0, waiting for transfers between devices: 253 us -> none  [the longest x1 54.9 us: local(): lax.all_gather(w_up, 'ctx', axis=0, tiled=True)]
    dot_general x49 -> x0, matrix products: 181 us -> none  [the longest x7 28.7 us: matmul(): return jnp.dot(left, right, preferred_element_type=jnp.float32)]
    psum x1 -> x0, waiting for transfers between devices: 53.3 us -> none  [local(): lax.psum(shards[1].astype(jnp.bfloat16), 'group').astype(jnp.float32)]
    dynamic_slice x25 -> x0, local copies, waits for them, and re-layouts: 26.2 us -> none  [the longest x8 12.4 us: step(): key_block = lax.dynamic_slice_in_dim(keys, start, KEYBLK, 0)]
    all_gather x2 -> x0, blocking collectives: 23.8 us -> none  [the longest x1 13.5 us: local(): lax.all_gather(norm1_gain, 'ctx', axis=0, tiled=True)]
    reduce_sum x6 -> x0, other arithmetic: 19.3 us -> none  [the longest x4 18 us: step(): total = total * jnp.exp(best - larger) + jnp.sum(terms, axis=-1)]
  transfers between devices with their start and end apart: 18 -> 0, of which waited for: 16 -> 0; matrix products, arithmetic and copies ran while one was open for 14% -> 0% of each run, Pallas kernels for 0% -> 0%
where the time goes in v2:
time: 309 us; the launch traced here: 306 us
  Pallas kernels  290 us (94%)
  other arithmetic  10.3 us (3%)
  local copies, waits for them, and re-layouts  4.31 us (1%)
    pallas_call x1, Pallas kernels, front(): comm_call(front_kernel, 'front', 1, shapes, [ANY] * 11, (ANY,) + (IN_VMEM...  159 us
    pallas_call x1, Pallas kernels, rear(): comm_call(rear_kernel, 'rear', 2, shapes, [pl.BlockSpec(memory_space=pltp...  131 us
    convert_element_type x7, other arithmetic, plane_local(): grad.astype(F32)  8.98 us

profile of v2, /device:TPU:0, one launch (start us, length us, event | category | flops | bytes accessed | tf_op | source)
XLA Modules:
  0.0 305.9 jit_solution(7565802016460070609)
XLA Ops:
  0.6 1.3 pad.12.table_ref
  1.9 1.3 fusion.3.small_ref
  3.2 159.2 %front.1 = (bf16[8,256,1024]{2,1,0:T(8,128)(2,1)}, bf16[4,64,1024]{2,1,0:T(8,128)(2,1)}, bf16[4,64,1024]{2,1,0:T(8,128)(2,1)}, f32[8,8,128]{2,1,0:T(8,128)}, bf1...) custom-call(bf16[256,1024]{1,0:T(8,128)(2,1)} %bitcast.12, ...), custom_call_target="tpu_custom_call" | custom-call | tf_op jit(solution)/shard_map/front/pallas_call | solution.py:995
  162.4 131.2 %rear.1 = (bf16[256,1024]{1,0:T(8,128)(2,1)}, bf16[256,1024]{1,0:T(8,128)(2,1)}, f32[8,128]{1,0:T(8,128)}, bf16[128,2816]{1,0:T(8,128)(2,1)}, bf16[128,2816]{1,0...) custom-call(s32[8,128]{1,0:T(8,128)} %get-tuple-element.39.table, ...), custom_call_target="tpu_custom_call" | custom-call | tf_op jit(solution)/shard_map/rear/pallas_call | solution.py:1226
  293.6 0.0 copy-start.6
  293.6 0.0 copy-start.5
  293.6 1.3 slice_bitcast_fusion
  294.9 0.0 copy-start.2
  294.9 1.9 convert_element_type.24
  296.7 1.8 convert_element_type.25
  298.5 0.0 copy-done.6
  298.5 0.8 convert_element_type.26
  299.4 0.0 copy-done.5
  299.4 0.0 copy-start.1
  299.4 0.8 convert_element_type.27
  300.2 0.0 copy-done.2
  300.2 1.2 convert_element_type.28
  301.4 0.0 copy-done.1
  301.4 0.0 copy-start
  301.4 1.2 convert_element_type.29
  302.6 0.2 copy-done
  302.8 0.0 copy-start.4
  302.8 0.0 copy-start.3
  302.8 1.3 convert_element_type.30
  304.1 0.0 copy-done.4
  304.1 0.8 copy.25
  304.9 0.0 copy-done.3
  304.9 0.8 copy.26
Async XLA Ops:
  293.6 4.9 %copy-start.6 = (bf16[128,1024]{1,0:T(8,128)(2,1)S(1)}, bf16[128,1024]{1,0:T(8,128)(2,1)}, u32[]{:S(2)}) copy-start(bf16[128,1024]{1,0:T(8,128)(2,1)} %get-tuple-element.62) | copy-start | bytes 786436
  293.6 5.8 %copy-start.5 = (bf16[128,1024]{1,0:T(8,128)(2,1)S(1)}, bf16[128,1024]{1,0:T(8,128)(2,1)}, u32[]{:S(2)}) copy-start(bf16[128,1024]{1,0:T(8,128)(2,1)} %get-tuple-element.63) | copy-start | bytes 786436
  294.9 5.3 %copy-start.2 = (bf16[128,2816]{1,0:T(8,128)(2,1)S(1)}, bf16[128,2816]{1,0:T(8,128)(2,1)}, u32[]{:S(2)}) copy-start(bf16[128,2816]{1,0:T(8,128)(2,1)} %get-tuple-element.64) | copy-start | bytes 2162692
  299.4 2.0 copy-start.1
  301.4 1.4 copy-start
  302.8 1.3 copy-start.4
  302.8 2.1 copy-start.3

commit v3 on v2

--- a/solution.py
+++ b/solution.py
@@ -332,7 +332,6 @@
 
 
 MESH = pl.DeviceIdType.MESH
-COPIES = 224
 
 
 def spots():
@@ -358,32 +357,54 @@
 class Copies:
     def __init__(self, sems, parent=None):
         self.sems, self.parent = sems, parent
-        self.count, self.started, self.branches = 0, [], []
+        self.counts, self.started, self.branches = [0, 0], [], []
 
     def branch(self):
         self.branches.append(Copies(self.sems, self))
         return self.branches[-1]
 
-    def number(self):
+    def number(self, side=0):
         if self.parent is not None:
-            return self.parent.number()
-        self.count += 1
-        return self.count - 1
-
-    def enter(self):
+            return self.parent.number(side)
+        self.counts[side] += 1
+        return self.counts[side] - 1
+
+    def left(self):
+        return self.sems[0].at[self.number(0)]
+
+    def enter(self, crossing=False):
         barrier = pltpu.get_barrier_semaphore()
         partners = plane_partners() + line_partners()
+        chip, line, core, side, over, far = spots()
+        if crossing:
+            partners += [(line, lax.rem(line + d, PLANE), core) for d in range(1, PLANE)]
+            partners += [(lax.rem(chip + d, PLANE), chip, core) for d in range(1, PLANE)]
+
+        def greet(partner):
+            pl.semaphore_signal(barrier, inc=1, device_id=partner, device_id_type=MESH)
+
         for partner in partners:
-            pl.semaphore_signal(barrier, inc=1, device_id=partner, device_id_type=MESH)
-        pl.semaphore_wait(barrier, len(partners))
+            greet(partner)
+        if not crossing:
+            pl.semaphore_wait(barrier, len(partners))
+            return
+
+        @pl.when(chip != line)
+        def _():
+            greet((line, line, core))
+            greet((chip, chip, core))
+            pl.semaphore_wait(barrier, len(partners) + 2)
+
+        @pl.when(chip == line)
+        def _():
+            pl.semaphore_wait(barrier, len(partners))
 
     def send(self, source, target, partner):
-        number = self.number()
         copy = pltpu.make_async_remote_copy(
             src_ref=source,
             dst_ref=target,
-            send_sem=self.sems.at[0, number],
-            recv_sem=self.sems.at[1, number],
+            send_sem=self.left(),
+            recv_sem=self.sems[1].at[self.number(1)],
             device_id=partner,
             device_id_type=MESH,
         )
@@ -392,7 +413,7 @@
         return copy
 
     def keep(self, source, target):
-        copy = pltpu.make_async_copy(source, target, self.sems.at[0, self.number()])
+        copy = pltpu.make_async_copy(source, target, self.left())
         copy.start()
         return copy
 
@@ -470,60 +491,65 @@
     yield
 
 
-def scatter_stream(copies, part_ref, out_ref, scratch):
-    twin, from_side, from_over, go = scratch
-    chip, line, core, side, over, far = spots()
-    rows = out_ref.shape[0]
-    half = rows // 2
-    to_far, to_side, to_over = plane_partners()
-    to_twin = (chip, line, 1 - core)
-    chips = (far, side, over, chip)
-    twins = [[], [], [], []]
-
-    def share(n, h):
-        half_rows = pl.ds(h * half, half)
-        source = part_ref.at[CORES * chips[n] + 1 - core, half_rows]
-        twins[n].append(copies.send(source, twin.at[n, half_rows], to_twin))
-
-    for n, h in ((1, 0), (2, 0), (2, 1), (1, 1), (3, 0), (3, 1)):
-        share(n, h)
-
-    def pair(n, h):
-        part = slice(h * half, (h + 1) * half)
-        twins[n][h].wait_recv()
-        own = part_ref[CORES * chips[n] + core, part]
-        return own.astype(F32) + twin[n, part].astype(F32)
-
-    def put(n, h, value):
-        part = slice(h * half, (h + 1) * half)
-        go[n, part] = value.astype(BF16)
-        return go.at[n, pl.ds(h * half, half)]
-
-    side0 = copies.send(put(1, 0, pair(1, 0)), from_side.at[1], to_side)
-    over1 = copies.send(put(2, 1, pair(2, 1)), from_over.at[2], to_over)
-    yield
-    share(0, 0)
-    share(0, 1)
-    far0 = copies.send(put(0, 0, pair(0, 0)), from_side.at[0], to_side)
-    far1 = copies.send(put(0, 1, pair(0, 1)), from_over.at[0], to_over)
-    yield
-    value = pair(2, 0)
-    far0.wait_recv()
-    over0 = copies.send(put(2, 0, value + from_side[0].astype(F32)), from_over.at[1], to_over)
-    value = pair(1, 1)
-    far1.wait_recv()
-    side1 = copies.send(put(1, 1, value + from_over[0].astype(F32)), from_side.at[2], to_side)
-    yield
-    first, second = pair(3, 0), pair(3, 1)
-    side0.wait_recv()
-    first = first + from_side[1].astype(F32)
-    over1.wait_recv()
-    second = second + from_over[2].astype(F32)
-    over0.wait_recv()
-    out_ref[0:half] = first + from_over[1].astype(F32)
-    side1.wait_recv()
-    out_ref[half:rows] = second + from_side[2].astype(F32)
-    yield
+class Scatter:
+    def __init__(self, copies, part_ref, out_ref, scratch):
+        self.copies, self.part_ref, self.out_ref = copies, part_ref, out_ref
+        self.twin, self.from_side, self.from_over, self.go = scratch
+        chip, line, self.core, side, over, far = spots()
+        self.half = out_ref.shape[0] // 2
+        ignored, self.to_side, self.to_over = plane_partners()
+        self.to_twin = (chip, line, 1 - self.core)
+        self.chips = (far, side, over, chip)
+        self.twins = [None] * 4
+
+    def share(self, *numbers):
+        for n in numbers:
+            self.twins[n] = []
+            for h in range(2):
+                rows = pl.ds(h * self.half, self.half)
+                source = self.part_ref.at[CORES * self.chips[n] + 1 - self.core, rows]
+                self.twins[n].append(self.copies.send(source, self.twin.at[n, rows], self.to_twin))
+
+    def _pair(self, n, h):
+        part = slice(h * self.half, (h + 1) * self.half)
+        self.twins[n][h].wait_recv()
+        own = self.part_ref[CORES * self.chips[n] + self.core, part]
+        return own.astype(F32) + self.twin[n, part].astype(F32)
+
+    def _send(self, n, h, value, target, partner):
+        self.go[n, h * self.half : (h + 1) * self.half] = value.astype(BF16)
+        return self.copies.send(self.go.at[n, pl.ds(h * self.half, self.half)], target, partner)
+
+    def far(self):
+        self.far0 = self._send(0, 0, self._pair(0, 0), self.from_side.at[0], self.to_side)
+        self.far1 = self._send(0, 1, self._pair(0, 1), self.from_over.at[0], self.to_over)
+
+    def side(self):
+        self.side0 = self._send(1, 0, self._pair(1, 0), self.from_side.at[1], self.to_side)
+
+    def over(self):
+        self.over1 = self._send(2, 1, self._pair(2, 1), self.from_over.at[2], self.to_over)
+
+    def cross(self):
+        value = self._pair(2, 0)
+        self.far0.wait_recv()
+        value = value + self.from_side[0].astype(F32)
+        self.over0 = self._send(2, 0, value, self.from_over.at[1], self.to_over)
+        value = self._pair(1, 1)
+        self.far1.wait_recv()
+        value = value + self.from_over[0].astype(F32)
+        self.side1 = self._send(1, 1, value, self.from_side.at[2], self.to_side)
+
+    def end(self):
+        first, second = self._pair(3, 0), self._pair(3, 1)
+        self.side0.wait_recv()
+        first = first + self.from_side[1].astype(F32)
+        self.over1.wait_recv()
+        second = second + self.from_over[2].astype(F32)
+        self.over0.wait_recv()
+        self.out_ref[0 : self.half] = first + self.from_over[1].astype(F32)
+        self.side1.wait_recv()
+        self.out_ref[self.half :] = second + self.from_side[2].astype(F32)
 
 
 def scatter_scratch(rows, width):
@@ -538,16 +564,21 @@
 def inward_stream(copies, own_ref, mid, out_ref):
     chip, line, core, side, over, far = spots()
     chunk = own_ref.shape[0] // PLANE
-
-    def rows(q):
-        return own_ref.at[pl.ds(q * chunk, chunk)]
-
-    sent = [copies.send(rows(q[0]), mid.at[chip], q) for q in plane_partners()]
-    local = copies.keep(rows(chip), mid.at[chip])
-    yield
-    local.wait()
-    arrived(sent)
-    moved = [copies.send(mid.at[q[1]], out_ref.at[line], q) for q in line_partners()[: PLANE - 1]]
+    half = chunk // 2
+    sent, moved, local = [[], []], [], []
+    for h in range(2):
+        part = pl.ds(h * half, half)
+        for q in plane_partners():
+            rows = own_ref.at[pl.ds(q[0] * chunk + h * half, half)]
+            sent[h].append(copies.send(rows, mid.at[chip, part], q))
+    local = [copies.keep(own_ref.at[pl.ds(chip * chunk, chunk)], mid.at[chip])]
+    yield
+    finished(local)
+    for h in range(2):
+        part = pl.ds(h * half, half)
+        arrived(sent[h])
+        for q in line_partners()[: PLANE - 1]:
+            moved.append(copies.send(mid.at[q[1], part], out_ref.at[line, part], q))
     local = copies.keep(mid.at[line], out_ref.at[line])
     yield
     arrived(moved)
@@ -555,21 +586,61 @@
     yield
 
 
-def outward_stream(copies, own_ref, mid, out_ref):
-    chip, line, core, side, over, far = spots()
-    chunk = own_ref.shape[1]
-    moved = [copies.send(own_ref.at[q[1]], mid.at[line], q) for q in line_partners()[: PLANE - 1]]
-    local = copies.keep(own_ref.at[line], mid.at[line])
-    yield
-    local.wait()
-    arrived(moved)
-    target = out_ref.at[pl.ds(chip * chunk, chunk)]
-    sent = [copies.send(mid.at[q[0]], target, q) for q in plane_partners()]
-    local = copies.keep(mid.at[chip], target)
-    yield
-    arrived(sent)
-    local.wait()
-    yield
+class Outward:
+    def __init__(self, copies, own_ref, out_ref):
+        self.chip, self.line, self.core = (lax.axis_index(name) for name in ("group", "z", "core"))
+        self.copies, self.chunk, self.out_ref = copies, own_ref.shape[1], out_ref
+        self.arrive = [copies.number(1) for ignored in range(PLANE)]
+        self.sends, self.away = [], self.chip != self.line
+        for d in range(PLANE):
+            z = lax.rem(self.line + d, PLANE)
+            copy = self._copy(own_ref.at[z], self.chip, z, copies.left())
+            self.sends.append(copy)
+            if d:
+                copy.start()
+        self.local = pltpu.make_async_copy(
+            own_ref.at[self.line], self._rows(self.chip), copies.left()
+        )
+
+        @pl.when(self.away)
+        def _():
+            self.sends[0].start()
+
+        @pl.when(self.chip == self.line)
+        def _():
+            self.local.start()
+
+    def _rows(self, chip):
+        return self.out_ref.at[pl.ds(pl.multiple_of(chip * self.chunk, self.chunk), self.chunk)]
+
+    def _copy(self, source, chip, z, left):
+        return pltpu.make_async_remote_copy(
+            src_ref=source,
+            dst_ref=self._rows(chip),
+            send_sem=left,
+            recv_sem=self.copies.sems[1].at[self.arrive[0] + chip],
+            device_id=(self.line, z, self.core),
+            device_id_type=MESH,
+        )
+
+    def wait(self):
+        for chip in range(PLANE):
+            copy = self._copy(self._rows(chip), chip, self.line, self.copies.sems[0].at[0])
+
+            @pl.when((chip != self.chip) | self.away)
+            def _():
+                copy.wait_recv()
+
+        @pl.when(self.chip == self.line)
+        def _():
+            self.local.wait()
+
+        @pl.when(self.away)
+        def _():
+            self.sends[0].wait_send()
+
+        for copy in self.sends[1:]:
+            copy.wait_send()
 
 
 def columns_stream(copies, piece_ref, out_ref, lanes):
@@ -583,17 +654,112 @@
     yield
 
 
-def rows_stream(copies, shard_ref, mid, out_ref):
+class Relay:
+    def __init__(self, copies, piece, slot, both=True):
+        self.line, self.core = lax.axis_index("z"), lax.axis_index("core")
+        self.copies, self.slot, self.both = copies, slot, both
+        self.cores = range(CORES) if both else (self.core,)
+        self.twin = None
+        count = PLANE * CORES if both else PLANE
+        self.arrive = [copies.number(1) for ignored in range(count)]
+        self.sends = []
+        mine = slot(self.line, self.core)
+        if both:
+            self.twin = self._copy(piece(1 - self.core), mine, self.line, self.core, self.line, 1 - self.core, copies.left())
+            self.twin.start()
+        self.local = copies.keep(piece(self.core), mine)
+        for step in (1, -1):
+            for core in self.cores:
+                copy = self._copy(piece(core), mine, self.line, self.core, self.line + step, core, copies.left())
+                self._start(self._inside(self.line + step), copy)
+
+    def _inside(self, z):
+        return (z >= 0) & (z < PLANE)
+
+    def _sem(self, z, core):
+        number = CORES * z + core if self.both else z
+        return self.copies.sems[1].at[self.arrive[0] + number]
+
+    def _copy(self, source, target, z, core, to, to_core, left=None):
+        return pltpu.make_async_remote_copy(
+            src_ref=source,
+            dst_ref=target,
+            send_sem=self.copies.sems[0].at[0] if left is None else left,
+            recv_sem=self._sem(z, core),
+            device_id=(lax.axis_index("group"), to, to_core),
+            device_id_type=MESH,
+        )
+
+    def _start(self, when, copy):
+        @pl.when(when)
+        def _():
+            copy.start()
+
+        self.sends.append((when, copy))
+
+    def hop(self, distance):
+        if distance == 1:
+            self.local.wait()
+            if self.both:
+                self._copy(*[self.slot(self.line, 1 - self.core)] * 2, self.line, 1 - self.core, self.line, self.core).wait_recv()
+        for step in (1, -1):
+            z = self.line - step * distance
+            there, on = self._inside(z), self._inside(z) & self._inside(self.line + step)
+            for core in self.cores:
+                slot = self.slot(jnp.clip(z, 0, PLANE - 1), core)
+                left = self.copies.left() if distance < PLANE - 1 else None
+                copy = self._copy(slot, slot, jnp.clip(z, 0, PLANE - 1), core, self.line + step, self.core, left)
+
+                @pl.when(there)
+                def _():
+                    copy.wait_recv()
+
+                if distance < PLANE - 1:
+                    self._start(on, copy)
+
+    def finish(self):
+        if self.both:
+            self.twin.wait_send()
+        for when, copy in self.sends:
+            @pl.when(when)
+            def _():
+                copy.wait_send()
+
+
+def columns_relay(copies, piece_ref, out_ref, lanes):
+    return Relay(
+        copies,
+        lambda core: piece_ref.at[core, :, lanes],
+        lambda z, core: out_ref.at[CORES * z + core, :, lanes],
+    )
+
+
+def sum_stream(copies, grad_ref, recv, sum_ref):
     chip, line, core, side, over, far = spots()
-    width = shard_ref.shape[1] // PLANE
-    quarter = pl.ds(pl.multiple_of(chip * width, width), width)
-    sent = [copies.send(shard_ref.at[:, quarter], mid.at[line], q) for q in line_partners()[: PLANE - 1]]
-    local = copies.keep(shard_ref.at[:, quarter], mid.at[line])
-    yield
+    sent = [
+        copies.send(grad_ref.at[q[1]], recv.at[line], q) for q in line_partners()[: PLANE - 1]
+    ]
+    local = copies.keep(grad_ref.at[line], recv.at[line])
+    yield
+    arrived(sent)
     local.wait()
-    arrived(sent)
-    sent = [copies.send(mid.at[q[0]], out_ref.at[:, quarter], q) for q in plane_partners()]
-    local = copies.keep(mid.at[chip], out_ref.at[:, quarter])
+    total = recv[0].astype(F32)
+    for family in range(1, PLANE):
+        total = total + recv[family].astype(F32)
+    sum_ref[...] = total.astype(BF16)
+    yield
+
+
+def quarter_columns(ref, number):
+    width = ref.shape[1] // PLANE
+    return ref.at[:, pl.ds(pl.multiple_of(number * width, width), width)]
+
+
+def to_ranks_stream(copies, mid, out_ref):
+    chip, line, core, side, over, far = spots()
+    target = quarter_columns(out_ref, chip)
+    sent = [copies.send(mid.at[q[0]], target, q) for q in plane_partners()]
+    local = copies.keep(mid.at[chip], target)
     yield
     arrived(sent)
     local.wait()
@@ -605,13 +771,13 @@
     return value * inverse, inverse
 
 
-def comm_call(kernel, name, number, out_shape, in_specs, out_specs, scratch, vmem_mib=32):
+def comm_call(kernel, name, number, out_shape, in_specs, out_specs, scratch, sends, arrivals, vmem_mib=60):
     return pl.pallas_call(
         kernel,
         out_shape=out_shape,
         in_specs=in_specs,
         out_specs=out_specs,
-        scratch_shapes=scratch + [pltpu.SemaphoreType.DMA((2, COPIES))],
+        scratch_shapes=scratch + [pltpu.SemaphoreType.DMA((sends,)), pltpu.SemaphoreType.DMA((arrivals,))],
         compiler_params=pltpu.CompilerParams(
             collective_id=number, has_side_effects=True, vmem_limit_bytes=vmem_mib << 20
         ),
@@ -699,6 +865,9 @@
     return back, jnp.sum(grad * unit, axis=0, keepdims=True)
 
 
+TABLE_ROW = 2
+
+
 def chunk_row(stored, part, chunk):
     plane, core, line = 2 * (stored % 2) + part, (stored // 2) % 2, stored // 4
     return ((plane * CORES + core) * PLANE + line) * chunk
@@ -715,7 +884,7 @@
     chunk = BLK // 2
     blocks = source.shape[0] // BLK
     for place in range(blocks):
-        flags = [table_ref[0, stored] == place for stored in range(blocks)]
+        flags = [table_ref[TABLE_ROW, stored] == float(place) for stored in range(blocks)]
         for part in range(2):
             rows = [chunk_row(stored, part, chunk) for stored in range(blocks)]
             block = chosen([source[row : row + chunk, lanes] for row in rows], flags)
@@ -727,7 +896,7 @@
     chunk = BLK // 2
     blocks = source.shape[0] // BLK
     for stored in range(blocks):
-        flags = [table_ref[0, stored] == place for place in range(blocks)]
+        flags = [table_ref[TABLE_ROW, stored] == float(place) for place in range(blocks)]
         for part in range(2):
             rows = [place * BLK + part * chunk for place in range(blocks)]
             block = chosen([source[row : row + chunk, :] for row in rows], flags)
@@ -766,9 +935,9 @@
 
 def chip_slots(group):
     chip, line, core, side, over, far = spots()
-    if group == 1:
+    if group == "near":
         return 2 * CORES, lambda n: CORES * (side + lax.div(n, CORES) * (over - side)) + lax.rem(n, CORES)
-    q = chip if group == 0 else far
+    q = {"own": chip, "side": side, "over": over, "far": far}[group]
     return CORES, lambda n: CORES * q + n
 
 
@@ -781,20 +950,28 @@
 
 
 def front_kernel(
-    tok_ref, cot_ref, small_ref, table_ref, wq_ref, wk_ref, wv_ref, wo_ref, wg_ref, wu_ref, wd_ref,
-    n1_out, x_ref, cotp_ref, line_ref, wqkv, wout, qs, ks, vs, ot_ref, lse_ref, att_ref,
-    h1_ref, dn2_ref, mix_out, ggu_ref, gd_ref, table_out,
+    tok_ref, cot_ref, small_ref, wq_ref, wk_ref, wv_ref, wo_ref, wg_ref, wu_ref, wd_ref,
+    n1_out, x_out, cot_out, line_out, wqkv_out, wo_out, q_out, k_out, v_out, ot_out, lse_out, att_out,
+    h1_out, dn2_out, mix_out, ggu_out, gd_out, table_out,
     *rest,
 ):
     scratch, other, rest = rest[:4], rest[4:8], rest[8:]
-    mid_x, mid_c, mid_o, mid_d, tables, table, pieces, gate_w, up_w, gu, normed, rest = *rest[:11], rest[11:]
-    n1s, n2s, cots, qkv, vt, att, parts, summed, wgu, wgu_t, wd, wd_t, us, dabs, sems = rest
+    x_ref, cotp_ref, line_ref, wqkv, wout, qs, ks, vs, ot_ref, lse_ref, att_ref, rest = *rest[:11], rest[11:]
+    h1_ref, dn2_ref, ggu_ref, gd_ref, rest = *rest[:4], rest[4:]
+    mid_x, mid_c, mid_o, down, tables, table, pieces, gate_w, up_w, gu, normed, rest = *rest[:11], rest[11:]
+    n1s, n2s, cots, qkv, vt, att, parts, summed, wgu, wgu_t, wd, wd_t, us, dabs, *sems = rest
     copies = Copies(sems)
     chip, line, core, side, over, far = spots()
     total, heads = qkv.shape[0], wo_ref.shape[0]
     hidden, lanes = wd_ref.shape[0], wd.shape[0]
     chunk, width = x_ref.shape[1], x_ref.shape[2]
+    rows = PLANE * chunk
     ranks = PLANE * CORES
+    share = hidden // PLANE
+    stores = []
+
+    def store(source, target):
+        stores.append(copies.keep(source, target))
 
     loads = [copies.keep(wg_ref, gate_w), copies.keep(wu_ref, up_w)]
     for c in range(CORES):
@@ -805,98 +982,122 @@
     tokens = inward_stream(copies, tok_ref, mid_x, x_ref)
     next(tokens)
     finished(loads)
-    query_key = columns_stream(copies, pieces, wqkv, pl.ds(0, 2 * heads))
-    next(query_key)
+    query_key = columns_relay(copies, pieces, wqkv, pl.ds(0, 2 * heads))
     mine = CORES * line + core
     small = [copies.send(small_ref, line_ref.at[mine], q) for q in line_partners()]
-    small += [copies.send(table_ref, tables.at[chip], q) for q in plane_partners()]
-    local = [copies.keep(small_ref, line_ref.at[mine]), copies.keep(table_ref, tables.at[chip])]
+    small += [copies.send(small_ref, tables.at[chip], q) for q in plane_partners()]
+    local = [copies.keep(small_ref, line_ref.at[mine]), copies.keep(small_ref, tables.at[chip])]
+    query_key.hop(1)
+    next(tokens)
+    cotangents = inward_stream(copies, cot_ref, mid_c, cotp_ref)
+    next(cotangents)
+    query_key.hop(2)
     gu[...] = jnp.zeros_like(gu)
     for k in range(PLANE):
         @pl.when(chip == k)
         def _():
             for c in range(CORES):
-                begin = (CORES * k + c) * hidden
-                gu[c, :, 0:hidden] = gate_w[:, begin : begin + hidden]
-                gu[c, :, lanes : lanes + hidden] = up_w[:, begin : begin + hidden]
+                for z in range(PLANE):
+                    begin, at = (CORES * z + c) * hidden + k * share, z * share
+                    gu[c, :, at : at + share] = gate_w[:, begin : begin + share]
+                    gu[c, :, lanes + at : lanes + at + share] = up_w[:, begin : begin + share]
     wd[hidden:lanes] = jnp.zeros((lanes - hidden, width), BF16)
-    next(tokens)
-    cotangents = inward_stream(copies, cot_ref, mid_c, cotp_ref)
-    next(cotangents)
     arrived(small)
     finished(local)
     load = [copies.keep(tables.at[line], table), copies.keep(tables.at[line], table_out)]
+    store(line_ref, line_out)
+    query_key.hop(3)
+    gain = gains_of(line_ref, 0)
     next(tokens)
     value = columns_stream(copies, pieces, wqkv, pl.ds(2 * heads, heads))
     next(value)
-    out_rows = rows_stream(copies, wo_ref, mid_o, wout)
-    next(out_rows)
-    finished(load)
-    gain = gains_of(line_ref, 0)
     for n in range(PLANE):
         unit, ignored = unit_rows(x_ref[n].astype(F32))
         normed[n * chunk : (n + 1) * chunk] = (unit * gain).astype(BF16)
     gathering = copies.branch()
     gather = gather_stream(gathering, normed, n1s)
     next(gather)
-    next(gather)
-    next(gather)
-    next(query_key)
+    finished(load)
+    next(gather)
     next(value)
+    out_quarter = Relay(copies, lambda core: quarter_columns(wo_ref, chip), lambda z, core: mid_o.at[z], False)
     next(cotangents)
 
+    def slot_rows(slot):
+        return pl.ds(pl.multiple_of(slot * rows, rows), rows)
+
     def project(slot):
-        rows = pl.ds(pl.multiple_of(slot * PLANE * chunk, PLANE * chunk), PLANE * chunk)
-        qkv[rows, :] = matmul(n1s[slot], wqkv[...].reshape(width, 3 * heads)).astype(BF16)
-
-    each_slot(0, project)
-    next(gather)
-    next(gather)
-    each_slot(1, project)
-    next(gather)
-    next(out_rows)
-    next(gather)
-    each_slot(2, project)
-    keep_n1 = copies.keep(n1s, n1_out)
-    next(cotangents)
-    gather_cot = gather_stream(copies, cotp_ref.reshape(PLANE * chunk, width), cots)
-    next(gather_cot)
-    gate_up = columns_stream(copies, gu, wgu, pl.ds(0, 2 * lanes))
-    next(gate_up)
-    down_rows = rows_stream(copies, wd_ref, mid_d, wd.at[pl.ds(0, hidden)])
-    next(down_rows)
+        qkv[slot_rows(slot), :] = matmul(n1s[slot], wqkv[...].reshape(width, 3 * heads)).astype(BF16)
+
+    each_slot("own", project)
+    next(gather)
+    out_quarter.hop(1)
+    next(gather)
+    next(gather)
+    out_quarter.hop(2)
+    each_slot("near", project)
+    next(gather)
+    next(gather)
+    each_slot("far", project)
+    for source, target in ((n1s, n1_out), (x_ref, x_out), (wqkv, wqkv_out)):
+        store(source, target)
 
     for n, ref in enumerate((qs, ks, vs)):
         scale = jnp.bfloat16(SCALE) if n == 0 else None
         in_place_order(table, qkv, slice(n * heads, (n + 1) * heads), ref, scale)
+    out_quarter.hop(3)
+    out_rows = to_ranks_stream(copies, mid_o, wout)
+    next(out_rows)
+    next(cotangents)
+    gather_cot = gather_stream(copies, cotp_ref.reshape(rows, width), cots)
+    next(gather_cot)
+    gate_up = columns_relay(copies, gu, wgu, pl.ds(0, 2 * lanes))
+    down_part = wd_ref.at[pl.ds(pl.multiple_of(chip * share, 8), share)]
+    down_rows = Relay(copies, lambda core: down_part, lambda z, core: down.at[z], False)
     for start in range(0, total, CONT):
-        rows = slice(start, start + CONT)
-        vt[:, rows] = vs[rows, :].astype(F32).T.astype(BF16)
+        part = slice(start, start + CONT)
+        vt[:, part] = vs[part, :].astype(F32).T.astype(BF16)
+    for source, target in ((qs, q_out), (ks, k_out), (vs, v_out), (cotp_ref, cot_out)):
+        store(source, target)
     for number in range(total // CONT):
         attend_block(number, total // 2, qs, ks, vt, att, ot_ref, lse_ref)
-        if number == 4:
+        if number == 5:
             next(gather_cot)
             next(gather_cot)
+            gate_up.hop(1)
     next(gather_cot)
+    down_rows.hop(1)
     in_gathered_order(table, att, att_ref, slice(0, heads))
     next(out_rows)
 
     def spread(slot):
-        rows = pl.ds(pl.multiple_of(slot * PLANE * chunk, PLANE * chunk), PLANE * chunk)
-        parts[slot] = matmul(att_ref[rows, :], wout[...]).astype(BF16)
-
-    for group in range(3):
-        each_slot(group, spread)
+        parts[slot] = matmul(att_ref[slot_rows(slot), :], wout[...]).astype(BF16)
+
     scattering = copies.branch()
-    scatter = scatter_stream(scattering, parts, summed, scratch)
-    next(scatter)
-    next(scatter)
-    for ignored in gather_cot:
-        pass
-    next(scatter)
-    next(scatter)
+    scatter = Scatter(scattering, parts, summed, scratch)
+    each_slot("far", spread)
+    scatter.share(0)
+    each_slot("near", spread)
+    scatter.share(1, 2)
+    each_slot("own", spread)
+    scatter.share(3)
+    scatter.far()
+    scatter.side()
+    scatter.over()
+    next(gather_cot)
+    next(gather_cot)
+    gate_up.hop(2)
+    down_rows.hop(2)
+    for source, target in ((wout, wo_out), (ot_ref, ot_out), (lse_ref, lse_out), (att_ref, att_out)):
+        store(source, target)
+    scatter.cross()
+    next(gather_cot)
+    gate_up.hop(3)
+    for s in range(ranks):
+        wgu_t[:, s * heads : (s + 1) * heads] = wgu[s].T
     gathering.finish()
     gain = gains_of(line_ref, 1)
+    scatter.end()
     for n in range(PLANE):
         part = slice(n * chunk, (n + 1) * chunk)
         hidden_rows = x_ref[n].astype(F32) + summed[part]
@@ -905,16 +1106,15 @@
         normed[part] = (unit * gain).astype(BF16)
     gather = gather_stream(copies, normed, n2s)
     next(gather)
-    next(gather)
-    next(gather)
-    next(gate_up)
-    for s in range(ranks):
-        wgu_t[:, s * heads : (s + 1) * heads] = wgu[s].T
-    next(gather)
-    next(down_rows)
+    store(h1_ref, h1_out)
+    down_rows.hop(3)
+    for z in range(PLANE):
+        wd[z * share : (z + 1) * share] = down[z]
+    wd_t[...] = wd[...].T
+    next(gather)
     scattering.finish()
-    next(down_rows)
-    wd_t[...] = wd[...].T
+    finished(stores)
+    stores.clear()
 
     def feed(slot):
         block, cot = n2s[slot], cots[slot]
@@ -934,20 +1134,24 @@
         dabs[slot, :, lanes:] = (du * active).astype(BF16)
         n1s[slot] = matmul(dabs[slot], wgu_t[...]).astype(BF16)
 
-    keep_n1.wait()
-    each_slot(0, feed)
-    next(gather)
-    each_slot(1, feed)
-    next(gather)
-    scatter = scatter_stream(copies, n1s, dn2_ref, other)
-    next(scatter)
-    next(gather)
-    each_slot(2, feed)
-    next(scatter)
-    keep_mix = copies.keep(parts, mix_out)
-
-    def tokens_of(ref, columns):
-        return jnp.concatenate([ref[slot, :, columns] for slot in range(ranks)], axis=0)
+    scatter = Scatter(copies, n1s, dn2_ref, other)
+    each_slot("own", feed)
+    scatter.share(3)
+    next(gather)
+    next(gather)
+    next(gather)
+    each_slot("side", feed)
+    scatter.share(1)
+    next(gather)
+    each_slot("over", feed)
+    scatter.share(2)
+    scatter.side()
+    next(gather)
+    each_slot("far", feed)
+    scatter.share(0)
+    scatter.over()
+    scatter.far()
+    store(parts, mix_out)
 
     def by_rows(s):
         columns = pl.ds(pl.multiple_of(s * heads, heads), heads)
@@ -957,18 +1161,26 @@
         ggu_ref[s] = grad.astype(BF16)
 
     pl.loop(0, ranks // 2)(by_rows)
-    next(scatter)
+    scatter.cross()
     pl.loop(ranks // 2, ranks)(by_rows)
+    store(ggu_ref, ggu_out)
     grad = jnp.zeros((lanes, width), F32)
     for slot in range(ranks):
         grad = grad + inner(us[slot], cots[slot])
-    gd_ref[...] = grad[0:hidden].astype(BF16)
-    next(scatter)
-    keep_mix.wait()
+    for z in range(PLANE):
+        for h in range(2):
+            block = grad[z * share : (z + 1) * share, h * (width // 2) : (h + 1) * (width // 2)]
+            gd_ref[z, h] = block.astype(BF16)
+    store(gd_ref, gd_out)
+    scatter.end()
+    store(dn2_ref, dn2_out)
+    for relay in (query_key, out_quarter, gate_up, down_rows):
+        relay.finish()
     copies.finish()
-
-
-def front(tokens, cotangent, small, table, w_query, w_key, w_value, w_out, w_gate, w_up, w_down):
+    finished(stores)
+
+
+def front(tokens, cotangent, small, w_query, w_key, w_value, w_out, w_gate, w_up, w_down):
     rows, width = tokens.shape
     heads, hidden = w_out.shape[0], w_down.shape[0]
     lanes = -(-hidden // 128) * 128
@@ -977,26 +1189,26 @@
     chunks, blocks = (PLANE, rows // PLANE, width), (ranks, rows, width)
     low = lambda *shape: jax.ShapeDtypeStruct(shape, BF16)
     wide = lambda *shape: jax.ShapeDtypeStruct(shape, F32)
-    shapes = (
-        low(*blocks), low(*chunks), low(*chunks), wide(ranks, *small.shape), low(ranks, heads, 3 * heads),
+    held = [
+        low(*chunks), low(*chunks), wide(ranks, *small.shape), low(ranks, heads, 3 * heads),
         low(heads, width), low(total, heads), low(total, heads), low(total, heads), low(heads, total),
-        wide(2, total), low(total, heads), wide(rows, width), wide(rows, width), low(*blocks),
-        low(ranks, heads, 2 * lanes), low(hidden, width), jax.ShapeDtypeStruct(table.shape, jnp.int32),
-    )
+        wide(2, total), low(total, heads), wide(rows, width), wide(rows, width),
+    ]
+    grads = [low(ranks, heads, 2 * lanes), low(PLANE, 2, hidden // PLANE, width // 2)]
+    shapes = [low(*blocks)] + held + [low(*blocks)] + grads + [wide(*small.shape)]
+    scratch = scatter_scratch(rows, width) * 2
+    scratch += [pltpu.VMEM(a.shape, a.dtype) for a in held + grads]
     held = lambda *shape: pltpu.VMEM(shape, BF16)
-    scratch = scatter_scratch(rows, width) * 2
-    scratch += [held(*chunks), held(*chunks), held(PLANE, heads, width // PLANE), held(PLANE, hidden, width // PLANE)]
-    scratch += [pltpu.VMEM((PLANE,) + table.shape, jnp.int32), pltpu.SMEM(table.shape, jnp.int32)]
+    scratch += [held(*chunks), held(*chunks), held(PLANE, heads, width // PLANE), held(PLANE, hidden // PLANE, width)]
+    scratch += [pltpu.VMEM((PLANE,) + small.shape, F32), pltpu.SMEM(small.shape, F32)]
     scratch += [held(CORES, heads, 3 * heads), held(*w_gate.shape), held(*w_up.shape), held(CORES, heads, 2 * lanes)]
     scratch += [held(rows, width), held(*blocks), held(*blocks), held(*blocks), held(total, 3 * heads)]
     scratch += [held(heads, total), held(total, heads), held(*blocks), pltpu.VMEM((rows, width), F32)]
     scratch += [held(ranks, heads, 2 * lanes), held(2 * lanes, width), held(lanes, width), held(width, lanes)]
     scratch += [held(ranks, rows, lanes), held(ranks, rows, 2 * lanes)]
     return comm_call(
-        front_kernel, "front", 1, shapes, [ANY] * 11,
-        (ANY,) + (IN_VMEM,) * 13 + (ANY, IN_VMEM, IN_VMEM, ANY),
-        scratch, 60,
-    )(tokens, cotangent, small, table, w_query, w_key, w_value, w_out, w_gate, w_up, w_down)
+        front_kernel, "front", 1, tuple(shapes), [ANY] * 10, (ANY,) * len(shapes), scratch, 194, 138,
+    )(tokens, cotangent, small, w_query, w_key, w_value, w_out, w_gate, w_up, w_down)
 
 
 def attend_back_block(number, prompt, qs, ks, vs, gs, kt, ot_ref, lse_ref, dqs, dks, dvs):
@@ -1028,25 +1240,39 @@
 
 
 def rear_kernel(
-    table, summed_ref, h1_ref, cot_ref, x_ref, line_ref, n1_ref, mix_ref, wqkv_ref, wo_ref,
-    qs, ks, vs, ot_ref, lse_ref, att_ref, gu_ref, down_ref,
-    out_ref, grad_ref, gains_ref, gate_out, up_out, q_out, k_out, v_out, wo_all, wd_all,
+    table, summed_in, h1_in, cot_in, x_in, line_in, n1_in, mix_in, wqkv_in, wo_in,
+    q_in, k_in, v_in, ot_in, lse_in, att_in, gu_ref, down_ref,
+    out_ref, grad_ref, gains_ref, gate_end, up_end, q_end, k_end, v_end, wo_all, wd_end,
     *rest,
 ):
     scratch, other, rest = rest[:4], rest[4:8], rest[8:]
+    summed_ref, h1_ref, cot_ref, x_ref, line_ref, wqkv_ref, wo_ref, rest = *rest[:7], rest[7:]
+    qs, ks, vs, ot_ref, lse_ref, att_ref, rest = *rest[:6], rest[6:]
+    gate_out, up_out, q_out, k_out, v_out, wd_out, rest = *rest[:6], rest[6:]
     n1s, parts, gas, datt, gs, kt, dqs, dks, dvs, dqkv, w_t, rest = *rest[:11], rest[11:]
-    dh1, summed, mixed, low, low_tok, low_out, mid_tok, mid_out, rest = *rest[:8], rest[8:]
+    dh1, summed, mixed, low, low_tok, low_out, rest = *rest[:6], rest[6:]
     recv_gu, sum_gu, gu_all, gqkv, recv_qkv, sum_qkv, qkv_all, gwo, rest = *rest[:8], rest[8:]
-    mid_wo, recv_wo, sum_wo, mid_wd, recv_wd, sum_wd, own, recv_gain, sum_gain, plane, sems = rest
+    mid_wo, recv_wo, sum_wo, recv_wd, sum_wd, down_all, own, recv_gain, sum_gain, plane, *sems = rest
     copies = Copies(sems)
     total, heads = att_ref.shape
     ranks = PLANE * CORES
     chunk, width = x_ref.shape[1], x_ref.shape[2]
     rows = PLANE * chunk
-    hidden = down_ref.shape[0]
+    share = down_ref.shape[2]
+    hidden = PLANE * share
     lanes = gu_ref.shape[2] // 2
-    load_mix, load_n1 = copies.keep(mix_ref, parts), copies.keep(n1_ref, n1s)
-    copies.enter()
+
+    def load(*pairs):
+        return [copies.keep(source, target) for source, target in pairs]
+
+    first = load((summed_in, summed_ref), (h1_in, h1_ref), (cot_in, cot_ref), (line_in, line_ref))
+    second_load = load((k_in, ks), (wqkv_in, wqkv_ref), (wo_in, wo_ref))
+    third = load((mix_in, parts))
+    fourth = load((q_in, qs), (v_in, vs), (ot_in, ot_ref), (lse_in, lse_ref), (x_in, x_ref))
+    fifth = load((n1_in, n1s), (att_in, att_ref))
+    stores = []
+    copies.enter(crossing=True)
+    finished(first)
     gain = gains_of(line_ref, 1)
     gain2_sum = jnp.zeros((1, width), F32)
     for n in range(PLANE):
@@ -1060,6 +1286,7 @@
     next(gather)
     gate_up = column_grads_stream(copies, gu_ref, recv_gu, sum_gu)
     next(gate_up)
+    finished(second_load)
     for start in range(0, total, CONT):
         part = slice(start, start + CONT)
         kt[:, part] = ks[part, :].astype(F32).T.astype(BF16)
@@ -1075,36 +1302,39 @@
         datt[slot_rows(slot), :] = outer(gas[slot], wo_ref[...]).astype(BF16)
 
     next(gather)
-    each_slot(0, attended_grad)
-    next(gather)
-    next(gather)
-    next(gather)
-    each_slot(1, attended_grad)
-    next(gather)
-    load_mix.wait()
+    each_slot("own", attended_grad)
+    next(gather)
+    finished(third)
+    next(gather)
+    next(gather)
+    each_slot("near", attended_grad)
+    next(gather)
     mixing = copies.branch()
-    second = scatter_stream(mixing, parts, mixed, other)
-    next(second)
-    next(gather)
-    each_slot(2, attended_grad)
+    second = Scatter(mixing, parts, mixed, other)
+    second.share(0, 1, 2, 3)
+    second.far()
+    second.side()
+    second.over()
+    next(gather)
+    each_slot("far", attended_grad)
     in_place_order(table, datt, slice(0, heads), gs)
-    down = row_grads_stream(copies, down_ref, mid_wd, recv_wd, sum_wd, wd_all)
+    finished(fourth)
+    finished(fifth)
     for number in range(total // CONT):
         attend_back_block(number, total // 2, qs, ks, vs, gs, kt, ot_ref, lse_ref, dqs, dks, dvs)
-        if number == 1:
-            next(second)
-        if number == 4:
-            next(second)
-            next(down)
+        if number == 3:
+            second.cross()
         if number == 6:
             next(gate_up)
             gather_gu = gather_stream(copies, sum_gu, gu_all, twin=False)
-    next(second)
+            next(gather_gu)
+            down = sum_stream(copies, down_ref, recv_wd, sum_wd)
+            next(down)
+    second.end()
     for n in range(PLANE):
         part = slice(n * chunk, (n + 1) * chunk)
         low_out[n] = (h1_ref[part] + mixed[part]).astype(BF16)
-    output = outward_stream(copies, low_out, mid_out, out_ref)
-    next(output)
+    output = Outward(copies, low_out, out_ref)
     ks_low, vs_low = gs, datt
     for start in range(0, total, CONT):
         part = slice(start, start + CONT)
@@ -1113,17 +1343,22 @@
     for n, ref in enumerate((dqs, ks_low, vs_low)):
         in_gathered_order(table, ref, dqkv, slice(n * heads, (n + 1) * heads))
     mixing.finish()
+    next(gather_gu)
+    next(gather_gu)
 
     def spread(slot):
         parts[slot] = matmul(dqkv[slot_rows(slot), :], w_t[...]).astype(BF16)
 
-    each_slot(1, spread)
-    each_slot(0, spread)
-    scatter = scatter_stream(copies, parts, summed, scratch)
-    next(scatter)
-    each_slot(2, spread)
-    next(scatter)
-    load_n1.wait()
+    scatter = Scatter(copies, parts, summed, scratch)
+    each_slot("far", spread)
+    scatter.share(0)
+    each_slot("near", spread)
+    scatter.share(1, 2)
+    each_slot("own", spread)
+    scatter.share(3)
+    scatter.far()
+    scatter.side()
+    scatter.over()
 
     def by_rows(s):
         columns = pl.ds(pl.multiple_of(s * heads, heads), heads)
@@ -1139,8 +1374,25 @@
     for slot in range(ranks):
         grad = grad + inner(att_ref[slot * rows : (slot + 1) * rows, :], gas[slot])
     gwo[...] = grad.astype(BF16)
-    next(scatter)
-    next(scatter)
+    out_w = row_grads_stream(copies, gwo, mid_wo, recv_wo, sum_wo, wo_all)
+    next(out_w)
+    for ignored in gather_gu:
+        pass
+    scatter.cross()
+    next(out_w)
+    next(down)
+    gather_down = gather_stream(copies, sum_wd, down_all, twin=False)
+    next(gather_down)
+
+    def format_gate(chip, c, z):
+        begin, at = (CORES * z + c) * hidden + chip * share, z * share
+        gate_out[:, begin : begin + share] = gu_all[chip, c, :, at : at + share]
+        up_out[:, begin : begin + share] = gu_all[chip, c, :, lanes + at : lanes + at + share]
+
+    places = [(chip, c, z) for chip in range(PLANE) for c in range(CORES) for z in range(PLANE)]
+    for place in places[: len(places) // 2]:
+        format_gate(*place)
+    scatter.end()
     gain = gains_of(line_ref, 0)
     gain1_sum = jnp.zeros((1, width), F32)
     for n in range(PLANE):
@@ -1148,8 +1400,7 @@
         back, by_gain = norm_back(summed[part], x_ref[n].astype(F32), gain)
         gain1_sum = gain1_sum + by_gain
         low_tok[n] = (dh1[part] + back).astype(BF16)
-    tokens = outward_stream(copies, low_tok, mid_tok, grad_ref)
-    next(tokens)
+    tokens = Outward(copies, low_tok, grad_ref)
     own[...] = jnp.zeros_like(own)
     for s in range(ranks):
         part = slice(s * heads, (s + 1) * heads)
@@ -1157,30 +1408,25 @@
         own[s, 1:2] = gain2_sum[:, part]
     gains = gain_grads_stream(copies, own, recv_gain, sum_gain, plane, gains_ref)
     next(gains)
-    next(gather_gu)
-    next(down)
-    out_w = row_grads_stream(copies, gwo, mid_wo, recv_wo, sum_wo, wo_all)
+    next(gather_down)
+    next(gather_down)
     next(out_w)
-    next(output)
-    next(gather_gu)
-    next(gather_gu)
+    for place in places[len(places) // 2 :]:
+        format_gate(*place)
+    stores += load((gate_out, gate_end), (up_out, up_end))
+    for ignored in gather_down:
+        pass
+    for chip in range(PLANE):
+        for h in range(2):
+            wd_out[chip * share : (chip + 1) * share, h * (width // 2) : (h + 1) * (width // 2)] = down_all[chip, h]
+    stores += load((wd_out, wd_end))
     next(qkv)
     gather_qkv = gather_stream(copies, sum_qkv, qkv_all, twin=False)
     next(gather_qkv)
-    next(out_w)
-    next(tokens)
     next(gains)
-    next(gather_gu)
-    for ignored in gather_gu:
-        pass
-    next(down)
-    for chip in range(PLANE):
-        for c in range(CORES):
-            begin = (CORES * chip + c) * hidden
-            gate_out[:, begin : begin + hidden] = gu_all[chip, c, :, 0:hidden]
-            up_out[:, begin : begin + hidden] = gu_all[chip, c, :, lanes : lanes + hidden]
     next(gather_qkv)
     next(gather_qkv)
+    next(gains)
     next(out_w)
     for ignored in gather_qkv:
         pass
@@ -1189,17 +1435,18 @@
             begin = (CORES * chip + c) * heads
             for n, ref in enumerate((q_out, k_out, v_out)):
                 ref[:, begin : begin + heads] = qkv_all[chip, c, :, n * heads : (n + 1) * heads]
-    for stream in (output, tokens, gains, down, out_w):
-        for ignored in stream:
-            pass
+    stores += load((q_out, q_end), (k_out, k_end), (v_out, v_end))
+    output.wait()
+    tokens.wait()
     copies.finish()
+    finished(stores)
 
 
 def rear(table, summed, h1, cot, x, lines, n1, mixed, w_qkv, w_o, qs, ks, vs, ot, lse, att, gate_up_grad, down_grad, ff):
     ranks = PLANE * CORES
     rows, width = h1.shape
     total, heads = att.shape
-    hidden = down_grad.shape[0]
+    hidden = PLANE * down_grad.shape[2]
     quarter = width // PLANE
     small = lines.shape[1:]
     low = lambda *shape: jax.ShapeDtypeStruct(shape, BF16)
@@ -1211,24 +1458,63 @@
     held = lambda *shape: pltpu.VMEM(shape, BF16)
     wide = lambda *shape: pltpu.VMEM(shape, F32)
     scratch = scatter_scratch(rows, width) * 2
+    scratch += [pltpu.VMEM(a.shape, a.dtype) for a in (summed, h1, cot, x, lines, w_qkv, w_o, qs, ks, vs, ot, lse, att)]
+    scratch += [held(*shapes[n].shape) for n in (3, 4, 5, 6, 7, 9)]
     scratch += [held(*n1.shape)] * 3 + [held(total, heads)] * 2 + [held(heads, total), held(total, heads)]
     scratch += [wide(total, heads)] * 2 + [held(total, 3 * heads), held(3 * heads, width)]
-    scratch += [wide(rows, width)] * 3 + [held(rows, width)] + [held(*x.shape)] * 4
+    scratch += [wide(rows, width)] * 3 + [held(rows, width)] + [held(*x.shape)] * 2
     for grad in (gate_up_grad, w_qkv):
         piece = (CORES,) + grad.shape[1:]
         if grad is w_qkv:
             scratch += [held(*grad.shape)]
         scratch += [held(CORES, PLANE, *grad.shape[1:]), held(*piece), held(PLANE, *piece)]
     scratch += [held(heads, width)]
-    for count in (heads, hidden):
-        scratch += [held(PLANE, count, quarter)] * 2 + [held(count, quarter)]
+    scratch += [held(PLANE, heads, quarter)] * 2 + [held(heads, quarter)]
+    scratch += [held(*down_grad.shape), held(*down_grad.shape[1:]), held(*down_grad.shape)]
     scratch += [wide(*lines.shape)] * 2 + [wide(*small), wide(PLANE, *small)]
     return comm_call(
         rear_kernel, "rear", 2, shapes,
-        [pl.BlockSpec(memory_space=pltpu.SMEM)] + [IN_VMEM] * 5 + [ANY] * 2 + [IN_VMEM] * 8 + [ANY] * 2,
-        (ANY, ANY) + (IN_VMEM,) * 6 + (ANY, ANY),
-        scratch, 60,
+        [pl.BlockSpec(memory_space=pltpu.SMEM)] + [ANY] * 17,
+        (ANY, ANY, IN_VMEM) + (ANY,) * 7,
+        scratch, 139, 104,
     )(table, summed, h1, cot, x, lines, n1, mixed, w_qkv, w_o, qs, ks, vs, ot, lse, att, gate_up_grad, down_grad)
+
+
+def finish_kernel(*refs):
+    count = (len(refs) - 1) // 4
+    inputs, outputs, held, stage = (refs[n * count : (n + 1) * count] for n in range(4))
+    sems = refs[-1]
+    loads, stores = [], []
+    for n, (source, buffer) in enumerate(zip(inputs, held)):
+        loads.append(pltpu.make_async_copy(source, buffer, sems.at[0, n]))
+        loads[-1].start()
+    for n, (target, buffer, wide) in enumerate(zip(outputs, held, stage)):
+        loads[n].wait()
+        if buffer.dtype != target.dtype:
+            wide[...] = buffer[...].astype(F32)
+            buffer = wide
+        stores.append(pltpu.make_async_copy(buffer, target, sems.at[1, n]))
+        stores[-1].start()
+    for copy in stores:
+        copy.wait()
+
+
+def finish(tokens, grads):
+    inputs = list(tokens) + list(grads)
+    shapes = [jax.ShapeDtypeStruct(a.shape, a.dtype) for a in tokens]
+    shapes += [jax.ShapeDtypeStruct(a.shape, F32) for a in grads]
+    small = pltpu.VMEM((8, 128), F32)
+    held = [pltpu.VMEM(a.shape, a.dtype) for a in inputs]
+    stage = [small] * len(tokens) + [pltpu.VMEM(a.shape, F32) for a in grads]
+    return pl.pallas_call(
+        finish_kernel,
+        out_shape=tuple(shapes),
+        in_specs=[ANY] * len(inputs),
+        out_specs=(ANY,) * len(inputs),
+        scratch_shapes=held + stage + [pltpu.SemaphoreType.DMA((2, len(inputs)))],
+        compiler_params=pltpu.CompilerParams(vmem_limit_bytes=60 << 20),
+        name="finish",
+    )(*inputs)
 
 
 def plane_local(
@@ -1247,17 +1533,17 @@
 ):
     rows, width = tokens.shape[1:]
     heads = width // (PLANE * CORES)
-    small = jnp.stack([norm1_gain, norm2_gain]).astype(F32)
-    small = jnp.pad(small, ((0, 6), (0, 0)))
-    tables = jnp.pad(block_table, ((0, 7), (0, heads - block_table.shape[1])))
+    table = jnp.pad(block_table.astype(F32), ((0, 0), (0, heads - block_table.shape[1])))
+    small = jnp.concatenate([norm1_gain[None].astype(F32), norm2_gain[None].astype(F32), table])
+    small = jnp.pad(small, ((0, 8 - small.shape[0]), (0, 0)))
     (
         n1, x, cot, gains, w_qkv, w_o, qs, ks, vs, ot, lse, att, h1, dn2, mixed, g_gu, g_down, table
-    ) = front(tokens[0], cotangent[0], small, tables, w_query, w_key, w_value, w_out, w_gate, w_up, w_down)
+    ) = front(tokens[0], cotangent[0], small, w_query, w_key, w_value, w_out, w_gate, w_up, w_down)
     output, tokens_grad, gain_grads, *grads = rear(
         table, dn2, h1, cot, x, gains, n1, mixed, w_qkv, w_o, qs, ks, vs, ot, lse, att, g_gu, g_down,
         w_gate.shape[1],
     )
-    gate, up, query, key, value, out, down = [grad.astype(F32) for grad in grads]
+    output, tokens_grad, gate, up, query, key, value, out, down = finish((output, tokens_grad), grads)
     return (
         output[None], tokens_grad[None],
         gain_grads[0], query, key, value, out, gain_grads[1], gate, up, down,

time: 309 us -> 275 us (0.89)
  Pallas kernels: 290 us -> 266 us
  other arithmetic: 10.3 us -> 1.34 us
    pallas_call x1, Pallas kernels: 131 us -> 116 us  [rear(): comm_call(rear_kernel, 'rear', 2, shapes, [pl.BlockSpec(memory_space=pltp...]
    pallas_call x1 -> x2, Pallas kernels: 159 us -> 150 us  [the longest x1 146 us: front(): comm_call(front_kernel, 'front', 1, tuple(shapes), [ANY] * 10, (ANY,) * l...]
    convert_element_type x7 -> x2, other arithmetic: 8.98 us -> 1.33 us  [the longest x1 0.67 us: plane_local(): norm2_gain[None].astype(F32)]
where the time goes in v3:
time: 275 us; the launch traced here: 270 us
  Pallas kernels  266 us (97%)
    pallas_call x1, Pallas kernels, front(): comm_call(front_kernel, 'front', 1, tuple(shapes), [ANY] * 10, (ANY,) * l...  146 us
    pallas_call x1, Pallas kernels, rear(): comm_call(rear_kernel, 'rear', 2, shapes, [pl.BlockSpec(memory_space=pltp...  116 us

profile of v3, /device:TPU:0, one launch (start us, length us, event | category | flops | bytes accessed | tf_op | source)
XLA Modules:
  0.0 270.1 jit_solution(8000682667436961107)
XLA Ops:
  0.6 0.7 convert_element_type.23
  1.3 0.7 bitcast_convert_fusion
  2.0 0.6 pad.9.small_ref
  2.6 145.6 %front.1 = (bf16[8,256,1024]{2,1,0:T(8,128)(2,1)}, bf16[4,64,1024]{2,1,0:T(8,128)(2,1)}, bf16[4,64,1024]{2,1,0:T(8,128)(2,1)}, f32[8,8,128]{2,1,0:T(8,128)}, bf1...) custom-call(bf16[256,1024]{1,0:T(8,128)(2,1)} %bitcast.14, ...), custom_call_target="tpu_custom_call" | custom-call | tf_op jit(solution)/shard_map/front/pallas_call | solution.py:1209
  148.2 115.8 %rear.1 = (bf16[256,1024]{1,0:T(8,128)(2,1)}, bf16[256,1024]{1,0:T(8,128)(2,1)}, f32[8,128]{1,0:T(8,128)}, bf16[128,2816]{1,0:T(8,128)(2,1)}, bf16[128,2816]{1,0...) custom-call(f32[8,128]{1,0:T(8,128)} %get-tuple-element.48.table, ...), custom_call_target="tpu_custom_call" | custom-call | tf_op jit(solution)/shard_map/rear/pallas_call | solution.py:1475
  264.0 1.3 slice_bitcast_fusion
  265.3 4.4 %finish.1 = (bf16[256,1024]{1,0:T(8,128)(2,1)}, bf16[256,1024]{1,0:T(8,128)(2,1)}, f32[128,2816]{1,0:T(8,128)}, f32[128,2816]{1,0:T(8,128)}, f32[128,1024]{1,0:T...) custom-call(bf16[256,1024]{1,0:T(8,128)(2,1)} %get-tuple-element.66.refs_0_, ...), custom_call_target="tpu_custom_call" | custom-call | tf_op jit(solution)/shard_map/finish/pallas_call | solution.py:1509
  (1 shorter events, 0.0 us)

commit v4 on v3

--- a/solution.py
+++ b/solution.py
@@ -332,6 +332,9 @@
 
 
 MESH = pl.DeviceIdType.MESH
+EARLY = 256
+FRONT_SEMS = (126, 137)
+REAR_SEMS = (114, 104)
 
 
 def spots():
@@ -354,10 +357,20 @@
     return same + [(chip, z, 1 - core) for z in lines] + [(chip, line, 1 - core)]
 
 
+class Kept:
+    def __init__(self, copies, copy, held):
+        self.copies, self.copy, self.held = copies, copy, held
+        copy.start()
+
+    def wait(self):
+        self.copy.wait()
+        self.copies.root().free.extend(self.held)
+
+
 class Copies:
     def __init__(self, sems, parent=None):
         self.sems, self.parent = sems, parent
-        self.counts, self.started, self.branches = [0, 0], [], []
+        self.counts, self.free, self.started, self.branches = [0, 0], [], [], []
 
     def branch(self):
         self.branches.append(Copies(self.sems, self))
@@ -369,8 +382,15 @@
         self.counts[side] += 1
         return self.counts[side] - 1
 
-    def left(self):
-        return self.sems[0].at[self.number(0)]
+    def root(self):
+        return self if self.parent is None else self.parent.root()
+
+    def left(self, held=None):
+        free = self.root().free
+        number = free.pop() if held is not None and free else self.number(0)
+        if held is not None:
+            held.append(number)
+        return self.sems[0].at[number]
 
     def enter(self, crossing=False):
         barrier = pltpu.get_barrier_semaphore()
@@ -399,27 +419,29 @@
         def _():
             pl.semaphore_wait(barrier, len(partners))
 
-    def send(self, source, target, partner):
+    def send(self, source, target, partner, start=True):
+        held = []
         copy = pltpu.make_async_remote_copy(
             src_ref=source,
             dst_ref=target,
-            send_sem=self.left(),
+            send_sem=self.left(held),
             recv_sem=self.sems[1].at[self.number(1)],
             device_id=partner,
             device_id_type=MESH,
         )
-        copy.start()
-        self.started.append(copy)
+        if start:
+            copy.start()
+        self.started.append((copy, held))
         return copy
 
     def keep(self, source, target):
-        copy = pltpu.make_async_copy(source, target, self.left())
-        copy.start()
-        return copy
+        held = []
+        return Kept(self, pltpu.make_async_copy(source, target, self.left(held)), held)
 
     def finish(self):
-        for copy in self.started:
+        for copy, held in self.started:
             copy.wait_send()
+            self.root().free.extend(held)
         self.started = []
         for branch in self.branches:
             branch.finish()
@@ -475,18 +497,27 @@
     far1 = on(slot_side, 1, to_over)
     twins += share(slot_side, 1)
     yield
+    arrived(twins)
+    yield
     sides[0].wait_recv()
-    twins += share(slot_side, 0)
+    twins = share(slot_side, 0)
     overs[1].wait_recv()
     twins += share(slot_over, 1)
     yield
     arrived(twins)
     yield
-    far0.wait_recv()
-    twins = share(slot_far, 0)
-    far1.wait_recv()
-    twins += share(slot_far, 1)
-    yield
+    twins = [
+        copies.send(part(slot_far, h), part(slot_far, h), to_twin, start=False)
+        for h in range(2 if twin else 0)
+    ]
+
+    def pass_on():
+        for number, copy in enumerate((far0, far1)):
+            copy.wait_recv()
+            if twin:
+                twins[number].start()
+
+    yield pass_on
     arrived(twins)
     yield
 
@@ -502,13 +533,25 @@
         self.chips = (far, side, over, chip)
         self.twins = [None] * 4
 
-    def share(self, *numbers):
+    def share(self, *numbers, start=True):
         for n in numbers:
             self.twins[n] = []
             for h in range(2):
                 rows = pl.ds(h * self.half, self.half)
                 source = self.part_ref.at[CORES * self.chips[n] + 1 - self.core, rows]
-                self.twins[n].append(self.copies.send(source, self.twin.at[n, rows], self.to_twin))
+                self.twins[n].append(self.copies.send(source, self.twin.at[n, rows], self.to_twin, start))
+
+    def share_between(self, n, slot_of, body):
+        self.share(n, start=False)
+
+        @pl.loop(0, CORES)
+        def _(number):
+            @pl.when(number == 1)
+            def _():
+                for copy in self.twins[n]:
+                    copy.start()
+
+            body(slot_of(number))
 
     def _pair(self, n, h):
         part = slice(h * self.half, (h + 1) * self.half)
@@ -550,6 +593,12 @@
         self.out_ref[0 : self.half] = first + self.from_over[1].astype(F32)
         self.side1.wait_recv()
         self.out_ref[self.half :] = second + self.from_side[2].astype(F32)
+
+
+def drain(gather):
+    for step in gather:
+        if step is not None:
+            step()
 
 
 def scatter_scratch(rows, width):
@@ -793,13 +842,13 @@
     return jnp.concatenate([line_ref[s, row : row + 1, :] for s in range(line_ref.shape[0])], axis=1)
 
 
-def column_grads_stream(copies, grad_ref, recv, sum_ref):
+def column_grads_stream(copies, grad_ref, recv, sum_ref, lanes):
     chip, line, core, side, over, far = spots()
     sent = [
-        copies.send(grad_ref.at[CORES * q[1] + q[2]], recv.at[core, line], q)
+        copies.send(grad_ref.at[CORES * q[1] + q[2], :, lanes], recv.at[core, line], q)
         for q in line_partners()
     ]
-    local = copies.keep(grad_ref.at[CORES * line + core], recv.at[core, line])
+    local = copies.keep(grad_ref.at[CORES * line + core, :, lanes], recv.at[core, line])
     yield
     arrived(sent)
     local.wait()
@@ -807,7 +856,7 @@
         total = recv[number, 0].astype(F32)
         for family in range(1, PLANE):
             total = total + recv[number, family].astype(F32)
-        sum_ref[number] = total.astype(BF16)
+        sum_ref[number, :, lanes] = total.astype(BF16)
     yield
 
 
@@ -937,8 +986,8 @@
     chip, line, core, side, over, far = spots()
     if group == "near":
         return 2 * CORES, lambda n: CORES * (side + lax.div(n, CORES) * (over - side)) + lax.rem(n, CORES)
-    q = {"own": chip, "side": side, "over": over, "far": far}[group]
-    return CORES, lambda n: CORES * q + n
+    q = {"own": chip, "far": far}[group]
+    return CORES, lambda n: CORES * q + lax.rem(core + 1 + n, CORES)
 
 
 def each_slot(group, body):
@@ -950,14 +999,15 @@
 
 
 def front_kernel(
-    tok_ref, cot_ref, small_ref, wq_ref, wk_ref, wv_ref, wo_ref, wg_ref, wu_ref, wd_ref,
+    tok_ref, cot_ref, gain1_ref, gain2_ref, place_ref, wq_ref, wk_ref, wv_ref, wo_ref, wg_ref, wu_ref, wd_ref,
     n1_out, x_out, cot_out, line_out, wqkv_out, wo_out, q_out, k_out, v_out, ot_out, lse_out, att_out,
-    h1_out, dn2_out, mix_out, ggu_out, gd_out, table_out,
+    h1_out, dn2_out, mix_out, ggu_out, gd_out, gusum_out, table_out,
     *rest,
 ):
     scratch, other, rest = rest[:4], rest[4:8], rest[8:]
     x_ref, cotp_ref, line_ref, wqkv, wout, qs, ks, vs, ot_ref, lse_ref, att_ref, rest = *rest[:11], rest[11:]
-    h1_ref, dn2_ref, ggu_ref, gd_ref, rest = *rest[:4], rest[4:]
+    h1_ref, dn2_ref, ggu_ref, gd_ref, gusum, rest = *rest[:5], rest[5:]
+    small_ref, recv_gu, rest = *rest[:2], rest[2:]
     mid_x, mid_c, mid_o, down, tables, table, pieces, gate_w, up_w, gu, normed, rest = *rest[:11], rest[11:]
     n1s, n2s, cots, qkv, vt, att, parts, summed, wgu, wgu_t, wd, wd_t, us, dabs, *sems = rest
     copies = Copies(sems)
@@ -978,20 +1028,25 @@
         column = pl.ds(pl.multiple_of((CORES * chip + c) * heads, heads), heads)
         for n, w in enumerate((wq_ref, wk_ref, wv_ref)):
             loads.append(copies.keep(w.at[:, column], pieces.at[c, :, n * heads : (n + 1) * heads]))
+    small_ref[...] = jnp.zeros_like(small_ref)
+    small_ref[0:1] = gain1_ref[...].astype(F32)
+    small_ref[1:2] = gain2_ref[...].astype(F32)
+    small_ref[TABLE_ROW : TABLE_ROW + 1, 0 : place_ref.shape[1]] = place_ref[...].astype(F32)
     copies.enter()
-    tokens = inward_stream(copies, tok_ref, mid_x, x_ref)
+    early = copies.branch()
+    tokens = inward_stream(early, tok_ref, mid_x, x_ref)
     next(tokens)
+    out_part = quarter_columns(wo_ref, chip)
+    out_sent = [early.send(out_part, mid_o.at[line], q) for q in line_partners()[: PLANE - 1]]
+    out_kept = copies.keep(out_part, mid_o.at[line])
+    mine = CORES * line + core
+    small = [early.send(small_ref, line_ref.at[mine], q) for q in line_partners()]
+    small += [early.send(small_ref, tables.at[chip], q) for q in plane_partners()]
+    local = [copies.keep(small_ref, line_ref.at[mine]), copies.keep(small_ref, tables.at[chip])]
     finished(loads)
-    query_key = columns_relay(copies, pieces, wqkv, pl.ds(0, 2 * heads))
-    mine = CORES * line + core
-    small = [copies.send(small_ref, line_ref.at[mine], q) for q in line_partners()]
-    small += [copies.send(small_ref, tables.at[chip], q) for q in plane_partners()]
-    local = [copies.keep(small_ref, line_ref.at[mine]), copies.keep(small_ref, tables.at[chip])]
-    query_key.hop(1)
     next(tokens)
-    cotangents = inward_stream(copies, cot_ref, mid_c, cotp_ref)
+    cotangents = inward_stream(early, cot_ref, mid_c, cotp_ref)
     next(cotangents)
-    query_key.hop(2)
     gu[...] = jnp.zeros_like(gu)
     for k in range(PLANE):
         @pl.when(chip == k)
@@ -1002,15 +1057,17 @@
                     gu[c, :, at : at + share] = gate_w[:, begin : begin + share]
                     gu[c, :, lanes + at : lanes + at + share] = up_w[:, begin : begin + share]
     wd[hidden:lanes] = jnp.zeros((lanes - hidden, width), BF16)
+    arrived(out_sent)
+    out_kept.wait()
+    out_rows = to_ranks_stream(early, mid_o, wout)
+    next(out_rows)
     arrived(small)
     finished(local)
     load = [copies.keep(tables.at[line], table), copies.keep(tables.at[line], table_out)]
     store(line_ref, line_out)
-    query_key.hop(3)
     gain = gains_of(line_ref, 0)
     next(tokens)
-    value = columns_stream(copies, pieces, wqkv, pl.ds(2 * heads, heads))
-    next(value)
+    projections = columns_relay(copies, pieces, wqkv, pl.ds(0, 3 * heads))
     for n in range(PLANE):
         unit, ignored = unit_rows(x_ref[n].astype(F32))
         normed[n * chunk : (n + 1) * chunk] = (unit * gain).astype(BF16)
@@ -1019,8 +1076,11 @@
     next(gather)
     finished(load)
     next(gather)
-    next(value)
-    out_quarter = Relay(copies, lambda core: quarter_columns(wo_ref, chip), lambda z, core: mid_o.at[z], False)
+    projections.hop(1)
+    next(gather)
+    projections.hop(2)
+    next(gather)
+    next(gather)
     next(cotangents)
 
     def slot_rows(slot):
@@ -1029,14 +1089,11 @@
     def project(slot):
         qkv[slot_rows(slot), :] = matmul(n1s[slot], wqkv[...].reshape(width, 3 * heads)).astype(BF16)
 
+    next(gather)
+    projections.hop(3)
+    next(gather)()
     each_slot("own", project)
-    next(gather)
-    out_quarter.hop(1)
-    next(gather)
-    next(gather)
-    out_quarter.hop(2)
     each_slot("near", project)
-    next(gather)
     next(gather)
     each_slot("far", project)
     for source, target in ((n1s, n1_out), (x_ref, x_out), (wqkv, wqkv_out)):
@@ -1045,9 +1102,6 @@
     for n, ref in enumerate((qs, ks, vs)):
         scale = jnp.bfloat16(SCALE) if n == 0 else None
         in_place_order(table, qkv, slice(n * heads, (n + 1) * heads), ref, scale)
-    out_quarter.hop(3)
-    out_rows = to_ranks_stream(copies, mid_o, wout)
-    next(out_rows)
     next(cotangents)
     gather_cot = gather_stream(copies, cotp_ref.reshape(rows, width), cots)
     next(gather_cot)
@@ -1064,9 +1118,8 @@
         if number == 5:
             next(gather_cot)
             next(gather_cot)
+            next(gather_cot)
             gate_up.hop(1)
-    next(gather_cot)
-    down_rows.hop(1)
     in_gathered_order(table, att, att_ref, slice(0, heads))
     next(out_rows)
 
@@ -1085,7 +1138,9 @@
     scatter.side()
     scatter.over()
     next(gather_cot)
+    down_rows.hop(1)
     next(gather_cot)
+    next(gather_cot)()
     gate_up.hop(2)
     down_rows.hop(2)
     for source, target in ((wout, wo_out), (ot_ref, ot_out), (lse_ref, lse_out), (att_ref, att_out)):
@@ -1095,6 +1150,11 @@
     gate_up.hop(3)
     for s in range(ranks):
         wgu_t[:, s * heads : (s + 1) * heads] = wgu[s].T
+    down_rows.hop(3)
+    for z in range(PLANE):
+        wd[z * share : (z + 1) * share] = down[z]
+    wd_t[...] = wd[...].T
+    early.finish()
     gathering.finish()
     gain = gains_of(line_ref, 1)
     scatter.end()
@@ -1107,17 +1167,13 @@
     gather = gather_stream(copies, normed, n2s)
     next(gather)
     store(h1_ref, h1_out)
-    down_rows.hop(3)
-    for z in range(PLANE):
-        wd[z * share : (z + 1) * share] = down[z]
-    wd_t[...] = wd[...].T
     next(gather)
     scattering.finish()
     finished(stores)
     stores.clear()
 
-    def feed(slot):
-        block, cot = n2s[slot], cots[slot]
+    def feed_rows(slot, at):
+        block, cot = n2s[slot, at, :], cots[slot, at, :]
         both = matmul(block, wgu[...].reshape(width, 2 * lanes))
         gate, upper = both[:, :lanes], both[:, lanes:]
         bend = jnp.tanh(0.7978845608028654 * (gate + 0.044715 * gate * gate * gate))
@@ -1127,29 +1183,43 @@
             1.0 + 3 * 0.044715 * gate * gate
         )
         mixed = (active * upper).astype(BF16)
-        us[slot] = mixed
-        parts[slot] = matmul(mixed, wd[...]).astype(BF16)
+        us[slot, at, :] = mixed
+        parts[slot, at, :] = matmul(mixed, wd[...]).astype(BF16)
         du = matmul(cot, wd_t[...])
-        dabs[slot, :, 0:lanes] = (du * upper * slope).astype(BF16)
-        dabs[slot, :, lanes:] = (du * active).astype(BF16)
-        n1s[slot] = matmul(dabs[slot], wgu_t[...]).astype(BF16)
+        dabs[slot, at, 0:lanes] = (du * upper * slope).astype(BF16)
+        dabs[slot, at, lanes:] = (du * active).astype(BF16)
+        n1s[slot, at, :] = matmul(dabs[slot, at, :], wgu_t[...]).astype(BF16)
+
+    def feed(slot):
+        feed_rows(slot, pl.ds(0, rows))
+
+    def feed_halves(which, between):
+        count, slot_of = chip_slots("near")
+        half = rows // 2
+
+        @pl.loop(0, count)
+        def _(n):
+            @pl.when(n == count - 1)
+            def _():
+                between()
+
+            number = 1 - lax.div(n, CORES) if which == 0 else lax.div(n, CORES)
+            feed_rows(slot_of(n), pl.ds(pl.multiple_of(number * half, half), half))
 
     scatter = Scatter(copies, n1s, dn2_ref, other)
     each_slot("own", feed)
     scatter.share(3)
     next(gather)
     next(gather)
-    next(gather)
-    each_slot("side", feed)
-    scatter.share(1)
-    next(gather)
-    each_slot("over", feed)
-    scatter.share(2)
+    feed_halves(0, lambda: None)
+    next(gather)
+    next(gather)
+    feed_halves(1, next(gather))
+    scatter.share(1, 2)
+    next(gather)
     scatter.side()
-    next(gather)
-    each_slot("far", feed)
-    scatter.share(0)
     scatter.over()
+    scatter.share_between(0, chip_slots("far")[1], feed)
     scatter.far()
     store(parts, mix_out)
 
@@ -1160,10 +1230,11 @@
             grad = grad + inner(n2s[slot, :, columns], dabs[slot])
         ggu_ref[s] = grad.astype(BF16)
 
-    pl.loop(0, ranks // 2)(by_rows)
+    pl.loop(0, ranks)(by_rows)
+    columns = column_grads_stream(copies, ggu_ref, recv_gu, gusum, pl.ds(0, EARLY))
+    next(columns)
+    store(ggu_ref, ggu_out)
     scatter.cross()
-    pl.loop(ranks // 2, ranks)(by_rows)
-    store(ggu_ref, ggu_out)
     grad = jnp.zeros((lanes, width), F32)
     for slot in range(ranks):
         grad = grad + inner(us[slot], cots[slot])
@@ -1174,41 +1245,46 @@
     store(gd_ref, gd_out)
     scatter.end()
     store(dn2_ref, dn2_out)
-    for relay in (query_key, out_quarter, gate_up, down_rows):
+    next(columns)
+    store(gusum, gusum_out)
+    for relay in (projections, gate_up, down_rows):
         relay.finish()
     copies.finish()
     finished(stores)
 
 
-def front(tokens, cotangent, small, w_query, w_key, w_value, w_out, w_gate, w_up, w_down):
+def front(tokens, cotangent, gain1, gain2, places, w_query, w_key, w_value, w_out, w_gate, w_up, w_down):
     rows, width = tokens.shape
     heads, hidden = w_out.shape[0], w_down.shape[0]
     lanes = -(-hidden // 128) * 128
     ranks = PLANE * CORES
     total = ranks * rows
+    small = (8, heads)
     chunks, blocks = (PLANE, rows // PLANE, width), (ranks, rows, width)
     low = lambda *shape: jax.ShapeDtypeStruct(shape, BF16)
     wide = lambda *shape: jax.ShapeDtypeStruct(shape, F32)
     held = [
-        low(*chunks), low(*chunks), wide(ranks, *small.shape), low(ranks, heads, 3 * heads),
+        low(*chunks), low(*chunks), wide(ranks, *small), low(ranks, heads, 3 * heads),
         low(heads, width), low(total, heads), low(total, heads), low(total, heads), low(heads, total),
         wide(2, total), low(total, heads), wide(rows, width), wide(rows, width),
     ]
-    grads = [low(ranks, heads, 2 * lanes), low(PLANE, 2, hidden // PLANE, width // 2)]
-    shapes = [low(*blocks)] + held + [low(*blocks)] + grads + [wide(*small.shape)]
+    grads = [low(ranks, heads, 2 * lanes), low(PLANE, 2, hidden // PLANE, width // 2), low(CORES, heads, EARLY)]
+    shapes = [low(*blocks)] + held + [low(*blocks)] + grads + [wide(*small)]
     scratch = scatter_scratch(rows, width) * 2
     scratch += [pltpu.VMEM(a.shape, a.dtype) for a in held + grads]
     held = lambda *shape: pltpu.VMEM(shape, BF16)
+    scratch += [pltpu.VMEM(small, F32), held(CORES, PLANE, heads, EARLY)]
     scratch += [held(*chunks), held(*chunks), held(PLANE, heads, width // PLANE), held(PLANE, hidden // PLANE, width)]
-    scratch += [pltpu.VMEM((PLANE,) + small.shape, F32), pltpu.SMEM(small.shape, F32)]
+    scratch += [pltpu.VMEM((PLANE,) + small, F32), pltpu.SMEM(small, F32)]
     scratch += [held(CORES, heads, 3 * heads), held(*w_gate.shape), held(*w_up.shape), held(CORES, heads, 2 * lanes)]
     scratch += [held(rows, width), held(*blocks), held(*blocks), held(*blocks), held(total, 3 * heads)]
     scratch += [held(heads, total), held(total, heads), held(*blocks), pltpu.VMEM((rows, width), F32)]
     scratch += [held(ranks, heads, 2 * lanes), held(2 * lanes, width), held(lanes, width), held(width, lanes)]
     scratch += [held(ranks, rows, lanes), held(ranks, rows, 2 * lanes)]
     return comm_call(
-        front_kernel, "front", 1, tuple(shapes), [ANY] * 10, (ANY,) * len(shapes), scratch, 194, 138,
-    )(tokens, cotangent, small, w_query, w_key, w_value, w_out, w_gate, w_up, w_down)
+        front_kernel, "front", 1, tuple(shapes), [ANY] * 2 + [IN_VMEM] * 3 + [ANY] * 7, (ANY,) * len(shapes),
+        scratch, FRONT_SEMS[0], FRONT_SEMS[1],
+    )(tokens, cotangent, gain1, gain2, places, w_query, w_key, w_value, w_out, w_gate, w_up, w_down)
 
 
 def attend_back_block(number, prompt, qs, ks, vs, gs, kt, ot_ref, lse_ref, dqs, dks, dvs):
@@ -1241,7 +1317,7 @@
 
 def rear_kernel(
     table, summed_in, h1_in, cot_in, x_in, line_in, n1_in, mix_in, wqkv_in, wo_in,
-    q_in, k_in, v_in, ot_in, lse_in, att_in, gu_ref, down_ref,
+    q_in, k_in, v_in, ot_in, lse_in, att_in, gu_ref, down_ref, gusum_in,
     out_ref, grad_ref, gains_ref, gate_end, up_end, q_end, k_end, v_end, wo_all, wd_end,
     *rest,
 ):
@@ -1249,7 +1325,7 @@
     summed_ref, h1_ref, cot_ref, x_ref, line_ref, wqkv_ref, wo_ref, rest = *rest[:7], rest[7:]
     qs, ks, vs, ot_ref, lse_ref, att_ref, rest = *rest[:6], rest[6:]
     gate_out, up_out, q_out, k_out, v_out, wd_out, rest = *rest[:6], rest[6:]
-    n1s, parts, gas, datt, gs, kt, dqs, dks, dvs, dqkv, w_t, rest = *rest[:11], rest[11:]
+    n1s, mix, parts, gas, datt, gs, kt, dqs, dks, dvs, dqkv, w_t, rest = *rest[:12], rest[12:]
     dh1, summed, mixed, low, low_tok, low_out, rest = *rest[:6], rest[6:]
     recv_gu, sum_gu, gu_all, gqkv, recv_qkv, sum_qkv, qkv_all, gwo, rest = *rest[:8], rest[8:]
     mid_wo, recv_wo, sum_wo, recv_wd, sum_wd, down_all, own, recv_gain, sum_gain, plane, *sems = rest
@@ -1267,9 +1343,9 @@
 
     first = load((summed_in, summed_ref), (h1_in, h1_ref), (cot_in, cot_ref), (line_in, line_ref))
     second_load = load((k_in, ks), (wqkv_in, wqkv_ref), (wo_in, wo_ref))
-    third = load((mix_in, parts))
+    third = load((mix_in, mix))
     fourth = load((q_in, qs), (v_in, vs), (ot_in, ot_ref), (lse_in, lse_ref), (x_in, x_ref))
-    fifth = load((n1_in, n1s), (att_in, att_ref))
+    fifth = load((n1_in, n1s), (att_in, att_ref), (gusum_in, sum_gu.at[:, :, pl.ds(0, EARLY)]))
     stores = []
     copies.enter(crossing=True)
     finished(first)
@@ -1284,8 +1360,10 @@
         low[part] = grad.astype(BF16)
     gather = gather_stream(copies, low, gas)
     next(gather)
-    gate_up = column_grads_stream(copies, gu_ref, recv_gu, sum_gu)
+    gate_up = column_grads_stream(copies, gu_ref, recv_gu, sum_gu, pl.ds(EARLY, 2 * lanes - EARLY))
     next(gate_up)
+    down = sum_stream(copies, down_ref, recv_wd, sum_wd)
+    next(down)
     finished(second_load)
     for start in range(0, total, CONT):
         part = slice(start, start + CONT)
@@ -1307,34 +1385,35 @@
     finished(third)
     next(gather)
     next(gather)
+    next(gather)
     each_slot("near", attended_grad)
-    next(gather)
+    next(gather)()
     mixing = copies.branch()
-    second = Scatter(mixing, parts, mixed, other)
+    second = Scatter(mixing, mix, mixed, other)
     second.share(0, 1, 2, 3)
     second.far()
     second.side()
     second.over()
     next(gather)
     each_slot("far", attended_grad)
-    in_place_order(table, datt, slice(0, heads), gs)
     finished(fourth)
     finished(fifth)
+    grad = jnp.zeros((heads, width), F32)
+    for slot in range(ranks):
+        grad = grad + inner(att_ref[slot * rows : (slot + 1) * rows, :], gas[slot])
+    gwo[...] = grad.astype(BF16)
+    out_w = row_grads_stream(copies, gwo, mid_wo, recv_wo, sum_wo, wo_all)
+    next(out_w)
+    in_place_order(table, datt, slice(0, heads), gs)
     for number in range(total // CONT):
         attend_back_block(number, total // 2, qs, ks, vs, gs, kt, ot_ref, lse_ref, dqs, dks, dvs)
         if number == 3:
             second.cross()
-        if number == 6:
+        if number == 4:
             next(gate_up)
             gather_gu = gather_stream(copies, sum_gu, gu_all, twin=False)
             next(gather_gu)
-            down = sum_stream(copies, down_ref, recv_wd, sum_wd)
-            next(down)
-    second.end()
-    for n in range(PLANE):
-        part = slice(n * chunk, (n + 1) * chunk)
-        low_out[n] = (h1_ref[part] + mixed[part]).astype(BF16)
-    output = Outward(copies, low_out, out_ref)
+            next(out_w)
     ks_low, vs_low = gs, datt
     for start in range(0, total, CONT):
         part = slice(start, start + CONT)
@@ -1342,9 +1421,6 @@
         vs_low[part, :] = dvs[part, :].astype(BF16)
     for n, ref in enumerate((dqs, ks_low, vs_low)):
         in_gathered_order(table, ref, dqkv, slice(n * heads, (n + 1) * heads))
-    mixing.finish()
-    next(gather_gu)
-    next(gather_gu)
 
     def spread(slot):
         parts[slot] = matmul(dqkv[slot_rows(slot), :], w_t[...]).astype(BF16)
@@ -1359,6 +1435,13 @@
     scatter.far()
     scatter.side()
     scatter.over()
+    next(gather_gu)
+    next(gather_gu)
+    second.end()
+    for n in range(PLANE):
+        part = slice(n * chunk, (n + 1) * chunk)
+        low_out[n] = (h1_ref[part] + mixed[part]).astype(BF16)
+    output = Outward(copies, low_out, out_ref)
 
     def by_rows(s):
         columns = pl.ds(pl.multiple_of(s * heads, heads), heads)
@@ -1368,30 +1451,25 @@
         gqkv[s] = grad.astype(BF16)
 
     pl.loop(0, ranks)(by_rows)
-    qkv = column_grads_stream(copies, gqkv, recv_qkv, sum_qkv)
+    qkv = column_grads_stream(copies, gqkv, recv_qkv, sum_qkv, pl.ds(0, 3 * heads))
     next(qkv)
-    grad = jnp.zeros((heads, width), F32)
-    for slot in range(ranks):
-        grad = grad + inner(att_ref[slot * rows : (slot + 1) * rows, :], gas[slot])
-    gwo[...] = grad.astype(BF16)
-    out_w = row_grads_stream(copies, gwo, mid_wo, recv_wo, sum_wo, wo_all)
-    next(out_w)
-    for ignored in gather_gu:
-        pass
     scatter.cross()
-    next(out_w)
     next(down)
     gather_down = gather_stream(copies, sum_wd, down_all, twin=False)
     next(gather_down)
+    next(out_w)
+    drain(gather_gu)
 
     def format_gate(chip, c, z):
         begin, at = (CORES * z + c) * hidden + chip * share, z * share
         gate_out[:, begin : begin + share] = gu_all[chip, c, :, at : at + share]
         up_out[:, begin : begin + share] = gu_all[chip, c, :, lanes + at : lanes + at + share]
 
-    places = [(chip, c, z) for chip in range(PLANE) for c in range(CORES) for z in range(PLANE)]
-    for place in places[: len(places) // 2]:
-        format_gate(*place)
+    for chip in range(PLANE):
+        for c in range(CORES):
+            for z in range(PLANE):
+                format_gate(chip, c, z)
+    stores += load((gate_out, gate_end), (up_out, up_end))
     scatter.end()
     gain = gains_of(line_ref, 0)
     gain1_sum = jnp.zeros((1, width), F32)
@@ -1410,39 +1488,33 @@
     next(gains)
     next(gather_down)
     next(gather_down)
-    next(out_w)
-    for place in places[len(places) // 2 :]:
-        format_gate(*place)
-    stores += load((gate_out, gate_end), (up_out, up_end))
-    for ignored in gather_down:
-        pass
+    next(qkv)
+    gather_qkv = gather_stream(copies, sum_qkv, qkv_all, twin=False)
+    next(gather_qkv)
+    drain(gather_down)
     for chip in range(PLANE):
         for h in range(2):
             wd_out[chip * share : (chip + 1) * share, h * (width // 2) : (h + 1) * (width // 2)] = down_all[chip, h]
     stores += load((wd_out, wd_end))
-    next(qkv)
-    gather_qkv = gather_stream(copies, sum_qkv, qkv_all, twin=False)
-    next(gather_qkv)
-    next(gains)
     next(gather_qkv)
     next(gather_qkv)
     next(gains)
-    next(out_w)
-    for ignored in gather_qkv:
-        pass
+    drain(gather_qkv)
     for chip in range(PLANE):
         for c in range(CORES):
             begin = (CORES * chip + c) * heads
             for n, ref in enumerate((q_out, k_out, v_out)):
                 ref[:, begin : begin + heads] = qkv_all[chip, c, :, n * heads : (n + 1) * heads]
     stores += load((q_out, q_end), (k_out, k_end), (v_out, v_end))
+    next(out_w)
+    next(gains)
     output.wait()
     tokens.wait()
     copies.finish()
     finished(stores)
 
 
-def rear(table, summed, h1, cot, x, lines, n1, mixed, w_qkv, w_o, qs, ks, vs, ot, lse, att, gate_up_grad, down_grad, ff):
+def rear(table, summed, h1, cot, x, lines, n1, mixed, w_qkv, w_o, qs, ks, vs, ot, lse, att, gate_up_grad, down_grad, gate_up_sum, ff):
     ranks = PLANE * CORES
     rows, width = h1.shape
     total, heads = att.shape
@@ -1460,24 +1532,28 @@
     scratch = scatter_scratch(rows, width) * 2
     scratch += [pltpu.VMEM(a.shape, a.dtype) for a in (summed, h1, cot, x, lines, w_qkv, w_o, qs, ks, vs, ot, lse, att)]
     scratch += [held(*shapes[n].shape) for n in (3, 4, 5, 6, 7, 9)]
-    scratch += [held(*n1.shape)] * 3 + [held(total, heads)] * 2 + [held(heads, total), held(total, heads)]
+    scratch += [held(*n1.shape)] * 4 + [held(total, heads)] * 2 + [held(heads, total), held(total, heads)]
     scratch += [wide(total, heads)] * 2 + [held(total, 3 * heads), held(3 * heads, width)]
     scratch += [wide(rows, width)] * 3 + [held(rows, width)] + [held(*x.shape)] * 2
     for grad in (gate_up_grad, w_qkv):
         piece = (CORES,) + grad.shape[1:]
         if grad is w_qkv:
             scratch += [held(*grad.shape)]
-        scratch += [held(CORES, PLANE, *grad.shape[1:]), held(*piece), held(PLANE, *piece)]
+        columns = grad.shape[2] - (0 if grad is w_qkv else EARLY)
+        scratch += [held(CORES, PLANE, grad.shape[1], columns), held(*piece), held(PLANE, *piece)]
     scratch += [held(heads, width)]
     scratch += [held(PLANE, heads, quarter)] * 2 + [held(heads, quarter)]
     scratch += [held(*down_grad.shape), held(*down_grad.shape[1:]), held(*down_grad.shape)]
     scratch += [wide(*lines.shape)] * 2 + [wide(*small), wide(PLANE, *small)]
     return comm_call(
         rear_kernel, "rear", 2, shapes,
-        [pl.BlockSpec(memory_space=pltpu.SMEM)] + [ANY] * 17,
+        [pl.BlockSpec(memory_space=pltpu.SMEM)] + [ANY] * 18,
         (ANY, ANY, IN_VMEM) + (ANY,) * 7,
-        scratch, 139, 104,
-    )(table, summed, h1, cot, x, lines, n1, mixed, w_qkv, w_o, qs, ks, vs, ot, lse, att, gate_up_grad, down_grad)
+        scratch, REAR_SEMS[0], REAR_SEMS[1],
+    )(
+        table, summed, h1, cot, x, lines, n1, mixed, w_qkv, w_o, qs, ks, vs, ot, lse, att,
+        gate_up_grad, down_grad, gate_up_sum,
+    )
 
 
 def finish_kernel(*refs):
@@ -1490,7 +1566,10 @@
         loads[-1].start()
     for n, (target, buffer, wide) in enumerate(zip(outputs, held, stage)):
         loads[n].wait()
-        if buffer.dtype != target.dtype:
+        if buffer.shape != target.shape:
+            wide[...] = buffer[n - len(inputs) + 2 : n - len(inputs) + 3, :]
+            buffer = wide
+        elif buffer.dtype != target.dtype:
             wide[...] = buffer[...].astype(F32)
             buffer = wide
         stores.append(pltpu.make_async_copy(buffer, target, sems.at[1, n]))
@@ -1499,13 +1578,13 @@
         copy.wait()
 
 
-def finish(tokens, grads):
-    inputs = list(tokens) + list(grads)
+def finish(tokens, grads, gains):
+    inputs = list(tokens) + list(grads) + [gains] * 2
     shapes = [jax.ShapeDtypeStruct(a.shape, a.dtype) for a in tokens]
     shapes += [jax.ShapeDtypeStruct(a.shape, F32) for a in grads]
-    small = pltpu.VMEM((8, 128), F32)
+    shapes += [jax.ShapeDtypeStruct((1, gains.shape[1]), F32)] * 2
     held = [pltpu.VMEM(a.shape, a.dtype) for a in inputs]
-    stage = [small] * len(tokens) + [pltpu.VMEM(a.shape, F32) for a in grads]
+    stage = [pltpu.VMEM((8, 128), F32)] * len(tokens) + [pltpu.VMEM(a.shape, F32) for a in shapes[len(tokens) :]]
     return pl.pallas_call(
         finish_kernel,
         out_shape=tuple(shapes),
@@ -1531,22 +1610,22 @@
     w_up,
     w_down,
 ):
-    rows, width = tokens.shape[1:]
-    heads = width // (PLANE * CORES)
-    table = jnp.pad(block_table.astype(F32), ((0, 0), (0, heads - block_table.shape[1])))
-    small = jnp.concatenate([norm1_gain[None].astype(F32), norm2_gain[None].astype(F32), table])
-    small = jnp.pad(small, ((0, 8 - small.shape[0]), (0, 0)))
     (
-        n1, x, cot, gains, w_qkv, w_o, qs, ks, vs, ot, lse, att, h1, dn2, mixed, g_gu, g_down, table
-    ) = front(tokens[0], cotangent[0], small, w_query, w_key, w_value, w_out, w_gate, w_up, w_down)
+        n1, x, cot, gains, w_qkv, w_o, qs, ks, vs, ot, lse, att, h1, dn2, mixed, g_gu, g_down, gu_sum, table
+    ) = front(
+        tokens[0], cotangent[0], norm1_gain[None], norm2_gain[None], block_table,
+        w_query, w_key, w_value, w_out, w_gate, w_up, w_down,
+    )
     output, tokens_grad, gain_grads, *grads = rear(
-        table, dn2, h1, cot, x, gains, n1, mixed, w_qkv, w_o, qs, ks, vs, ot, lse, att, g_gu, g_down,
+        table, dn2, h1, cot, x, gains, n1, mixed, w_qkv, w_o, qs, ks, vs, ot, lse, att, g_gu, g_down, gu_sum,
         w_gate.shape[1],
     )
-    output, tokens_grad, gate, up, query, key, value, out, down = finish((output, tokens_grad), grads)
+    output, tokens_grad, gate, up, query, key, value, out, down, gain1, gain2 = finish(
+        (output, tokens_grad), grads, gain_grads
+    )
     return (
         output[None], tokens_grad[None],
-        gain_grads[0], query, key, value, out, gain_grads[1], gate, up, down,
+        gain1[0], query, key, value, out, gain2[0], gate, up, down,
     )
 
 

time: 275 us -> 256 us (0.931)
  Pallas kernels: 266 us -> 251 us
    pallas_call x1, Pallas kernels: 116 us -> 107 us  [rear(): comm_call(rear_kernel, 'rear', 2, shapes, [pl.BlockSpec(memory_space=pltp...]
    pallas_call x1, Pallas kernels: 146 us -> 139 us  [front(): comm_call(front_kernel, 'front', 1, tuple(shapes), [ANY] * 2 + [IN_VMEM]...]
where the time goes in v4:
time: 256 us; the launch traced here: 252 us
  Pallas kernels  251 us (98%)
    pallas_call x1, Pallas kernels, front(): comm_call(front_kernel, 'front', 1, tuple(shapes), [ANY] * 2 + [IN_VMEM]...  139 us
    pallas_call x1, Pallas kernels, rear(): comm_call(rear_kernel, 'rear', 2, shapes, [pl.BlockSpec(memory_space=pltp...  107 us

profile of v4, /device:TPU:0, one launch (start us, length us, event | category | flops | bytes accessed | tf_op | source)
XLA Modules:
  0.0 251.8 jit_solution(1150237648568404309)
XLA Ops:
  0.6 138.9 %front.1 = (bf16[8,256,1024]{2,1,0:T(8,128)(2,1)}, bf16[4,64,1024]{2,1,0:T(8,128)(2,1)}, bf16[4,64,1024]{2,1,0:T(8,128)(2,1)}, f32[8,8,128]{2,1,0:T(8,128)}, bf1...) custom-call(bf16[256,1024]{1,0:T(8,128)(2,1)} %bitcast.8, ...), custom_call_target="tpu_custom_call" | custom-call | tf_op jit(solution)/shard_map/front/pallas_call | solution.py:1284
  139.5 107.3 %rear.1 = (bf16[256,1024]{1,0:T(8,128)(2,1)}, bf16[256,1024]{1,0:T(8,128)(2,1)}, f32[8,128]{1,0:T(8,128)}, bf16[128,2816]{1,0:T(8,128)(2,1)}, bf16[128,2816]{1,0...) custom-call(f32[8,128]{1,0:T(8,128)} %get-tuple-element.51.table, ...), custom_call_target="tpu_custom_call" | custom-call | tf_op jit(solution)/shard_map/rear/pallas_call | solution.py:1548
  246.8 4.4 %finish.1 = (bf16[256,1024]{1,0:T(8,128)(2,1)}, bf16[256,1024]{1,0:T(8,128)(2,1)}, f32[128,2816]{1,0:T(8,128)}, f32[128,2816]{1,0:T(8,128)}, f32[128,1024]{1,0:T...) custom-call(bf16[256,1024]{1,0:T(8,128)(2,1)} %get-tuple-element.70., ...), custom_call_target="tpu_custom_call" | custom-call | tf_op jit(solution)/shard_map/finish/pallas_call | solution.py:1588

commit v5 on v4

--- a/solution.py
+++ b/solution.py
@@ -392,7 +392,7 @@
             held.append(number)
         return self.sems[0].at[number]
 
-    def enter(self, crossing=False):
+    def greet(self, crossing=False):
         barrier = pltpu.get_barrier_semaphore()
         partners = plane_partners() + line_partners()
         chip, line, core, side, over, far = spots()
@@ -400,24 +400,33 @@
             partners += [(line, lax.rem(line + d, PLANE), core) for d in range(1, PLANE)]
             partners += [(lax.rem(chip + d, PLANE), chip, core) for d in range(1, PLANE)]
 
-        def greet(partner):
+        def signal(partner):
             pl.semaphore_signal(barrier, inc=1, device_id=partner, device_id_type=MESH)
 
         for partner in partners:
-            greet(partner)
-        if not crossing:
-            pl.semaphore_wait(barrier, len(partners))
+            signal(partner)
+        if crossing:
+            @pl.when(chip != line)
+            def _():
+                signal((line, line, core))
+                signal((chip, chip, core))
+
+        self.crossing, self.expected = crossing, len(partners)
+
+    def welcome(self):
+        barrier = pltpu.get_barrier_semaphore()
+        if not self.crossing:
+            pl.semaphore_wait(barrier, self.expected)
             return
-
-        @pl.when(chip != line)
+        away = lax.axis_index("group") != lax.axis_index("z")
+
+        @pl.when(away)
         def _():
-            greet((line, line, core))
-            greet((chip, chip, core))
-            pl.semaphore_wait(barrier, len(partners) + 2)
-
-        @pl.when(chip == line)
+            pl.semaphore_wait(barrier, self.expected + 2)
+
+        @pl.when(jnp.logical_not(away))
         def _():
-            pl.semaphore_wait(barrier, len(partners))
+            pl.semaphore_wait(barrier, self.expected)
 
     def send(self, source, target, partner, start=True):
         held = []
@@ -1028,11 +1037,12 @@
         column = pl.ds(pl.multiple_of((CORES * chip + c) * heads, heads), heads)
         for n, w in enumerate((wq_ref, wk_ref, wv_ref)):
             loads.append(copies.keep(w.at[:, column], pieces.at[c, :, n * heads : (n + 1) * heads]))
+    copies.greet()
     small_ref[...] = jnp.zeros_like(small_ref)
     small_ref[0:1] = gain1_ref[...].astype(F32)
     small_ref[1:2] = gain2_ref[...].astype(F32)
     small_ref[TABLE_ROW : TABLE_ROW + 1, 0 : place_ref.shape[1]] = place_ref[...].astype(F32)
-    copies.enter()
+    copies.welcome()
     early = copies.branch()
     tokens = inward_stream(early, tok_ref, mid_x, x_ref)
     next(tokens)
@@ -1132,9 +1142,9 @@
     scatter.share(0)
     each_slot("near", spread)
     scatter.share(1, 2)
+    scatter.far()
     each_slot("own", spread)
     scatter.share(3)
-    scatter.far()
     scatter.side()
     scatter.over()
     next(gather_cot)
@@ -1347,7 +1357,7 @@
     fourth = load((q_in, qs), (v_in, vs), (ot_in, ot_ref), (lse_in, lse_ref), (x_in, x_ref))
     fifth = load((n1_in, n1s), (att_in, att_ref), (gusum_in, sum_gu.at[:, :, pl.ds(0, EARLY)]))
     stores = []
-    copies.enter(crossing=True)
+    copies.greet(crossing=True)
     finished(first)
     gain = gains_of(line_ref, 1)
     gain2_sum = jnp.zeros((1, width), F32)
@@ -1358,6 +1368,7 @@
         gain2_sum = gain2_sum + by_gain
         dh1[part] = grad
         low[part] = grad.astype(BF16)
+    copies.welcome()
     gather = gather_stream(copies, low, gas)
     next(gather)
     gate_up = column_grads_stream(copies, gu_ref, recv_gu, sum_gu, pl.ds(EARLY, 2 * lanes - EARLY))
@@ -1380,17 +1391,17 @@
         datt[slot_rows(slot), :] = outer(gas[slot], wo_ref[...]).astype(BF16)
 
     next(gather)
-    each_slot("own", attended_grad)
-    next(gather)
     finished(third)
-    next(gather)
-    next(gather)
-    next(gather)
-    each_slot("near", attended_grad)
-    next(gather)()
     mixing = copies.branch()
     second = Scatter(mixing, mix, mixed, other)
     second.share(0, 1, 2, 3)
+    each_slot("own", attended_grad)
+    next(gather)
+    next(gather)
+    next(gather)
+    next(gather)
+    each_slot("near", attended_grad)
+    next(gather)()
     second.far()
     second.side()
     second.over()
@@ -1413,6 +1424,7 @@
             next(gate_up)
             gather_gu = gather_stream(copies, sum_gu, gu_all, twin=False)
             next(gather_gu)
+        if number == 6:
             next(out_w)
     ks_low, vs_low = gs, datt
     for start in range(0, total, CONT):
@@ -1430,9 +1442,9 @@
     scatter.share(0)
     each_slot("near", spread)
     scatter.share(1, 2)
+    scatter.far()
     each_slot("own", spread)
     scatter.share(3)
-    scatter.far()
     scatter.side()
     scatter.over()
     next(gather_gu)
@@ -1491,6 +1503,8 @@
     next(qkv)
     gather_qkv = gather_stream(copies, sum_qkv, qkv_all, twin=False)
     next(gather_qkv)
+    next(gather_qkv)
+    next(gather_qkv)
     drain(gather_down)
     for chip in range(PLANE):
         for h in range(2):

time: 256 us -> 253 us (0.988)
  Pallas kernels: 251 us -> 248 us
    pallas_call x1, Pallas kernels: 107 us -> 104 us  [rear(): comm_call(rear_kernel, 'rear', 2, shapes, [pl.BlockSpec(memory_space=pltp...]
where the time goes in v5:
time: 253 us; the launch traced here: 249 us
  Pallas kernels  248 us (98%)
    pallas_call x1, Pallas kernels, front(): comm_call(front_kernel, 'front', 1, tuple(shapes), [ANY] * 2 + [IN_VMEM]...  139 us
    pallas_call x1, Pallas kernels, rear(): comm_call(rear_kernel, 'rear', 2, shapes, [pl.BlockSpec(memory_space=pltp...  104 us

profile of v5, /device:TPU:0, one launch (start us, length us, event | category | flops | bytes accessed | tf_op | source)
XLA Modules:
  0.0 248.7 jit_solution(6337621848568267688)
XLA Ops:
  0.6 138.8 %front.1 = (bf16[8,256,1024]{2,1,0:T(8,128)(2,1)}, bf16[4,64,1024]{2,1,0:T(8,128)(2,1)}, bf16[4,64,1024]{2,1,0:T(8,128)(2,1)}, f32[8,8,128]{2,1,0:T(8,128)}, bf1...) custom-call(bf16[256,1024]{1,0:T(8,128)(2,1)} %bitcast.8, ...), custom_call_target="tpu_custom_call" | custom-call | tf_op jit(solution)/shard_map/front/pallas_call | solution.py:1294
  139.4 104.4 %rear.1 = (bf16[256,1024]{1,0:T(8,128)(2,1)}, bf16[256,1024]{1,0:T(8,128)(2,1)}, f32[8,128]{1,0:T(8,128)}, bf16[128,2816]{1,0:T(8,128)(2,1)}, bf16[128,2816]{1,0...) custom-call(f32[8,128]{1,0:T(8,128)} %get-tuple-element.51.table, ...), custom_call_target="tpu_custom_call" | custom-call | tf_op jit(solution)/shard_map/rear/pallas_call | solution.py:1562
  243.8 4.4 %finish.1 = (bf16[256,1024]{1,0:T(8,128)(2,1)}, bf16[256,1024]{1,0:T(8,128)(2,1)}, f32[128,2816]{1,0:T(8,128)}, f32[128,2816]{1,0:T(8,128)}, f32[128,1024]{1,0:T...) custom-call(bf16[256,1024]{1,0:T(8,128)(2,1)} %get-tuple-element.70., ...), custom_call_target="tpu_custom_call" | custom-call | tf_op jit(solution)/shard_map/finish/pallas_call | solution.py:1602

commit v6 on v5

--- a/solution.py
+++ b/solution.py
@@ -1233,16 +1233,19 @@
     scatter.far()
     store(parts, mix_out)
 
-    def by_rows(s):
-        columns = pl.ds(pl.multiple_of(s * heads, heads), heads)
-        grad = jnp.zeros((heads, 2 * lanes), F32)
-        for slot in range(ranks):
-            grad = grad + inner(n2s[slot, :, columns], dabs[slot])
-        ggu_ref[s] = grad.astype(BF16)
-
-    pl.loop(0, ranks)(by_rows)
+    def by_rows(begin, size):
+        @pl.loop(0, ranks)
+        def _(s):
+            columns = pl.ds(pl.multiple_of(s * heads, heads), heads)
+            grad = jnp.zeros((heads, size), F32)
+            for slot in range(ranks):
+                grad = grad + inner(n2s[slot, :, columns], dabs[slot, :, begin : begin + size])
+            ggu_ref[s, :, begin : begin + size] = grad.astype(BF16)
+
+    by_rows(0, EARLY)
     columns = column_grads_stream(copies, ggu_ref, recv_gu, gusum, pl.ds(0, EARLY))
     next(columns)
+    by_rows(EARLY, 2 * lanes - EARLY)
     store(ggu_ref, ggu_out)
     scatter.cross()
     grad = jnp.zeros((lanes, width), F32)
@@ -1420,11 +1423,10 @@
         attend_back_block(number, total // 2, qs, ks, vs, gs, kt, ot_ref, lse_ref, dqs, dks, dvs)
         if number == 3:
             second.cross()
-        if number == 4:
+        if number == 6:
             next(gate_up)
             gather_gu = gather_stream(copies, sum_gu, gu_all, twin=False)
             next(gather_gu)
-        if number == 6:
             next(out_w)
     ks_low, vs_low = gs, datt
     for start in range(0, total, CONT):

time: 253 us -> 252 us (level)
  no operation moved by 1% of the time
where the time goes in v6:
time: 252 us; the launch traced here: 247 us
  Pallas kernels  246 us (98%)
    pallas_call x1, Pallas kernels, front(): comm_call(front_kernel, 'front', 1, tuple(shapes), [ANY] * 2 + [IN_VMEM]...  139 us
    pallas_call x1, Pallas kernels, rear(): comm_call(rear_kernel, 'rear', 2, shapes, [pl.BlockSpec(memory_space=pltp...  103 us

profile of v6, /device:TPU:0, one launch (start us, length us, event | category | flops | bytes accessed | tf_op | source)
XLA Modules:
  0.0 247.4 jit_solution(10758281250754323908)
XLA Ops:
  0.6 138.8 %front.1 = (bf16[8,256,1024]{2,1,0:T(8,128)(2,1)}, bf16[4,64,1024]{2,1,0:T(8,128)(2,1)}, bf16[4,64,1024]{2,1,0:T(8,128)(2,1)}, f32[8,8,128]{2,1,0:T(8,128)}, bf1...) custom-call(bf16[256,1024]{1,0:T(8,128)(2,1)} %bitcast.8, ...), custom_call_target="tpu_custom_call" | custom-call | tf_op jit(solution)/shard_map/front/pallas_call | solution.py:1297
  139.4 103.1 %rear.1 = (bf16[256,1024]{1,0:T(8,128)(2,1)}, bf16[256,1024]{1,0:T(8,128)(2,1)}, f32[8,128]{1,0:T(8,128)}, bf16[128,2816]{1,0:T(8,128)(2,1)}, bf16[128,2816]{1,0...) custom-call(f32[8,128]{1,0:T(8,128)} %get-tuple-element.51.table, ...), custom_call_target="tpu_custom_call" | custom-call | tf_op jit(solution)/shard_map/rear/pallas_call | solution.py:1564
  242.5 4.4 %finish.1 = (bf16[256,1024]{1,0:T(8,128)(2,1)}, bf16[256,1024]{1,0:T(8,128)(2,1)}, f32[128,2816]{1,0:T(8,128)}, f32[128,2816]{1,0:T(8,128)}, f32[128,1024]{1,0:T...) custom-call(bf16[256,1024]{1,0:T(8,128)(2,1)} %get-tuple-element.70., ...), custom_call_target="tpu_custom_call" | custom-call | tf_op jit(solution)/shard_map/finish/pallas_call | solution.py:1604
